TPU v7x, 32 devices: a whole 2x2x4 slice. The times are simulated.
32 devices in a mesh: cuts: 2 (over x), frame: 8 (over z, y), coil: 2 (over core).
Axes of the slice: x: 2, y: 2, z: 4, core: 2. Of those that a mesh axis runs over, the one named last changes fastest.
Arguments:
- spatial: bfloat16 [512, 32, 512], P(('cuts', 'coil', 'frame')), parts along dimension 0, may hold values from -6 to 6
- temporal: bfloat16 [32, 64], P(('cuts', 'frame')), parts along dimension 0, may hold values from -0.75 to 0.75
- kspace: bfloat16 [32, 32, 256, 512], P(('cuts', 'frame'), 'coil'), parts along dimension 0, may hold values from -2 to 2
- sampled: int32 [32, 256], P(('cuts', 'frame')), parts along dimension 0, may hold values 0 or 1
- sensitivity: bfloat16 [64, 256, 512], P(('cuts', 'coil')), parts along dimension 0, may hold values from -1 to 1
Outputs:
- spatial_grad: float32 [512, 32, 512], P(('cuts', 'coil', 'frame')), parts along dimension 0
- temporal_grad: float32 [32, 64], P(('cuts', 'frame')), parts along dimension 0
There are 2 independent parts, one for each index of `cuts`. A program takes and returns all parts, laid end to end along the dimension named above; each array names one. Nothing has to cross between parts.
All inputs are finite; a program needn't handle non-finite values. No bound on the sum of `sampled` on one device may be relied on, other than what follows from the above.
Results may differ from a plain program's by a relative error of at most 0.003.
Values may be sent and summed in bfloat16 or wider, within the bound.
No kernel may reach another device: no remote copies, remote signals or barrier semaphores. Data moves between devices by JAX's collectives and lax.ppermute only.
A program may use at most 128 MiB of HBM per device.

v0:
```python
import math

import jax
import jax.numpy as jnp
from jax import lax
from jax.sharding import PartitionSpec as P


def split_parts(values):
    half_width = values.shape[-1] // 2
    return (values[..., :half_width], values[..., half_width:])


def dft_block(length):
    index = jnp.arange(length, dtype=jnp.int32)
    angles = (index[:, None] * index[None, :] % length).astype(jnp.float32) * (
        2.0 * math.pi / length
    )
    norm_factor = 1.0 / math.sqrt(length)
    cosine = jnp.cos(angles) * norm_factor
    sine_part = -jnp.sin(angles) * norm_factor
    upper_rows = jnp.concatenate([cosine, sine_part], 1)
    lower_rows = jnp.concatenate([-sine_part, cosine], 1)
    return jnp.concatenate([upper_rows, lower_rows], 0).astype(jnp.bfloat16)


def to_image(temporal, spatial):
    temp_real, temp_imag = split_parts(temporal)
    spat_real, spat_imag = split_parts(spatial)
    image_real = jnp.einsum(
        "tr,xry->txy", temp_real, spat_real, preferred_element_type=jnp.float32
    ) - jnp.einsum("tr,xry->txy", temp_imag, spat_imag, preferred_element_type=jnp.float32)
    image_imag = jnp.einsum(
        "tr,xry->txy", temp_real, spat_imag, preferred_element_type=jnp.float32
    ) + jnp.einsum("tr,xry->txy", temp_imag, spat_real, preferred_element_type=jnp.float32)
    return jnp.concatenate([image_real, image_imag], -1).astype(jnp.bfloat16)


def factor_grad(temporal, grad_image):
    temp_real, temp_imag = split_parts(temporal)
    grad_real, grad_imag = split_parts(grad_image)
    spatial_real = jnp.einsum(
        "tr,txy->xry", temp_real, grad_real, preferred_element_type=jnp.float32
    ) + jnp.einsum("tr,txy->xry", temp_imag, grad_imag, preferred_element_type=jnp.float32)
    spatial_imag = jnp.einsum(
        "tr,txy->xry", temp_real, grad_imag, preferred_element_type=jnp.float32
    ) - jnp.einsum("tr,txy->xry", temp_imag, grad_real, preferred_element_type=jnp.float32)
    return jnp.concatenate([spatial_real, spatial_imag], -1)


def frame_grad(spatial, grad_image):
    spat_real, spat_imag = split_parts(spatial)
    grad_real, grad_imag = split_parts(grad_image)
    temporal_real = jnp.einsum(
        "xry,txy->tr", spat_real, grad_real, preferred_element_type=jnp.float32
    ) + jnp.einsum("xry,txy->tr", spat_imag, grad_imag, preferred_element_type=jnp.float32)
    temporal_imag = jnp.einsum(
        "xry,txy->tr", spat_real, grad_imag, preferred_element_type=jnp.float32
    ) - jnp.einsum("xry,txy->tr", spat_imag, grad_real, preferred_element_type=jnp.float32)
    return jnp.concatenate([temporal_real, temporal_imag], -1)


def coil_adjoint(image, measured, sampled_row, sensitivity, block):
    image_real, image_imag = split_parts(image.astype(jnp.float32))
    sens_real, sens_imag = split_parts(sensitivity.astype(jnp.float32))
    coil_real = sens_real * image_real[None] - sens_imag * image_imag[None]
    coil_imag = sens_real * image_imag[None] + sens_imag * image_real[None]
    coil_image = jnp.concatenate([coil_real, coil_imag], -1).astype(jnp.bfloat16)
    coil_count, row_count, full_width = coil_image.shape
    spectrum = jnp.dot(
        coil_image.reshape(coil_count * row_count, full_width),
        block,
        preferred_element_type=jnp.float32,
    ).reshape(coil_count, row_count, full_width)
    line_keep = jnp.concatenate([sampled_row, sampled_row]).astype(jnp.float32)
    misfit = (line_keep * (spectrum - measured.astype(jnp.float32))).astype(jnp.bfloat16)
    adjoint = jnp.dot(
        misfit.reshape(coil_count * row_count, full_width),
        block.T,
        preferred_element_type=jnp.float32,
    ).reshape(coil_count, row_count, full_width)
    back_real, back_imag = split_parts(adjoint)
    grad_real = jnp.sum(sens_real * back_real + sens_imag * back_imag, axis=0)
    grad_imag = jnp.sum(sens_real * back_imag - sens_imag * back_real, axis=0)
    return jnp.concatenate([grad_real, grad_imag], -1)


def on_device(spatial, temporal, kspace, sampled, sensitivity):
    block = dft_block(spatial.shape[2] // 2)
    temporal_all = lax.all_gather(temporal, "frame", axis=0, tiled=True)
    image_rows = to_image(temporal_all, spatial)
    image_half = lax.all_to_all(image_rows, "frame", split_axis=0, concat_axis=1, tiled=True)
    image_full = lax.all_gather(image_half, "coil", axis=1, tiled=True)
    coil_partial = lax.map(
        lambda frame_item: coil_adjoint(
            frame_item[0], frame_item[1], frame_item[2], sensitivity, block
        ),
        (image_full, kspace, sampled),
    )
    grad_half = lax.psum_scatter(coil_partial, "coil", scatter_dimension=1, tiled=True).astype(
        jnp.bfloat16
    )
    grad_rows = lax.all_to_all(grad_half, "frame", split_axis=1, concat_axis=0, tiled=True)
    spatial_grad = factor_grad(temporal_all, grad_rows)
    temporal_part = lax.psum_scatter(
        frame_grad(spatial, grad_rows), "frame", scatter_dimension=0, tiled=True
    )
    temporal_grad = lax.psum(temporal_part, "coil")
    return (spatial_grad, temporal_grad)


def solution(mesh):
    placed = (
        P(("cuts", "coil", "frame"), None, None),
        P(("cuts", "frame"), None),
        P(("cuts", "frame"), "coil", None, None),
        P(("cuts", "frame"), None),
        P(("cuts", "coil"), None, None),
    )
    return jax.shard_map(
        on_device,
        mesh=mesh,
        in_specs=placed,
        out_specs=(P(("cuts", "coil", "frame"), None, None), P(("cuts", "frame"), None)),
        check_vma=False,
    )
```

profile of v0, /device:TPU:0, one launch (start us, length us, event | category | flops | bytes accessed | tf_op | source)
XLA Modules:
  0.0 152.4 jit_solution(3036720703098302424)
XLA Ops:
  0.6 22.5 %all-gather = bf16[8,2,64]{2,1,0:T(2,128)(2,1)S(1)} all-gather(bf16[1,2,64]{2,1,0:T(2,128)(2,1)} %bitcast.83), channel_id=1, replica_groups=mesh['cuts'=2,'frame'=8,'coil'=2] {'frame'}, dimensions={0}, use_global_device_ids=true | all-gather | bytes 2304 | tf_op jit(solution)/shard_map/all_gather | solution.py:90
  23.1 1.1 fusion.41
  24.2 1.1 fusion.35
  25.3 1.2 fusion.22
  26.5 1.2 fusion.23
  28.6 3.4 %all-to-all-start = ((bf16[16,16,512]{2,1,0:T(8,128)(2,1)}), bf16[16,16,512]{2,1,0:T(8,128)(2,1)S(1)}, u32[]{:S(2)}, u32[]{:S(2)}) async-start(bf16[16,16,512]{2,1,0:T(8,128)(2,1)} %copy.13), calls=%async_computation | async-start | bytes 524288 | tf_op jit(solution)/shard_map/all_to_all | solution.py:92
  32.0 1.3 dynamic-slice
  33.9 1.0 fusion.32
  34.9 1.1 negate_convert_fusion
  36.9 3.3 %all-to-all-done = bf16[16,16,512]{2,1,0:T(8,128)(2,1)S(1)} async-done(((bf16[16,16,512]{2,1,0:T(8,128)(2,1)}), bf16[16,16,512]{2,1,0:T(8,128)(2,1)S(1)}, u32[]{:S(2)}, u32[]{:S(2)}) %all-to-all-start) | async-done | bytes 262176 | tf_op jit(solution)/shard_map/all_to_all | solution.py:92
  40.2 2.2 %all_gather.7 = bf16[2,256,512]{2,1,0:T(8,128)(2,1)S(1)} all-gather(bf16[2,128,512]{2,1,0:T(8,128)(2,1)S(1)} %bitcast.70), channel_id=1, replica_groups=mesh['cuts'=2,'frame'=8,'coil'=2] {'coil'}, dimensions={1}, use_global_device_ids=true | all-gather | bytes 786432 | tf_op jit(solution)/shard_map/all_gather | solution.py:93
  42.4 62.9 %while.10 = (s32[]{:T(128)}, f32[2,256,512]{2,0,1:T(2,128)}, bf16[16,256,512]{2,1,0:T(8,128)(2,1)}, s32[2,256]{1,0:T(2,128)S(1)}, bf16[2,256,512]{2,1,0:T(8,128)...) while((s32[]{:T(128)}, f32[2,256,512]{2,0,1:T(2,128)}, ...), condition=%wide.region_3.4_spmd, body=%wide.region_0.3_spmd.sunk | while | flops 4330750976 | bytes 107749048 | solution.py:94
  42.5 3.4 %convert_element_type.64 = f32[16,256,512]{2,1,0:T(8,128)S(1)} convert(bf16[16,256,512]{2,1,0:T(8,128)(2,1)} %get-tuple-element.137) | non-fusion elementwise | flops 2097152 | bytes 12582912 | tf_op jit(solution)/shard_map/while/body/eval_jaxpr/convert_element_type | solution.py:65
  45.9 3.0 %subtract_convert_fusion.2 = (bf16[16,256,256]{2,1,0:T(8,128)(2,1)S(1)}, bf16[16,256,256]{2,1,0:T(8,128)(2,1)}) fusion(f32[16,256,512]{2,1,0:T(8,128)S(1)} %convert_element_type.64, f32[256,256]{1,0:T(8,128)S(1)} %get-tuple-element.111, f32[256,256]{1,0:T(8,128)S(1)} %get-tuple-element.112), kind=kLoop, calls=%fused_computation.13.clone.1 | loop fusion | flops 8388608 | bytes 13107200 | tf_op jit(solution)/shard_map/convert.2
  49.7 10.8 %fusion.65 = f32[16,256,512]{2,1,0:T(8,128)} fusion(bf16[2,16,256,512]{3,2,1,0:T(8,128)(2,1)} %get-tuple-element.141, s32[]{:T(128)} %get-tuple-element.126, f32[512]{0:T(512)S(1)} %add_convert_fusion.3, bf16[16,256,256]{2,1,0:T(8,128)(2,1)} %get-tuple-element.113, bf16[16,256,256]{2,1,0:T(8,128)(2,1)S(1)} %get-tuple-element.114, ...), kind=kOutput, calls=%fused_computation.3.clone.1 | convolution fusion | flops 4311744512 | bytes 17828352 | tf_op jit(solution)/shard_map/while/body/eval_jaxpr/dot_general | solution.py:77
  60.5 7.0 %add_reduce_fusion.2 = (f32[256,256]{1,0:T(8,128)S(1)}, f32[256,256]{1,0:T(8,128)S(1)}) fusion(f32[16,256,512]{2,1,0:T(8,128)} %fusion.65, f32[16,256,512]{2,1,0:T(8,128)} %copy-done), kind=kLoop, calls=%fused_computation.10.clone.1 | loop fusion | flops 8257536 | bytes 17301504 | tf_op jit(solution)/shard_map/while/body/eval_jaxpr/reduce_sum | solution.py:83
  68.2 4.7 %dynamic_update_slice.5 = f32[2,256,512]{2,0,1:T(2,128)S(1)} dynamic-update-slice(f32[2,256,512]{2,0,1:T(2,128)S(1)} %copy-done.2, f32[1,256,512]{2,0,1:T(1,128)S(1)} %copy.22, s32[]{:T(128)} %get-tuple-element.126, s32[]{:T(128)} %constant.31.clone.1..sunk, s32[]{:T(128)} %constant.31.clone.1..sunk) | dynamic-update-slice | bytes 1048580 | tf_op jit(solution)/shard_map/while/body/jit(dynamic_update_index_in_dim)/dynamic_update_slice | solution.py:94
  72.9 1.0 copy-done.3
  74.0 3.3 %convert_element_type.64 = f32[16,256,512]{2,1,0:T(8,128)S(1)} convert(bf16[16,256,512]{2,1,0:T(8,128)(2,1)} %get-tuple-element.137) | non-fusion elementwise | flops 2097152 | bytes 12582912 | tf_op jit(solution)/shard_map/while/body/eval_jaxpr/convert_element_type | solution.py:65
  77.3 3.0 %subtract_convert_fusion.2 = (bf16[16,256,256]{2,1,0:T(8,128)(2,1)S(1)}, bf16[16,256,256]{2,1,0:T(8,128)(2,1)}) fusion(f32[16,256,512]{2,1,0:T(8,128)S(1)} %convert_element_type.64, f32[256,256]{1,0:T(8,128)S(1)} %get-tuple-element.111, f32[256,256]{1,0:T(8,128)S(1)} %get-tuple-element.112), kind=kLoop, calls=%fused_computation.13.clone.1 | loop fusion | flops 8388608 | bytes 13107200 | tf_op jit(solution)/shard_map/convert.2
  80.3 0.9 copy-done
  81.2 10.8 %fusion.65 = f32[16,256,512]{2,1,0:T(8,128)} fusion(bf16[2,16,256,512]{3,2,1,0:T(8,128)(2,1)} %get-tuple-element.141, s32[]{:T(128)} %get-tuple-element.126, f32[512]{0:T(512)S(1)} %add_convert_fusion.3, bf16[16,256,256]{2,1,0:T(8,128)(2,1)} %get-tuple-element.113, bf16[16,256,256]{2,1,0:T(8,128)(2,1)S(1)} %get-tuple-element.114, ...), kind=kOutput, calls=%fused_computation.3.clone.1 | convolution fusion | flops 4311744512 | bytes 17828352 | tf_op jit(solution)/shard_map/while/body/eval_jaxpr/dot_general | solution.py:77
  91.9 7.0 %add_reduce_fusion.2 = (f32[256,256]{1,0:T(8,128)S(1)}, f32[256,256]{1,0:T(8,128)S(1)}) fusion(f32[16,256,512]{2,1,0:T(8,128)} %fusion.65, f32[16,256,512]{2,1,0:T(8,128)} %copy-done), kind=kLoop, calls=%fused_computation.10.clone.1 | loop fusion | flops 8257536 | bytes 17301504 | tf_op jit(solution)/shard_map/while/body/eval_jaxpr/reduce_sum | solution.py:83
  99.6 4.7 %dynamic_update_slice.5 = f32[2,256,512]{2,0,1:T(2,128)S(1)} dynamic-update-slice(f32[2,256,512]{2,0,1:T(2,128)S(1)} %copy-done.2, f32[1,256,512]{2,0,1:T(1,128)S(1)} %copy.22, s32[]{:T(128)} %get-tuple-element.126, s32[]{:T(128)} %constant.31.clone.1..sunk, s32[]{:T(128)} %constant.31.clone.1..sunk) | dynamic-update-slice | bytes 1048580 | tf_op jit(solution)/shard_map/while/body/jit(dynamic_update_index_in_dim)/dynamic_update_slice | solution.py:94
  104.3 1.0 copy-done.3
  105.3 6.9 %all-reduce.3 = bf16[2,256,512]{2,0,1:T(2,128)(2,1)S(1)} all-reduce(f32[2,256,512]{2,0,1:T(2,128)} %get-tuple-element.39), channel_id=2, replica_groups=mesh['cuts'=2,'frame'=8,'coil'=2] {'coil'}, use_global_device_ids=true, to_apply=%region_4.5.clone | all-reduce | flops 262144 | bytes 1572864
  112.2 0.9 dynamic-slice_convert_fusion
  113.1 3.4 %all-to-all-start.1 = ((bf16[2,128,512]{2,0,1:T(2,128)(2,1)}), bf16[2,128,512]{2,0,1:T(2,128)(2,1)S(1)}, u32[]{:S(2)}, u32[]{:S(2)}) async-start(bf16[2,128,512]{2,0,1:T(2,128)(2,1)} %dynamic-slice_convert_fusion), calls=%async_computation.1 | async-start | bytes 524288 | tf_op jit(solution)/shard_map/all_to_all | solution.py:103
  117.7 8.4 %all-to-all-done.1 = bf16[2,128,512]{2,0,1:T(2,128)(2,1)S(1)} async-done(((bf16[2,128,512]{2,0,1:T(2,128)(2,1)}), bf16[2,128,512]{2,0,1:T(2,128)(2,1)S(1)}, u32[]{:S(2)}, u32[]{:S(2)}) %all-to-all-start.1) | async-done | bytes 262176 | tf_op jit(solution)/shard_map/all_to_all | solution.py:103
  127.9 19.6 %all-reduce.1 = f32[16,64]{1,0:T(8,128)S(1)} all-reduce(f32[16,64]{1,0:T(8,128)S(1)} %pad_maximum_fusion.2), channel_id=3, replica_groups=mesh['cuts'=2,'frame'=8,'coil'=2] {'frame'}, use_global_device_ids=true, to_apply=%region_5.6.clone | all-reduce | flops 1024 | bytes 8192
  147.6 3.0 %psum.7 = f32[2,64]{1,0:T(2,128)} all-reduce(f32[2,64]{1,0:T(2,128)S(1)} %constant_dynamic-slice_fusion.1), channel_id=1, replica_groups=mesh['cuts'=2,'frame'=8,'coil'=2] {'coil'}, use_global_device_ids=true, to_apply=%region_6.7 | all-reduce | flops 128 | bytes 1024 | tf_op jit(solution)/shard_map/psum | solution.py:108
  151.3 1.1 pad_maximum_fusion
  (45 shorter events, 7.0 us)
Async XLA Ops:
  0.6 41.7 %copy-start.4 = (s32[2,256]{1,0:T(2,128)S(1)}, s32[2,256]{1,0:T(2,128)}, u32[]{:S(2)}) copy-start(s32[2,256]{1,0:T(2,128)} %param.10) | copy-start | bytes 6148
  28.6 11.6 %all-to-all-start = ((bf16[16,16,512]{2,1,0:T(8,128)(2,1)}), bf16[16,16,512]{2,1,0:T(8,128)(2,1)S(1)}, u32[]{:S(2)}, u32[]{:S(2)}) async-start(bf16[16,16,512]{2,1,0:T(8,128)(2,1)} %copy.13), calls=%async_computation | async-start | bytes 524288 | tf_op jit(solution)/shard_map/all_to_all | solution.py:92
  42.4 74.1 %copy-start.5 = (u32[32]{0:T(128)S(1)}, u32[32]{0:T(128)}, u32[]{:S(2)}) copy-start(u32[32]{0:T(128)} %constant.47) | copy-start | bytes 388
  42.4 84.1 %copy-start.1 = (bf16[16,32,512]{2,1,0:T(8,128)(2,1)S(1)}, bf16[16,32,512]{2,1,0:T(8,128)(2,1)}, u32[]{:S(2)}) copy-start(bf16[16,32,512]{2,1,0:T(8,128)(2,1)} %param.7) | copy-start | bytes 1572868
  45.9 3.8 %copy-start = (f32[16,256,512]{2,1,0:T(8,128)}, f32[16,256,512]{2,1,0:T(8,128)S(1)}, u32[]{:S(2)}) copy-start(f32[16,256,512]{2,1,0:T(8,128)S(1)} %convert_element_type.64) | copy-start | bytes 25165828 | tf_op jit(solution)/shard_map/while
  60.5 7.6 %copy-start.2 = (f32[2,256,512]{2,0,1:T(2,128)S(1)}, f32[2,256,512]{2,0,1:T(2,128)}, u32[]{:S(2)}) copy-start(f32[2,256,512]{2,0,1:T(2,128)} %get-tuple-element.127) | copy-start | bytes 3145732 | tf_op jit(solution)/shard_map/while
  72.9 1.0 copy-start.3
  77.3 3.8 %copy-start = (f32[16,256,512]{2,1,0:T(8,128)}, f32[16,256,512]{2,1,0:T(8,128)S(1)}, u32[]{:S(2)}) copy-start(f32[16,256,512]{2,1,0:T(8,128)S(1)} %convert_element_type.64) | copy-start | bytes 25165828 | tf_op jit(solution)/shard_map/while
  91.9 7.6 %copy-start.2 = (f32[2,256,512]{2,0,1:T(2,128)S(1)}, f32[2,256,512]{2,0,1:T(2,128)}, u32[]{:S(2)}) copy-start(f32[2,256,512]{2,0,1:T(2,128)} %get-tuple-element.127) | copy-start | bytes 3145732 | tf_op jit(solution)/shard_map/while
  104.3 1.0 copy-start.3
  113.1 13.1 %all-to-all-start.1 = ((bf16[2,128,512]{2,0,1:T(2,128)(2,1)}), bf16[2,128,512]{2,0,1:T(2,128)(2,1)S(1)}, u32[]{:S(2)}, u32[]{:S(2)}) async-start(bf16[2,128,512]{2,0,1:T(2,128)(2,1)} %dynamic-slice_convert_fusion), calls=%async_computation.1 | async-start | bytes 524288 | tf_op jit(solution)/shard_map/all_to_all | solution.py:103
where the time goes:
time: 153 us; the launch traced here: 152 us
  blocking collectives  54.2 us (35%)
  other arithmetic  31 us (20%)
  matrix products  28.1 us (18%)
  local copies, waits for them, and re-layouts  18.2 us (12%)
  waiting for transfers between devices  11.7 us (8%)
  starting transfers between devices  6.82 us (4%)
  between operations  2.1 us (1%)
    unnamed x2, blocking collectives  26.5 us
    all_gather x1, blocking collectives, on_device(): temporal_all = lax.all_gather(temporal, 'frame', axis=0, tiled=True)  22.5 us
    dot_general x2, matrix products, coil_adjoint(): jnp.dot(misfit.reshape(coil_count * row_count, full_width), block.T, pref...  21.6 us
    reduce_sum x2, other arithmetic, coil_adjoint(): grad_real = jnp.sum(sens_real * back_real + sens_imag * back_imag, axis=0)  14 us
    dynamic_update_slice x4, local copies, waits for them, and re-layouts, on_device(): lax.map(lambda frame_item: coil_adjoint(frame_item[0], frame_item[1], fra...  10.5 us
    all_to_all x1, waiting for transfers between devices, on_device(): lax.all_to_all(grad_half, 'frame', split_axis=1, concat_axis=0, tiled=True)  8.41 us
    another operation x4, other arithmetic  8 us
    convert_element_type x2, other arithmetic, coil_adjoint(): sens_real, sens_imag = split_parts(sensitivity.astype(jnp.float32))  6.72 us
  transfers between devices with their start and end apart: 2, of which 2 were waited for; matrix products, arithmetic and copies ran while one was open for 3% of the time, Pallas kernels for 0%

commit v1 on v0

v1 whole, which is shorter than its diff:
```python
import functools
import math

import jax
import jax.numpy as jnp
from jax import lax
from jax.experimental import pallas as pl
from jax.experimental.pallas import tpu as pltpu
from jax.sharding import PartitionSpec as P

F32 = jnp.float32
BF16 = jnp.bfloat16


def dft_block(length):
    index = jnp.arange(length, dtype=jnp.int32)
    angles = (index[:, None] * index[None, :] % length).astype(F32) * (2.0 * math.pi / length)
    norm_factor = 1.0 / math.sqrt(length)
    cosine = jnp.cos(angles) * norm_factor
    sine_part = -jnp.sin(angles) * norm_factor
    upper_rows = jnp.concatenate([cosine, sine_part], 1)
    lower_rows = jnp.concatenate([-sine_part, cosine], 1)
    return jnp.concatenate([upper_rows, lower_rows], 0).astype(BF16)


def dot(a, b):
    return jnp.dot(a, b, preferred_element_type=F32)


def dot_t(a, b):
    return lax.dot_general(a, b, (((1,), (1,)), ((), ())), preferred_element_type=F32)


def iota(shape, axis):
    return lax.broadcasted_iota(jnp.int32, shape, axis)


def spread(factors, total, rows, rank):
    groups, lanes = factors.shape
    per = total // groups
    height = 2 * total * rows
    frame = iota((height, groups), 0) // rows % total
    pick = jnp.where(frame // per == iota((height, groups), 1), 1.0, 0.0).astype(BF16)
    picked = dot(pick, factors)
    row = iota((height, lanes), 0)
    lane = iota((height, lanes), 1)
    mine = (lane // rank) == (row // rows % total % per) * 2 + row // (total * rows)
    return jnp.where(mine, picked, 0.0).astype(BF16)


def image_kernel(total, rows, rank, factors_ref, spatial_ref, image_ref):
    mid = spread(factors_ref[...], total, rows, rank)
    lanes = mid.shape[1]
    width = rows * rank
    tile = jnp.where(iota((lanes, width), 0) % rank == iota((lanes, width), 1) % rank, 1.0, 0.0)
    wide = dot(mid, tile.astype(BF16))
    height = wide.shape[0]
    same = iota((height, width), 0) % rows == iota((height, width), 1) // rank
    wide = jnp.where(same, wide, 0.0).astype(BF16)
    product = dot(wide, spatial_ref[...])
    half = height // 2
    mid_col = product.shape[1] // 2
    image_ref[:, :mid_col] = (product[:half, :mid_col] - product[half:, mid_col:]).astype(BF16)
    image_ref[:, mid_col:] = (product[:half, mid_col:] + product[half:, :mid_col]).astype(BF16)


def both_parts(grad):
    half = grad.shape[1] // 2
    turned = jnp.concatenate([grad[:, half:], -grad[:, :half]], 1)
    return jnp.concatenate([grad, turned], 0)


def spatial_kernel(total, rows, rank, factors_ref, grad_ref, out_ref):
    mid = spread(factors_ref[...], total, rows, rank)
    lanes = mid.shape[1]
    width = rows * rank
    tile = jnp.where(iota((width, lanes), 0) % rank == iota((width, lanes), 1) % rank, 1.0, 0.0)
    wide = dot_t(tile.astype(BF16), mid)
    height = mid.shape[0]
    same = iota((width, height), 1) % rows == iota((width, height), 0) // rank
    wide = jnp.where(same, wide, 0.0).astype(BF16)
    out_ref[...] = dot(wide, both_parts(grad_ref[...]))


def temporal_kernel(total, rows, rank, spatial_ref, grad_ref, out_ref):
    product = dot_t(both_parts(grad_ref[...]), spatial_ref[...])
    height, width = product.shape
    same = iota((height, width), 0) % rows == iota((height, width), 1) // rank
    product = jnp.where(same, product, 0.0)
    lanes = 128
    fold = product[:, :lanes]
    for start in range(lanes, width, lanes):
        fold = fold + product[:, start : start + lanes]
    if rows % 8 == 0:
        fold = jnp.sum(fold.reshape(2 * total, rows, lanes), axis=1)
    else:
        pick = iota((2 * total, height), 0) == iota((2 * total, height), 1) // rows
        fold = jnp.dot(
            jnp.where(pick, 1.0, 0.0), fold, precision=lax.Precision.HIGHEST, preferred_element_type=F32
        )
    shift = lanes // 2
    while shift >= rank:
        fold = fold + pltpu.roll(fold, shift, 1)
        shift //= 2
    lane = iota((total, lanes), 1)
    both = jnp.where(lane < rank, fold[:total], fold[total:])
    groups, copies, per, span = out_ref.shape
    for group in range(groups):
        for copy in range(copies):
            out_ref[group, copy] = both[group * per : (group + 1) * per, :span]


def conj_sum(adjoint, sens_r, sens_i):
    half = sens_r.shape[-1]
    back_r, back_i = adjoint[..., :half], adjoint[..., half:]
    return (
        jnp.sum(sens_r * back_r + sens_i * back_i, axis=0),
        jnp.sum(sens_r * back_i - sens_i * back_r, axis=0),
    )


def data_kernel(kspace_ref, sens_ref, back_ref, out_ref):
    frames, coils, rows, width = kspace_ref.shape
    half = width // 2
    sens = sens_ref[...].astype(F32)
    sens_r, sens_i = sens[..., :half], sens[..., half:]
    for t in range(frames):
        adjoint = dot(kspace_ref[t].reshape(coils * rows, width), back_ref[t])
        real, imag = conj_sum(adjoint.reshape(coils, rows, width), sens_r, sens_i)
        out_ref[t, :, :half] = real
        out_ref[t, :, half:] = imag


def normal_kernel(part_ref, image_ref, sens_ref, normal_ref, data_ref, out_ref):
    groups, frames, per, width = image_ref.shape
    coils, rows, _ = sens_ref.shape
    half = width // 2
    sens = sens_ref[...].astype(F32)
    sens_r, sens_i = sens[..., :half], sens[..., half:]
    for t in range(frames):
        image = image_ref[:, t].reshape(rows, width).astype(F32)
        image_r, image_i = image[:, :half], image[:, half:]
        coil_r = (sens_r * image_r - sens_i * image_i).astype(BF16)
        coil_i = (sens_r * image_i + sens_i * image_r).astype(BF16)
        coil = jnp.concatenate([coil_r, coil_i], -1).reshape(coils * rows, width)
        adjoint = dot(coil, normal_ref[t])
        real, imag = conj_sum(adjoint.reshape(coils, rows, width), sens_r, sens_i)
        out_ref[:, t, :, :half] = (real - data_ref[t, :, :half]).reshape(groups, per, half)
        out_ref[:, t, :, half:] = (imag - data_ref[t, :, half:]).reshape(groups, per, half)


def whole(shape):
    return pl.BlockSpec(shape, lambda *_: (0,) * len(shape))


def cost(flops, moved):
    return pl.CostEstimate(flops=int(flops), bytes_accessed=int(moved), transcendentals=0)


def data_term(kspace, sens, back, tile):
    frames, coils, rows, width = kspace.shape
    return pl.pallas_call(
        data_kernel,
        grid=(rows // tile,),
        in_specs=[
            pl.BlockSpec((frames, coils, tile, width), lambda i: (0, 0, i, 0)),
            pl.BlockSpec((coils, tile, width), lambda i: (0, i, 0)),
            whole(back.shape),
        ],
        out_specs=pl.BlockSpec((frames, tile, width), lambda i: (0, i, 0)),
        out_shape=jax.ShapeDtypeStruct((frames, rows, width), F32),
        cost_estimate=cost(2 * frames * coils * rows * width * width, 2 * kspace.size + 2 * sens.size),
        name="data_term",
    )(kspace, sens, back)


def normal_term(part, image, sens, normal, data, tile):
    groups, frames, per, width = image.shape
    coils = sens.shape[0]
    step = tile // per
    steps = groups // step
    return pl.pallas_call(
        normal_kernel,
        grid_spec=pltpu.PrefetchScalarGridSpec(
            num_scalar_prefetch=1,
            grid=(steps,),
            in_specs=[
                pl.BlockSpec((step, frames, per, width), lambda i, part_ref: (i, 0, 0, 0)),
                pl.BlockSpec((coils, tile, width), lambda i, part_ref: (0, part_ref[0] * steps + i, 0)),
                pl.BlockSpec(normal.shape, lambda i, part_ref: (0, 0, 0)),
                pl.BlockSpec((frames, tile, width), lambda i, part_ref: (0, part_ref[0] * steps + i, 0)),
            ],
            out_specs=pl.BlockSpec((step, frames, per, width), lambda i, part_ref: (i, 0, 0, 0)),
        ),
        out_shape=jax.ShapeDtypeStruct((groups, frames, per, width), F32),
        cost_estimate=cost(
            2 * frames * coils * groups * per * width * width, coils * groups * per * width * 2
        ),
        name="normal_term",
    )(part, image, sens, normal, data)


def on_device(frame_size, coil_size, spatial, temporal, kspace, sampled, sensitivity):
    rows, rank, width = spatial.shape
    per = temporal.shape[0]
    total = per * frame_size
    half_rows = rows * frame_size
    swap = [(i, (i + 1) % coil_size) for i in range(coil_size)]
    own = lax.axis_index("coil")
    other = (own + 1) % coil_size
    spatial2 = spatial.reshape(rows * rank, width)

    lanes = per * 2 * rank
    factors = lax.all_to_all(
        jnp.broadcast_to(temporal.reshape(1, lanes), (frame_size, lanes)), "frame", 0, 0, tiled=True
    )

    block = dft_block(width // 2)
    keep = jnp.concatenate([sampled, sampled], 1).astype(BF16)
    back = block.T[None] * keep[:, :, None]
    normal = jnp.einsum("ij,tjk->tik", block, back, preferred_element_type=F32).astype(BF16)
    data = data_term(kspace, sensitivity, back, 32)

    image = pl.pallas_call(
        functools.partial(image_kernel, total, rows, rank),
        out_shape=jax.ShapeDtypeStruct((total * rows, width), BF16),
        name="image_rows",
    )(factors, spatial2)
    image = lax.all_to_all(
        image.reshape(frame_size, per, rows, width), "frame", 0, 0, tiled=True
    )
    regroup = rows % 16 != 0
    if regroup:
        image = image.transpose(1, 0, 2, 3).reshape(per, half_rows // 16, 16, width).transpose(1, 0, 2, 3)
    image_other = lax.ppermute(image, "coil", swap)
    send = normal_term(other.reshape(1), image_other, sensitivity, normal, data, 32)
    received = lax.ppermute(send, "coil", swap)
    keep_own = normal_term(own.reshape(1), image, sensitivity, normal, data, 32)
    grad = (keep_own + received).astype(BF16)
    if regroup:
        grad = grad.transpose(1, 0, 2, 3).reshape(per, frame_size, rows, width).transpose(1, 0, 2, 3)
    grad = lax.all_to_all(grad, "frame", 0, 0, tiled=True).reshape(total * rows, width)

    partial = pl.pallas_call(
        functools.partial(temporal_kernel, total, rows, rank),
        out_shape=jax.ShapeDtypeStruct((frame_size, coil_size, per, 2 * rank), F32),
        name="temporal_rows",
    )(spatial2, grad)
    partial = partial.reshape(frame_size * coil_size, per, 2 * rank)
    partial = lax.all_to_all(partial, ("frame", "coil"), 0, 0, tiled=True)
    spatial_grad = pl.pallas_call(
        functools.partial(spatial_kernel, total, rows, rank),
        out_shape=jax.ShapeDtypeStruct((rows * rank, width), F32),
        name="spatial_rows",
    )(factors, grad)
    return (spatial_grad.reshape(rows, rank, width), jnp.sum(partial, axis=0))


def solution(mesh):
    placed = (
        P(("cuts", "coil", "frame"), None, None),
        P(("cuts", "frame"), None),
        P(("cuts", "frame"), "coil", None, None),
        P(("cuts", "frame"), None),
        P(("cuts", "coil"), None, None),
    )
    return jax.shard_map(
        functools.partial(on_device, mesh.shape["frame"], mesh.shape["coil"]),
        mesh=mesh,
        in_specs=placed,
        out_specs=(P(("cuts", "coil", "frame"), None, None), P(("cuts", "frame"), None)),
        check_vma=False,
    )
```

time: 153 us -> 81.1 us (0.53)
  blocking collectives: 54.2 us -> 15 us
  Pallas kernels: 0 us -> 29.6 us
  matrix products: 28.1 us -> 1.78 us
  other arithmetic: 31 us -> 6.37 us
  local copies, waits for them, and re-layouts: 18.2 us -> 4.81 us
  starting transfers between devices: 6.82 us -> 15 us
  waiting for transfers between devices: 11.7 us -> 7.12 us
    pallas_call x0 -> x6, Pallas kernels: none -> 29.6 us  [the longest x2 11.4 us: normal_term(): pl.pallas_call(normal_kernel, grid_spec=pltpu.PrefetchScalarGridSpec(num_...]
    unnamed x2 -> x0, blocking collectives: 26.5 us -> none
    dot_general x14 -> x1, matrix products: 28.1 us -> 1.78 us  [on_device(): jnp.einsum('ij,tjk->tik', block, back, preferred_element_type=F32)]
    all_gather x2 -> x0, blocking collectives: 24.6 us -> none  [the longest x1 22.5 us: on_device(): temporal_all = lax.all_gather(temporal, 'frame', axis=0, tiled=True)]
    all_to_all x0 -> x1, blocking collectives: none -> 15 us  [on_device(): lax.all_to_all(grad, 'frame', 0, 0, tiled=True).reshape(total * rows, width)]
    reduce_sum x2 -> x1, other arithmetic: 14 us -> 0.59 us  [on_device(): return (spatial_grad.reshape(rows, rank, width), jnp.sum(partial, axis=0))]
    dynamic_update_slice x4 -> x0, local copies, waits for them, and re-layouts: 10.5 us -> none  [on_device(): lax.map(lambda frame_item: coil_adjoint(frame_item[0], frame_item[1], fra...]
    all_to_all x2 -> x3, starting transfers between devices: 6.82 us -> 14.4 us  [the longest x1 7.31 us: on_device(): lax.all_to_all(jnp.broadcast_to(temporal.reshape(1, lanes), (frame_size,...]
  transfers between devices with their start and end apart: 2 -> 5, of which waited for: 2 -> 2; matrix products, arithmetic and copies ran while one was open for 3% -> 7% of each run, Pallas kernels for 0% -> 24%
where the time goes in v1:
time: 81.1 us; the launch traced here: 80.3 us
  Pallas kernels  29.6 us (36%)
  starting transfers between devices  15 us (18%)
  blocking collectives  15 us (18%)
  waiting for transfers between devices  7.12 us (9%)
  other arithmetic  6.37 us (8%)
  local copies, waits for them, and re-layouts  4.81 us (6%)
  matrix products  1.78 us (2%)
    all_to_all x1, blocking collectives, on_device(): lax.all_to_all(grad, 'frame', 0, 0, tiled=True).reshape(total * rows, width)  15 us
    pallas_call x2, Pallas kernels, normal_term(): pl.pallas_call(normal_kernel, grid_spec=pltpu.PrefetchScalarGridSpec(num_...  11.4 us
    pallas_call x1, Pallas kernels, data_term(): pl.pallas_call(data_kernel, grid=(rows // tile,), in_specs=[pl.BlockSpec(...  10.6 us
    all_to_all x1, starting transfers between devices, on_device(): lax.all_to_all(jnp.broadcast_to(temporal.reshape(1, lanes), (frame_size,...  7.31 us
    all_to_all x1, waiting for transfers between devices, on_device(): partial = lax.all_to_all(partial, ('frame', 'coil'), 0, 0, tiled=True)  3.75 us
    all_to_all x1, starting transfers between devices, on_device(): partial = lax.all_to_all(partial, ('frame', 'coil'), 0, 0, tiled=True)  3.69 us
    all_to_all x1, starting transfers between devices, on_device(): lax.all_to_all(image.reshape(frame_size, per, rows, width), 'frame', 0, 0...  3.41 us
    all_to_all x1, waiting for transfers between devices, on_device(): lax.all_to_all(jnp.broadcast_to(temporal.reshape(1, lanes), (frame_size,...  3.35 us
  transfers between devices with their start and end apart: 5, of which 2 were waited for; matrix products, arithmetic and copies ran while one was open for 7% of the time, Pallas kernels for 24%

profile of v1, /device:TPU:0, one launch (start us, length us, event | category | flops | bytes accessed | tf_op | source)
XLA Modules:
  0.0 80.3 jit_solution(14318934890472932701)
XLA Ops:
  0.6 0.7 broadcast_in_dim.4
  1.4 0.6 broadcast_in_dim.5
  2.0 7.3 %all-to-all-start = ((bf16[8,1,128]{2,1,0:T(2,128)(2,1)}), bf16[8,1,128]{2,1,0:T(2,128)(2,1)S(1)}, u32[]{:S(2)}, u32[]{:S(2)}) async-start(bf16[8,1,128]{2,1,0:T(2,128)(2,1)} %broadcast_in_dim.5), calls=%async_computation | async-start | bytes 8192 | tf_op jit(solution)/shard_map/all_to_all | solution.py:214
  9.3 1.1 %negate_convert_fusion = (bf16[256,256]{1,0:T(8,128)(2,1)S(1)}, bf16[256,256]{1,0:T(8,128)(2,1)S(1)}) fusion(), kind=kLoop, calls=%fused_computation.12 | loop fusion | flops 1310720 | bytes 262144 | tf_op jit(solution)/shard_map/convert.4
  10.4 1.0 %fusion.8 = bf16[256,256]{1,0:T(8,128)(2,1)S(1)} fusion(), kind=kLoop, calls=%fused_computation.18 | loop fusion | flops 1114112 | bytes 131072 | tf_op jit(solution)/shard_map/convert.7
  11.4 0.7 convert.21
  12.1 0.2 copy.13
  12.3 3.4 %all-to-all-done = bf16[8,1,128]{2,1,0:T(2,128)(2,1)S(1)} async-done(((bf16[8,1,128]{2,1,0:T(2,128)(2,1)}), bf16[8,1,128]{2,1,0:T(2,128)(2,1)S(1)}, u32[]{:S(2)}, u32[]{:S(2)}) %all-to-all-start) | async-done | bytes 2080 | tf_op jit(solution)/shard_map/all_to_all | solution.py:214
  15.7 0.6 copy.20
  16.3 2.5 %image_rows.1 = bf16[256,512]{1,0:T(8,128)(2,1)} custom-call(bf16[8,128]{1,0:T(8,128)(2,1)} %bitcast.24, bf16[512,512]{1,0:T(8,128)(2,1)} %bitcast.19), custom_call_target="tpu_custom_call" | custom-call | tf_op jit(solution)/shard_map/image_rows/pallas_call | solution.py:224
  18.7 3.4 %all-to-all-start.1 = ((bf16[8,2,16,512]{3,2,1,0:T(8,128)(2,1)}), bf16[8,2,16,512]{3,2,1,0:T(8,128)(2,1)S(1)}, u32[]{:S(2)}, u32[]{:S(2)}) async-start(bf16[8,2,16,512]{3,2,1,0:T(8,128)(2,1)} %bitcast.22), calls=%async_computation.1 | async-start | bytes 524288 | tf_op jit(solution)/shard_map/all_to_all | solution.py:229
  22.1 1.2 %broadcast_multiply_fusion.back_ref = bf16[2,512,512]{2,1,0:T(8,128)(2,1)} fusion(bf16[2,512]{1,0:T(2,128)(2,1)S(1)} %pad_maximum_fusion, bf16[512,512]{1,0:T(8,128)(2,1)S(1)} %copy.13), kind=kLoop, calls=%fused_computation.5 | loop fusion | flops 524288 | bytes 1574912 | tf_op jit(solution)/shard_map/mul | solution.py:220
  23.3 10.6 %data_term.1.data_ref = f32[2,256,512]{2,1,0:T(8,128)} custom-call(bf16[2,16,256,512]{3,2,1,0:T(8,128)(2,1)} %kspace_ref.1, bf16[16,256,512]{2,1,0:T(8,128)(2,1)} %sens_ref.5, bf16[2,512,512]{2,1,0:T(8,128)(2,1)} %broadcast_multiply_fusion.back_ref), custom_call_target="tpu_custom_call" | custom-call | flops 4294967296 | bytes 12582912 | tf_op jit(solution)/shard_map/data_term/pallas_call | solution.py:162
  34.0 0.0 all-to-all-done.1.image_ref
  34.0 0.1 collective-permute-start
  34.1 1.8 %fusion.normal_ref = bf16[2,512,512]{2,1,0:T(8,128)(2,1)} fusion(bf16[256,256]{1,0:T(8,128)(2,1)S(1)} %get-tuple-element.3, bf16[256,256]{1,0:T(8,128)(2,1)S(1)} %get-tuple-element.2, bf16[256,256]{1,0:T(8,128)(2,1)S(1)} %fusion.8, bf16[2,512]{1,0:T(2,128)(2,1)S(1)} %pad_maximum_fusion, bf16[512,512]{1,0:T(8,128)(2,1)S(1)} %copy.13), kind=kOutput, calls=%fused_computation.1 | convolution fusion | flops 541589504 | bytes 1968128 | tf_op jit(solution)/shard_map/ij,tjk->tik/dot_general | solution.py:221
  35.8 0.0 collective-permute-done.image_ref
  35.9 0.7 copy-done.1
  36.5 5.7 %normal_term.3 = f32[8,2,16,512]{3,2,1,0:T(8,128)} custom-call(s32[1]{0:T(128)} %bitcast.6.part_ref, bf16[8,2,16,512]{3,2,1,0:T(8,128)(2,1)} %copy-done.1, bf16[16,256,512]{2,1,0:T(8,128)(2,1)} %sens_ref.5, bf16[2,512,512]{2,1,0:T(8,128)(2,1)} %fusion.normal_ref, f32[2,256,512]{2,1,0:T(8,128)} %data_term.1.data_ref), custom_call_target="tpu_custom_call" | custom-call | flops 2147483648 | bytes 2097152 | tf_op jit(solution)/shard_map/normal_term/pallas_call | solution.py:182
  42.3 0.5 collective-permute-start.1
  42.8 5.7 %normal_term.2 = f32[8,2,16,512]{3,2,1,0:T(8,128)} custom-call(s32[1]{0:T(128)} %bitcast.part_ref, bf16[8,2,16,512]{3,2,1,0:T(8,128)(2,1)} %copy-done, bf16[16,256,512]{2,1,0:T(8,128)(2,1)} %sens_ref.5, bf16[2,512,512]{2,1,0:T(8,128)(2,1)} %fusion.normal_ref, f32[2,256,512]{2,1,0:T(8,128)} %data_term.1.data_ref), custom_call_target="tpu_custom_call" | custom-call | flops 2147483648 | bytes 2097152 | tf_op jit(solution)/shard_map/normal_term/pallas_call | solution.py:182
  48.5 1.1 %add_convert_fusion = bf16[8,2,16,512]{3,2,1,0:T(8,128)(2,1)S(1)} fusion(f32[8,2,16,512]{3,2,1,0:T(8,128)} %normal_term.2, f32[8,2,16,512]{3,2,1,0:T(8,128)S(1)} %collective-permute-done.1), kind=kLoop, calls=%fused_computation.4 | loop fusion | flops 262144 | bytes 1310720 | tf_op jit(solution)/shard_map/convert_element_type | solution.py:239
  49.6 15.0 %all_to_all.23 = bf16[8,2,16,512]{3,2,1,0:T(8,128)(2,1)} all-to-all(bf16[8,2,16,512]{3,2,1,0:T(8,128)(2,1)S(1)} %add_convert_fusion), channel_id=1, replica_groups=mesh['cuts'=2,'frame'=8,'coil'=2] {'frame'}, dimensions={0} | all-to-all | bytes 524288 | tf_op jit(solution)/shard_map/all_to_all | solution.py:242
  64.6 2.3 %temporal_rows.1 = f32[8,2,2,64]{3,2,1,0:T(2,128)} custom-call(bf16[512,512]{1,0:T(8,128)(2,1)} %bitcast.20, bf16[256,512]{1,0:T(8,128)(2,1)} %bitcast.17), custom_call_target="tpu_custom_call" | custom-call | tf_op jit(solution)/shard_map/temporal_rows/pallas_call | solution.py:244
  66.9 1.4 %reshape.58 = f32[16,1,128]{2,1,0:T(1,128)} reshape(f32[16,2,64]{2,1,0:T(2,128)} %bitcast.23) | data formatting | bytes 16384
  68.3 3.7 %all-to-all-start.3 = ((f32[16,1,128]{2,1,0:T(1,128)}), f32[16,1,128]{2,1,0:T(1,128)S(1)}, u32[]{:S(2)}, u32[]{:S(2)}) async-start(f32[16,1,128]{2,1,0:T(1,128)} %reshape.58), calls=%async_computation.3 | async-start | bytes 16384 | tf_op jit(solution)/shard_map/all_to_all | solution.py:250
  72.0 2.7 %spatial_rows.1 = f32[512,512]{1,0:T(8,128)} custom-call(bf16[8,128]{1,0:T(8,128)(2,1)} %bitcast.25, bf16[256,512]{1,0:T(8,128)(2,1)} %bitcast.18), custom_call_target="tpu_custom_call" | custom-call | tf_op jit(solution)/shard_map/spatial_rows/pallas_call | solution.py:251
  74.7 3.8 %all-to-all-done.3 = f32[16,1,128]{2,1,0:T(1,128)S(1)} async-done(((f32[16,1,128]{2,1,0:T(1,128)}), f32[16,1,128]{2,1,0:T(1,128)S(1)}, u32[]{:S(2)}, u32[]{:S(2)}) %all-to-all-start.3) | async-done | bytes 8224 | tf_op jit(solution)/shard_map/all_to_all | solution.py:250
  78.4 0.5 broadcast.26
  78.9 0.7 reduce
  79.6 0.1 reshape.59
  79.7 0.6 reduce_sum.9
  (6 shorter events, 0.0 us)
Async XLA Ops:
  2.0 13.7 %all-to-all-start = ((bf16[8,1,128]{2,1,0:T(2,128)(2,1)}), bf16[8,1,128]{2,1,0:T(2,128)(2,1)S(1)}, u32[]{:S(2)}, u32[]{:S(2)}) async-start(bf16[8,1,128]{2,1,0:T(2,128)(2,1)} %broadcast_in_dim.5), calls=%async_computation | async-start | bytes 8192 | tf_op jit(solution)/shard_map/all_to_all | solution.py:214
  18.7 15.2 %all-to-all-start.1 = ((bf16[8,2,16,512]{3,2,1,0:T(8,128)(2,1)}), bf16[8,2,16,512]{3,2,1,0:T(8,128)(2,1)S(1)}, u32[]{:S(2)}, u32[]{:S(2)}) async-start(bf16[8,2,16,512]{3,2,1,0:T(8,128)(2,1)} %bitcast.22), calls=%async_computation.1 | async-start | bytes 524288 | tf_op jit(solution)/shard_map/all_to_all | solution.py:229
  34.0 1.9 %copy-start = (bf16[8,2,16,512]{3,2,1,0:T(8,128)(2,1)}, bf16[8,2,16,512]{3,2,1,0:T(8,128)(2,1)S(1)}, u32[]{:S(2)}) copy-start(bf16[8,2,16,512]{3,2,1,0:T(8,128)(2,1)S(1)} %all-to-all-done.1.image_ref) | copy-start | bytes 786436
  34.0 1.9 %collective-permute-start = (bf16[8,2,16,512]{3,2,1,0:T(8,128)(2,1)S(1)}, bf16[8,2,16,512]{3,2,1,0:T(8,128)(2,1)S(1)}, u32[]{:S(2)}, u32[]{:S(2)}) collective-permute-start(bf16[8,2,16,512]{3,2,1,0:T(8,128)(2,1)S(1)} %all-to-all-done.1.image_ref), channel_id=1, source_target_pairs={{0,1},{1,0},{2,3},{3,2},{4,5},{5,4},{6,7},{7,6},{8,9},{9,8},{10,11... | collective-permute-start | bytes 786440 | tf_op jit(solution)/shard_map/ppermute | solution.py:235
  35.9 0.7 copy-start.1
  42.3 6.2 %collective-permute-start.1 = (f32[8,2,16,512]{3,2,1,0:T(8,128)}, f32[8,2,16,512]{3,2,1,0:T(8,128)S(1)}, u32[]{:S(2)}, u32[]{:S(2)}) collective-permute-start(f32[8,2,16,512]{3,2,1,0:T(8,128)} %normal_term.3), channel_id=1, source_target_pairs={{0,1},{1,0},{2,3},{3,2},{4,5},{5,4},{6,7},{7,6},{8,9},{9,8},{10,11... | collective-permute-start | bytes 1572872 | tf_op jit(solution)/shard_map/ppermute | solution.py:237
  68.3 10.1 %all-to-all-start.3 = ((f32[16,1,128]{2,1,0:T(1,128)}), f32[16,1,128]{2,1,0:T(1,128)S(1)}, u32[]{:S(2)}, u32[]{:S(2)}) async-start(f32[16,1,128]{2,1,0:T(1,128)} %reshape.58), calls=%async_computation.3 | async-start | bytes 16384 | tf_op jit(solution)/shard_map/all_to_all | solution.py:250

commit v2 on v1

v2 whole, which is shorter than its diff:
```python
import functools
import math

import jax
import jax.numpy as jnp
import numpy as np
from jax import lax
from jax.experimental import pallas as pl
from jax.experimental.pallas import tpu as pltpu
from jax.sharding import PartitionSpec as P

F32 = jnp.float32
BF16 = jnp.bfloat16


def dft_block(length):
    index = np.arange(length)
    angles = (index[:, None] * index[None, :] % length) * (2.0 * math.pi / length)
    cosine = np.cos(angles) / math.sqrt(length)
    sine_part = -np.sin(angles) / math.sqrt(length)
    block = np.block([[cosine, sine_part], [-sine_part, cosine]])
    return block.astype(np.float32).astype(BF16)


def dot(a, b):
    return jnp.dot(a, b, preferred_element_type=F32)


def dot_t(a, b):
    return lax.dot_general(a, b, (((1,), (1,)), ((), ())), preferred_element_type=F32)


def iota(shape, axis):
    return lax.broadcasted_iota(jnp.int32, shape, axis)


def spread(factors_ref, total, rows, rank):
    groups, per, lanes = factors_ref.shape
    height = 2 * total * rows
    frame = iota((height, groups), 0) // rows % total
    factors = factors_ref[...].astype(F32)
    picked = jnp.zeros((height, lanes), F32)
    for t in range(per):
        pick = jnp.where(frame == iota((height, groups), 1) * per + t, 1.0, 0.0).astype(BF16)
        picked = picked + dot(pick, factors[:, t].astype(BF16))
    mine = iota((height, lanes), 1) // rank == iota((height, lanes), 0) // (total * rows)
    return jnp.where(mine, picked, 0.0).astype(BF16)


def image_kernel(total, rows, rank, factors_ref, spatial_ref, image_ref):
    mid = spread(factors_ref, total, rows, rank)
    lanes = mid.shape[1]
    width = rows * rank
    tile = jnp.where(iota((lanes, width), 0) % rank == iota((lanes, width), 1) % rank, 1.0, 0.0)
    wide = dot(mid, tile.astype(BF16))
    height = wide.shape[0]
    same = iota((height, width), 0) % rows == iota((height, width), 1) // rank
    wide = jnp.where(same, wide, 0.0).astype(BF16)
    product = dot(wide, spatial_ref[...])
    half = height // 2
    mid_col = product.shape[1] // 2
    image_ref[:, :mid_col] = (product[:half, :mid_col] - product[half:, mid_col:]).astype(BF16)
    image_ref[:, mid_col:] = (product[:half, mid_col:] + product[half:, :mid_col]).astype(BF16)


def both_parts(grad):
    half = grad.shape[1] // 2
    turned = jnp.concatenate([grad[:, half:], -grad[:, :half]], 1)
    return jnp.concatenate([grad, turned], 0)


def spatial_kernel(total, rows, rank, factors_ref, grad_ref, out_ref):
    mid = spread(factors_ref, total, rows, rank)
    lanes = mid.shape[1]
    width = rows * rank
    tile = jnp.where(iota((width, lanes), 0) % rank == iota((width, lanes), 1) % rank, 1.0, 0.0)
    wide = dot_t(tile.astype(BF16), mid)
    height = mid.shape[0]
    same = iota((width, height), 1) % rows == iota((width, height), 0) // rank
    wide = jnp.where(same, wide, 0.0).astype(BF16)
    out_ref[...] = dot(wide, both_parts(grad_ref[...]))


def temporal_kernel(total, rows, rank, spatial_ref, grad_ref, out_ref):
    product = dot_t(both_parts(grad_ref[...]), spatial_ref[...])
    height, width = product.shape
    same = iota((height, width), 0) % rows == iota((height, width), 1) // rank
    product = jnp.where(same, product, 0.0)
    lanes = 128
    fold = product[:, :lanes]
    for start in range(lanes, width, lanes):
        fold = fold + product[:, start : start + lanes]
    if rows % 8 == 0:
        fold = jnp.sum(fold.reshape(2 * total, rows, lanes), axis=1)
    else:
        pick = iota((2 * total, height), 0) == iota((2 * total, height), 1) // rows
        fold = jnp.dot(
            jnp.where(pick, 1.0, 0.0), fold, precision=lax.Precision.HIGHEST, preferred_element_type=F32
        )
    shift = lanes // 2
    while shift >= rank:
        fold = fold + pltpu.roll(fold, shift, 1)
        shift //= 2
    lane = iota((total, lanes), 1)
    both = jnp.where(lane // rank % 2 == 0, fold[:total], fold[total:])
    groups, _, span = out_ref.shape
    per = span // (2 * rank)
    copies = groups * per // total
    place = iota((1, span), 1) // (2 * rank)
    for group in range(groups // copies):
        line = both[group * per : group * per + 1, :span]
        for t in range(1, per):
            line = jnp.where(place == t, both[group * per + t : group * per + t + 1, :span], line)
        for copy in range(copies):
            out_ref[group * copies + copy] = line


def sum_kernel(parts_ref, out_ref):
    line = jnp.sum(parts_ref[...], axis=0)
    per, span = out_ref.shape
    for t in range(per):
        out_ref[t : t + 1, :] = line[:, t * span : (t + 1) * span]


def conj_sum(adjoint, sens_r, sens_i):
    half = sens_r.shape[-1]
    back_r, back_i = adjoint[..., :half], adjoint[..., half:]
    return (
        jnp.sum(sens_r * back_r + sens_i * back_i, axis=0),
        jnp.sum(sens_r * back_i - sens_i * back_r, axis=0),
    )


def masked(block, sampled_ref, t):
    keep = sampled_ref[t : t + 1, :].astype(F32)
    return (block.astype(F32) * jnp.concatenate([keep, keep], 1)).astype(BF16)


def prepare_kernel(sampled_ref, block_ref, spatial_ref, normal_ref, staged_ref, sem):
    staging = pltpu.make_async_copy(spatial_ref, staged_ref, sem)
    staging.start()
    block = block_ref[...]
    for t in range(sampled_ref.shape[0]):
        normal_ref[t] = dot_t(masked(block, sampled_ref, t), block).astype(BF16)
    staging.wait()


def data_kernel(tile, ahead, sampled_ref, block_ref, kspace_ref, sens_ref, out_ref,
                block_held, back_held, kspace_held, sens_held, block_sem, kspace_sem, sens_sem):
    frames, coils, rows, width = kspace_ref.shape
    half = width // 2
    steps = rows // tile

    def fetch(step):
        slot = lax.rem(step, ahead + 1)
        place = pl.ds(step * tile, tile)
        return (
            pltpu.make_async_copy(kspace_ref.at[:, :, place], kspace_held.at[slot], kspace_sem.at[slot]),
            pltpu.make_async_copy(sens_ref.at[:, place], sens_held.at[slot], sens_sem.at[slot]),
        )

    def begin(step):
        for copy in fetch(step):
            copy.start()

    table = pltpu.make_async_copy(block_ref, block_held, block_sem)
    table.start()
    for step in range(min(ahead, steps)):
        begin(step)
    table.wait()
    block = block_held[...]
    for t in range(frames):
        back_held[t] = masked(block, sampled_ref, t).T

    @pl.loop(0, steps)
    def _(step):
        @pl.when(step + ahead < steps)
        def _():
            begin(step + ahead)

        for copy in fetch(step):
            copy.wait()
        place = pl.ds(step * tile, tile)
        slot = lax.rem(step, ahead + 1)
        sens = sens_held[slot].astype(F32)
        sens_r, sens_i = sens[..., :half], sens[..., half:]
        for t in range(frames):
            adjoint = dot(kspace_held[slot, t].reshape(coils * tile, width), back_held[t])
            real, imag = conj_sum(adjoint.reshape(coils, tile, width), sens_r, sens_i)
            out_ref[t, place, :half] = real
            out_ref[t, place, half:] = imag


def normal_kernel(tile, part_ref, image_ref, sens_ref, normal_ref, data_ref, out_ref, sens_held, sem):
    groups, frames, per, width = image_ref.shape
    coils = sens_ref.shape[0]
    half = width // 2
    step_groups = tile // per
    steps = groups // step_groups

    def spot(step):
        return pl.ds(pl.multiple_of(part_ref[0] * (groups * per) + step * tile, tile), tile)

    def fetch(step):
        return pltpu.make_async_copy(sens_ref.at[:, spot(step)], sens_held.at[step], sem.at[step])

    for step in range(steps):
        fetch(step).start()

    @pl.loop(0, steps)
    def _(step):
        place = spot(step)
        group = pl.ds(step * step_groups, step_groups)
        fetch(step).wait()
        sens = sens_held[step].astype(F32)
        sens_r, sens_i = sens[..., :half], sens[..., half:]
        for t in range(frames):
            image = image_ref[group, t].reshape(tile, width).astype(F32)
            image_r, image_i = image[:, :half], image[:, half:]
            coil_r = (sens_r * image_r - sens_i * image_i).astype(BF16)
            coil_i = (sens_r * image_i + sens_i * image_r).astype(BF16)
            coil = jnp.concatenate([coil_r, coil_i], -1).reshape(coils * tile, width)
            adjoint = dot(coil, normal_ref[t])
            real, imag = conj_sum(adjoint.reshape(coils, tile, width), sens_r, sens_i)
            shape = (step_groups, per, half)
            out_ref[group, t, :, :half] = (real - data_ref[t, place, :half]).reshape(shape)
            out_ref[group, t, :, half:] = (imag - data_ref[t, place, half:]).reshape(shape)


def cost(flops, moved):
    return pl.CostEstimate(flops=int(flops), bytes_accessed=int(moved), transcendentals=0)


VMEM = pl.BlockSpec(memory_space=pltpu.VMEM)
SMEM = pl.BlockSpec(memory_space=pltpu.SMEM)
HBM = pl.BlockSpec(memory_space=pltpu.HBM)
MIB = 1 << 20


def local(array):
    return pltpu.with_memory_space_constraint(array, pltpu.VMEM)


def remote(array):
    return pltpu.with_memory_space_constraint(array, pltpu.HBM)


def grant(mib):
    return pltpu.CompilerParams(vmem_limit_bytes=mib * MIB)


def prepare(sampled, block, spatial):
    frames = sampled.shape[0]
    return pl.pallas_call(
        prepare_kernel,
        in_specs=[VMEM, VMEM, HBM],
        out_specs=[VMEM, VMEM],
        out_shape=[pltpu.VMEM((frames, *block.shape), BF16), pltpu.VMEM(spatial.shape, BF16)],
        scratch_shapes=[pltpu.SemaphoreType.DMA],
        cost_estimate=cost(2 * frames * block.shape[0] ** 3, 4 * block.size),
        compiler_params=grant(12),
        name="prepare",
    )(sampled, block, remote(spatial))


def data_term(sampled, block, kspace, sens, tile, ahead):
    frames, coils, rows, width = kspace.shape
    return pl.pallas_call(
        functools.partial(data_kernel, tile, ahead),
        in_specs=[VMEM, HBM, HBM, HBM],
        out_specs=VMEM,
        out_shape=pltpu.VMEM((frames, rows, width), F32),
        scratch_shapes=[
            pltpu.VMEM((width, width), BF16),
            pltpu.VMEM((frames, width, width), BF16),
            pltpu.VMEM((ahead + 1, frames, coils, tile, width), BF16),
            pltpu.VMEM((ahead + 1, coils, tile, width), BF16),
            pltpu.SemaphoreType.DMA,
            pltpu.SemaphoreType.DMA((ahead + 1,)),
            pltpu.SemaphoreType.DMA((ahead + 1,)),
        ],
        cost_estimate=cost(2 * frames * coils * rows * width * width, 2 * kspace.size),
        compiler_params=grant(24),
        name="data_term",
    )(sampled, remote(block), remote(kspace), remote(sens))


def normal_term(part, image, sens, normal, data, tile):
    groups, frames, per, width = image.shape
    coils = sens.shape[0]
    steps = groups * per // tile
    return pl.pallas_call(
        functools.partial(normal_kernel, tile),
        in_specs=[SMEM, VMEM, HBM, VMEM, VMEM],
        out_specs=VMEM,
        out_shape=pltpu.VMEM((groups, frames, per, width), F32),
        scratch_shapes=[pltpu.VMEM((steps, coils, tile, width), BF16), pltpu.SemaphoreType.DMA((steps,))],
        cost_estimate=cost(
            2 * frames * coils * groups * per * width * width, coils * groups * per * width * 2
        ),
        compiler_params=grant(20),
        name="normal_term",
    )(part, image, remote(sens), normal, data)


def on_device(frame_size, coil_size, spatial, temporal, kspace, sampled, sensitivity):
    rows, rank, width = spatial.shape
    per = temporal.shape[0]
    total = per * frame_size
    half_rows = rows * frame_size
    swap = [(i, (i + 1) % coil_size) for i in range(coil_size)]
    own = lax.axis_index("coil")
    other = (own + 1) % coil_size
    spatial2 = spatial.reshape(rows * rank, width)

    factors = lax.all_to_all(
        jnp.broadcast_to(temporal[None], (frame_size, per, 2 * rank)), "frame", 0, 0, tiled=True
    )
    block = jnp.asarray(dft_block(width // 2))
    normal, spatial2 = prepare(sampled, block, spatial2)

    image = pl.pallas_call(
        functools.partial(image_kernel, total, rows, rank),
        in_specs=[VMEM, VMEM],
        out_specs=VMEM,
        out_shape=pltpu.VMEM((total * rows, width), BF16),
        compiler_params=grant(12),
        name="image_rows",
    )(local(factors), spatial2)
    image, sampled = lax.optimization_barrier((image, sampled))
    image = lax.all_to_all(image.reshape(frame_size, per, rows, width), "frame", 0, 0, tiled=True)
    data = data_term(sampled, block, kspace, sensitivity, 32, 3)
    image, data = lax.optimization_barrier((image, data))
    regroup = rows % 16 != 0
    if regroup:
        image = image.transpose(1, 0, 2, 3).reshape(per, half_rows // 16, 16, width).transpose(1, 0, 2, 3)
    image_other = lax.ppermute(image, "coil", swap)
    send = normal_term(other.reshape(1), local(image_other), sensitivity, normal, data, 32)
    received = lax.ppermute(send, "coil", swap)
    keep_own = normal_term(own.reshape(1), local(image), sensitivity, normal, data, 32)
    grad = (keep_own + received).astype(BF16)
    if regroup:
        grad = grad.transpose(1, 0, 2, 3).reshape(per, frame_size, rows, width).transpose(1, 0, 2, 3)
    grad = lax.all_to_all(grad, "frame", 0, 0, tiled=True).reshape(total * rows, width)
    grad = local(grad)

    partial = pl.pallas_call(
        functools.partial(temporal_kernel, total, rows, rank),
        in_specs=[VMEM, VMEM],
        out_specs=VMEM,
        out_shape=pltpu.VMEM((frame_size * coil_size, 1, per * 2 * rank), F32),
        compiler_params=grant(12),
        name="temporal_rows",
    )(spatial2, grad)
    partial = lax.all_to_all(partial, ("frame", "coil"), 0, 0, tiled=True)
    spatial_grad = pl.pallas_call(
        functools.partial(spatial_kernel, total, rows, rank),
        in_specs=[VMEM, VMEM],
        out_specs=VMEM,
        out_shape=jax.ShapeDtypeStruct((rows * rank, width), F32),
        compiler_params=grant(12),
        name="spatial_rows",
    )(local(factors), grad)
    temporal_grad = pl.pallas_call(
        sum_kernel,
        in_specs=[VMEM],
        out_specs=VMEM,
        out_shape=jax.ShapeDtypeStruct((per, 2 * rank), F32),
        compiler_params=grant(2),
        name="temporal_sum",
    )(partial)
    return (spatial_grad.reshape(rows, rank, width), temporal_grad)


def solution(mesh):
    placed = (
        P(("cuts", "coil", "frame"), None, None),
        P(("cuts", "frame"), None),
        P(("cuts", "frame"), "coil", None, None),
        P(("cuts", "frame"), None),
        P(("cuts", "coil"), None, None),
    )
    return jax.shard_map(
        functools.partial(on_device, mesh.shape["frame"], mesh.shape["coil"]),
        mesh=mesh,
        in_specs=placed,
        out_specs=(P(("cuts", "coil", "frame"), None, None), P(("cuts", "frame"), None)),
        check_vma=False,
    )
```

time: 81.1 us -> 68.1 us (0.84)
  Pallas kernels: 29.6 us -> 23.3 us
  other arithmetic: 6.37 us -> 0.11 us
  waiting for transfers between devices: 7.12 us -> 9.84 us
  matrix products: 1.78 us -> 0 us
  local copies, waits for them, and re-layouts: 4.81 us -> 3.65 us
    pallas_call x6 -> x8, Pallas kernels: 29.6 us -> 23.3 us  [the longest x2 8.82 us: normal_term(): pl.pallas_call(functools.partial(normal_kernel, tile), in_specs=[SMEM, VM...]
    another operation x3 -> x0, other arithmetic: 2.78 us -> none
    dot_general x1 -> x0, matrix products: 1.78 us -> none  [on_device(): jnp.einsum('ij,tjk->tik', block, back, preferred_element_type=F32)]
    ppermute x1, waiting for transfers between devices: 0.01 us -> 1.51 us  [on_device(): image_other = lax.ppermute(image, 'coil', swap)]
    mul x1 -> x0, other arithmetic: 1.18 us -> none  [on_device(): back = block.T[None] * keep[:, :, None]]
    convert_element_type x1, other arithmetic: 1.11 us -> 0.11 us  [on_device(): grad = (keep_own + received).astype(BF16)]
    all_to_all x1, waiting for transfers between devices: 3.75 us -> 4.69 us  [on_device(): partial = lax.all_to_all(partial, ('frame', 'coil'), 0, 0, tiled=True)]
    unnamed x7 -> x6, local copies, waits for them, and re-layouts: 2.75 us -> 2.4 us
  transfers between devices with their start and end apart: 5 -> 5, of which waited for: 2 -> 3; matrix products, arithmetic and copies ran while one was open for 7% -> 0% of each run, Pallas kernels for 24% -> 23%
where the time goes in v2:
time: 68.1 us; the launch traced here: 67.5 us
  Pallas kernels  23.3 us (34%)
  blocking collectives  15.2 us (22%)
  starting transfers between devices  14.7 us (22%)
  waiting for transfers between devices  9.84 us (14%)
  local copies, waits for them, and re-layouts  3.65 us (5%)
  between operations  0.73 us (1%)
    all_to_all x1, blocking collectives, on_device(): lax.all_to_all(grad, 'frame', 0, 0, tiled=True).reshape(total * rows, width)  15.2 us
    pallas_call x2, Pallas kernels, normal_term(): pl.pallas_call(functools.partial(normal_kernel, tile), in_specs=[SMEM, VM...  8.82 us
    pallas_call x1, Pallas kernels, data_term(): pl.pallas_call(functools.partial(data_kernel, tile, ahead), in_specs=[VME...  8.24 us
    all_to_all x1, starting transfers between devices, on_device(): lax.all_to_all(jnp.broadcast_to(temporal[None], (frame_size, per, 2 * ran...  7.31 us
    all_to_all x1, waiting for transfers between devices, on_device(): partial = lax.all_to_all(partial, ('frame', 'coil'), 0, 0, tiled=True)  4.69 us
    all_to_all x1, starting transfers between devices, on_device(): partial = lax.all_to_all(partial, ('frame', 'coil'), 0, 0, tiled=True)  3.69 us
    all_to_all x1, waiting for transfers between devices, on_device(): lax.all_to_all(jnp.broadcast_to(temporal[None], (frame_size, per, 2 * ran...  3.64 us
    all_to_all x1, starting transfers between devices, on_device(): lax.all_to_all(image.reshape(frame_size, per, rows, width), 'frame', 0, 0...  3.41 us
  transfers between devices with their start and end apart: 5, of which 3 were waited for; matrix products, arithmetic and copies ran while one was open for 0% of the time, Pallas kernels for 23%

profile of v2, /device:TPU:0, one launch (start us, length us, event | category | flops | bytes accessed | tf_op | source)
XLA Modules:
  0.0 67.5 jit_solution(5496037690771861569)
XLA Ops:
  0.6 1.2 %broadcast_in_dim.2 = bf16[8,2,64]{2,1,0:T(2,128)(2,1)} broadcast(bf16[2,64]{1,0:T(2,128)(2,1)} %param.7), dimensions={1,2} | broadcast | bytes 2304 | tf_op jit(solution)/shard_map/broadcast_in_dim | solution.py:317
  1.9 7.3 %all-to-all-start = ((bf16[8,2,64]{2,1,0:T(2,128)(2,1)}), bf16[8,2,64]{2,1,0:T(2,128)(2,1)S(1)}, u32[]{:S(2)}, u32[]{:S(2)}) async-start(bf16[8,2,64]{2,1,0:T(2,128)(2,1)} %broadcast_in_dim.2), calls=%async_computation | async-start | bytes 8192 | tf_op jit(solution)/shard_map/all_to_all | solution.py:316
  9.2 0.0 copy-start
  9.2 0.7 %copy-done = s32[2,256]{1,0:T(2,128)S(1)} copy-done((s32[2,256]{1,0:T(2,128)S(1)}, s32[2,256]{1,0:T(2,128)}, u32[]{:S(2)}) %copy-start) | copy-done | bytes 2072
  9.9 0.0 copy-start.2
  9.9 1.0 %copy-done.2 = bf16[512,512]{1,0:T(8,128)(2,1)S(1)} copy-done((bf16[512,512]{1,0:T(8,128)(2,1)S(1)}, bf16[512,512]{1,0:T(8,128)(2,1)}, u32[]{:S(2)}) %copy-start.2) | copy-done | bytes 524312
  10.9 1.0 %prepare.1 = (bf16[2,512,512]{2,1,0:T(8,128)(2,1)S(1)}, bf16[512,512]{1,0:T(8,128)(2,1)S(1)}) custom-call(s32[2,256]{1,0:T(2,128)S(1)} %copy-done, bf16[512,512]{1,0:T(8,128)(2,1)S(1)} %copy-done.2, bf16[512,512]{1,0:T(8,128)(2,1)} %bitcast.9), custom_call_target="tpu_custom_call" | custom-call | flops 536870912 | bytes 1048576 | tf_op jit(solution)/shard_map/prepare/pallas_call | solution.py:254
  12.0 3.6 %all-to-all-done.factors_ref = bf16[8,2,64]{2,1,0:T(2,128)(2,1)S(1)} async-done(((bf16[8,2,64]{2,1,0:T(2,128)(2,1)}), bf16[8,2,64]{2,1,0:T(2,128)(2,1)S(1)}, u32[]{:S(2)}, u32[]{:S(2)}) %all-to-all-start) | async-done | bytes 2080 | tf_op jit(solution)/shard_map/all_to_all | solution.py:316
  15.6 1.6 %image_rows.1 = bf16[256,512]{1,0:T(8,128)(2,1)} custom-call(bf16[8,2,64]{2,1,0:T(2,128)(2,1)S(1)} %all-to-all-done.factors_ref, bf16[512,512]{1,0:T(8,128)(2,1)S(1)} %get-tuple-element.8.spatial_ref), custom_call_target="tpu_custom_call" | custom-call | tf_op jit(solution)/shard_map/image_rows/pallas_call | solution.py:322
  17.2 3.4 %all-to-all-start.1 = ((bf16[8,2,16,512]{3,2,1,0:T(8,128)(2,1)}), bf16[8,2,16,512]{3,2,1,0:T(8,128)(2,1)S(1)}, u32[]{:S(2)}, u32[]{:S(2)}) async-start(bf16[8,2,16,512]{3,2,1,0:T(8,128)(2,1)} %bitcast.2), calls=%async_computation.1 | async-start | bytes 524288 | tf_op jit(solution)/shard_map/all_to_all | solution.py:331
  20.7 0.0 copy-start.1
  20.7 0.7 copy-done.1
  21.4 8.2 %data_term.1.data_ref = f32[2,256,512]{2,1,0:T(8,128)S(1)} custom-call(s32[2,256]{1,0:T(2,128)S(1)} %copy-done.1, bf16[512,512]{1,0:T(8,128)(2,1)} %constant.20.clone.block_ref, bf16[2,16,256,512]{3,2,1,0:T(8,128)(2,1)} %kspace_ref.1, bf16[16,256,512]{2,1,0:T(8,128)(2,1)} %sens_ref.5), custom_call_target="tpu_custom_call" | custom-call | flops 4294967296 | bytes 8388608 | tf_op jit(solution)/shard_map/data_term/pallas_call | solution.py:268
  29.6 0.0 all-to-all-done.1.image_ref
  29.6 0.1 collective-permute-start
  29.7 1.5 %collective-permute-done.image_ref = bf16[8,2,16,512]{3,2,1,0:T(8,128)(2,1)S(1)} collective-permute-done((bf16[8,2,16,512]{3,2,1,0:T(8,128)(2,1)S(1)}, bf16[8,2,16,512]{3,2,1,0:T(8,128)(2,1)S(1)}, u32[]{:S(2)}, u32[]{:S(2)}) %collective-permute-start) | collective-permute-done | bytes 262176 | tf_op jit(solution)/shard_map/ppermute | solution.py:337
  31.2 4.4 %normal_term.3 = f32[8,2,16,512]{3,2,1,0:T(8,128)S(1)} custom-call(s32[1]{0:T(128)} %bitcast.3.part_ref, bf16[8,2,16,512]{3,2,1,0:T(8,128)(2,1)S(1)} %collective-permute-done.image_ref, bf16[16,256,512]{2,1,0:T(8,128)(2,1)} %sens_ref.5, bf16[2,512,512]{2,1,0:T(8,128)(2,1)S(1)} %get-tuple-element.12.normal_ref, f32[2,256,512]{2,1,0:T(8,128)S(1)} %data_term.1.data_ref), custom_call_target="tpu_custom_call" | custom-call | flops 2147483648 | bytes 2097152 | tf_op jit(solution)/shard_map/normal_term/pallas_call | solution.py:292
  35.6 0.2 collective-permute-start.1
  35.8 4.4 %normal_term.2 = f32[8,2,16,512]{3,2,1,0:T(8,128)S(1)} custom-call(s32[1]{0:T(128)} %bitcast.part_ref, bf16[8,2,16,512]{3,2,1,0:T(8,128)(2,1)S(1)} %all-to-all-done.1.image_ref, bf16[16,256,512]{2,1,0:T(8,128)(2,1)} %sens_ref.5, bf16[2,512,512]{2,1,0:T(8,128)(2,1)S(1)} %get-tuple-element.12.normal_ref, f32[2,256,512]{2,1,0:T(8,128)S(1)} %data_term.1.data_ref), custom_call_target="tpu_custom_call" | custom-call | flops 2147483648 | bytes 2097152 | tf_op jit(solution)/shard_map/normal_term/pallas_call | solution.py:292
  40.2 0.0 collective-permute-done.1
  40.3 0.1 add_convert_fusion
  40.4 15.2 %all_to_all.20 = bf16[8,2,16,512]{3,2,1,0:T(8,128)(2,1)S(1)} all-to-all(bf16[8,2,16,512]{3,2,1,0:T(8,128)(2,1)S(1)} %add_convert_fusion), channel_id=1, replica_groups=mesh['cuts'=2,'frame'=8,'coil'=2] {'frame'}, dimensions={0} | all-to-all | bytes 524288 | tf_op jit(solution)/shard_map/all_to_all | solution.py:344
  55.5 1.2 %temporal_rows.1 = f32[16,1,128]{2,1,0:T(1,128)} custom-call(bf16[512,512]{1,0:T(8,128)(2,1)S(1)} %get-tuple-element.8.spatial_ref, bf16[256,512]{1,0:T(8,128)(2,1)S(1)} %bitcast.6), custom_call_target="tpu_custom_call" | custom-call | tf_op jit(solution)/shard_map/temporal_rows/pallas_call | solution.py:347
  56.8 3.7 %all-to-all-start.3 = ((f32[16,1,128]{2,1,0:T(1,128)}), f32[16,1,128]{2,1,0:T(1,128)S(1)}, u32[]{:S(2)}, u32[]{:S(2)}) async-start(f32[16,1,128]{2,1,0:T(1,128)} %temporal_rows.1), calls=%async_computation.3 | async-start | bytes 16384 | tf_op jit(solution)/shard_map/all_to_all | solution.py:355
  60.5 1.7 %spatial_rows.1 = f32[512,512]{1,0:T(8,128)} custom-call(bf16[8,2,64]{2,1,0:T(2,128)(2,1)S(1)} %all-to-all-done.factors_ref, bf16[256,512]{1,0:T(8,128)(2,1)S(1)} %bitcast.7), custom_call_target="tpu_custom_call" | custom-call | tf_op jit(solution)/shard_map/spatial_rows/pallas_call | solution.py:356
  62.2 4.7 %all-to-all-done.3.parts_ref = f32[16,1,128]{2,1,0:T(1,128)S(1)} async-done(((f32[16,1,128]{2,1,0:T(1,128)}), f32[16,1,128]{2,1,0:T(1,128)S(1)}, u32[]{:S(2)}, u32[]{:S(2)}) %all-to-all-start.3) | async-done | bytes 8224 | tf_op jit(solution)/shard_map/all_to_all | solution.py:355
  66.9 0.6 temporal_sum.1
Async XLA Ops:
  1.9 13.7 %all-to-all-start = ((bf16[8,2,64]{2,1,0:T(2,128)(2,1)}), bf16[8,2,64]{2,1,0:T(2,128)(2,1)S(1)}, u32[]{:S(2)}, u32[]{:S(2)}) async-start(bf16[8,2,64]{2,1,0:T(2,128)(2,1)} %broadcast_in_dim.2), calls=%async_computation | async-start | bytes 8192 | tf_op jit(solution)/shard_map/all_to_all | solution.py:316
  9.2 0.7 %copy-start = (s32[2,256]{1,0:T(2,128)S(1)}, s32[2,256]{1,0:T(2,128)}, u32[]{:S(2)}) copy-start(s32[2,256]{1,0:T(2,128)} %sampled_ref.2) | copy-start | bytes 6148
  9.9 1.0 %copy-start.2 = (bf16[512,512]{1,0:T(8,128)(2,1)S(1)}, bf16[512,512]{1,0:T(8,128)(2,1)}, u32[]{:S(2)}) copy-start(bf16[512,512]{1,0:T(8,128)(2,1)} %constant.20.clone.block_ref) | copy-start | bytes 1572868
  17.2 12.4 %all-to-all-start.1 = ((bf16[8,2,16,512]{3,2,1,0:T(8,128)(2,1)}), bf16[8,2,16,512]{3,2,1,0:T(8,128)(2,1)S(1)}, u32[]{:S(2)}, u32[]{:S(2)}) async-start(bf16[8,2,16,512]{3,2,1,0:T(8,128)(2,1)} %bitcast.2), calls=%async_computation.1 | async-start | bytes 524288 | tf_op jit(solution)/shard_map/all_to_all | solution.py:331
  20.7 0.7 %copy-start.1 = (s32[2,256]{1,0:T(2,128)S(1)}, s32[2,256]{1,0:T(2,128)}, u32[]{:S(2)}) copy-start(s32[2,256]{1,0:T(2,128)} %sampled_ref.2) | copy-start | bytes 6148
  29.6 1.6 %collective-permute-start = (bf16[8,2,16,512]{3,2,1,0:T(8,128)(2,1)S(1)}, bf16[8,2,16,512]{3,2,1,0:T(8,128)(2,1)S(1)}, u32[]{:S(2)}, u32[]{:S(2)}) collective-permute-start(bf16[8,2,16,512]{3,2,1,0:T(8,128)(2,1)S(1)} %all-to-all-done.1.image_ref), channel_id=1, source_target_pairs={{0,1},{1,0},{2,3},{3,2},{4,5},{5,4},{6,7},{7,6},{8,9},{9,8},{10,11... | collective-permute-start | bytes 786440 | tf_op jit(solution)/shard_map/ppermute | solution.py:337
  35.6 4.6 %collective-permute-start.1 = (f32[8,2,16,512]{3,2,1,0:T(8,128)S(1)}, f32[8,2,16,512]{3,2,1,0:T(8,128)S(1)}, u32[]{:S(2)}, u32[]{:S(2)}) collective-permute-start(f32[8,2,16,512]{3,2,1,0:T(8,128)S(1)} %normal_term.3), channel_id=1, source_target_pairs={{0,1},{1,0},{2,3},{3,2},{4,5},{5,4},{6,7},{7,6},{8,9},{9,8},{10,11... | collective-permute-start | bytes 1572872 | tf_op jit(solution)/shard_map/ppermute | solution.py:339
  56.8 10.1 %all-to-all-start.3 = ((f32[16,1,128]{2,1,0:T(1,128)}), f32[16,1,128]{2,1,0:T(1,128)S(1)}, u32[]{:S(2)}, u32[]{:S(2)}) async-start(f32[16,1,128]{2,1,0:T(1,128)} %temporal_rows.1), calls=%async_computation.3 | async-start | bytes 16384 | tf_op jit(solution)/shard_map/all_to_all | solution.py:355

commit v3 on v2

--- a/solution.py
+++ b/solution.py
@@ -47,7 +47,9 @@
     return jnp.where(mine, picked, 0.0).astype(BF16)
 
 
-def image_kernel(total, rows, rank, factors_ref, spatial_ref, image_ref):
+def image_kernel(total, rows, rank, factors_ref, spatial_ref, image_ref, staged_ref, sem):
+    staging = pltpu.make_async_copy(spatial_ref, staged_ref, sem)
+    staging.start()
     mid = spread(factors_ref, total, rows, rank)
     lanes = mid.shape[1]
     width = rows * rank
@@ -56,7 +58,8 @@
     height = wide.shape[0]
     same = iota((height, width), 0) % rows == iota((height, width), 1) // rank
     wide = jnp.where(same, wide, 0.0).astype(BF16)
-    product = dot(wide, spatial_ref[...])
+    staging.wait()
+    product = dot(wide, staged_ref[...])
     half = height // 2
     mid_col = product.shape[1] // 2
     image_ref[:, :mid_col] = (product[:half, :mid_col] - product[half:, mid_col:]).astype(BF16)
@@ -136,41 +139,46 @@
     return (block.astype(F32) * jnp.concatenate([keep, keep], 1)).astype(BF16)
 
 
-def prepare_kernel(sampled_ref, block_ref, spatial_ref, normal_ref, staged_ref, sem):
-    staging = pltpu.make_async_copy(spatial_ref, staged_ref, sem)
-    staging.start()
+def prepare_kernel(sampled_ref, block_ref, normal_ref):
     block = block_ref[...]
     for t in range(sampled_ref.shape[0]):
         normal_ref[t] = dot_t(masked(block, sampled_ref, t), block).astype(BF16)
-    staging.wait()
-
-
-def data_kernel(tile, ahead, sampled_ref, block_ref, kspace_ref, sens_ref, out_ref,
-                block_held, back_held, kspace_held, sens_held, block_sem, kspace_sem, sens_sem):
+
+
+def data_kernel(tile, ahead, sampled_ref, block_ref, kspace_ref, sens_ref, out_ref, block_held, sampled_held,
+                back_held, kspace_held, sens_held, sampled_sem, block_sem, kspace_sem, sens_sem):
     frames, coils, rows, width = kspace_ref.shape
     half = width // 2
     steps = rows // tile
 
-    def fetch(step):
+    def fetch_sens(step):
         slot = lax.rem(step, ahead + 1)
         place = pl.ds(step * tile, tile)
-        return (
-            pltpu.make_async_copy(kspace_ref.at[:, :, place], kspace_held.at[slot], kspace_sem.at[slot]),
-            pltpu.make_async_copy(sens_ref.at[:, place], sens_held.at[slot], sens_sem.at[slot]),
+        return pltpu.make_async_copy(sens_ref.at[:, place], sens_held.at[slot], sens_sem.at[slot])
+
+    def fetch_kspace(step, t):
+        slot = lax.rem(step, ahead + 1)
+        place = pl.ds(step * tile, tile)
+        return pltpu.make_async_copy(
+            kspace_ref.at[t, :, place], kspace_held.at[slot, t], kspace_sem.at[slot, t]
         )
 
     def begin(step):
-        for copy in fetch(step):
-            copy.start()
+        fetch_sens(step).start()
+        for t in range(frames):
+            fetch_kspace(step, t).start()
 
     table = pltpu.make_async_copy(block_ref, block_held, block_sem)
+    mask = pltpu.make_async_copy(sampled_ref, sampled_held, sampled_sem)
     table.start()
+    mask.start()
     for step in range(min(ahead, steps)):
         begin(step)
     table.wait()
+    mask.wait()
     block = block_held[...]
     for t in range(frames):
-        back_held[t] = masked(block, sampled_ref, t).T
+        back_held[t] = masked(block, sampled_held, t).T
 
     @pl.loop(0, steps)
     def _(step):
@@ -178,13 +186,13 @@
         def _():
             begin(step + ahead)
 
-        for copy in fetch(step):
-            copy.wait()
+        fetch_sens(step).wait()
         place = pl.ds(step * tile, tile)
         slot = lax.rem(step, ahead + 1)
         sens = sens_held[slot].astype(F32)
         sens_r, sens_i = sens[..., :half], sens[..., half:]
         for t in range(frames):
+            fetch_kspace(step, t).wait()
             adjoint = dot(kspace_held[slot, t].reshape(coils * tile, width), back_held[t])
             real, imag = conj_sum(adjoint.reshape(coils, tile, width), sens_r, sens_i)
             out_ref[t, place, :half] = real
@@ -249,40 +257,40 @@
     return pltpu.CompilerParams(vmem_limit_bytes=mib * MIB)
 
 
-def prepare(sampled, block, spatial):
+def prepare(sampled, block):
     frames = sampled.shape[0]
     return pl.pallas_call(
         prepare_kernel,
-        in_specs=[VMEM, VMEM, HBM],
-        out_specs=[VMEM, VMEM],
-        out_shape=[pltpu.VMEM((frames, *block.shape), BF16), pltpu.VMEM(spatial.shape, BF16)],
-        scratch_shapes=[pltpu.SemaphoreType.DMA],
+        in_specs=[VMEM, VMEM],
+        out_specs=VMEM,
+        out_shape=pltpu.VMEM((frames, *block.shape), BF16),
         cost_estimate=cost(2 * frames * block.shape[0] ** 3, 4 * block.size),
         compiler_params=grant(12),
         name="prepare",
-    )(sampled, block, remote(spatial))
+    )(sampled, block)
 
 
 def data_term(sampled, block, kspace, sens, tile, ahead):
     frames, coils, rows, width = kspace.shape
     return pl.pallas_call(
         functools.partial(data_kernel, tile, ahead),
-        in_specs=[VMEM, HBM, HBM, HBM],
-        out_specs=VMEM,
-        out_shape=pltpu.VMEM((frames, rows, width), F32),
+        in_specs=[HBM, HBM, HBM, HBM],
+        out_specs=[VMEM, VMEM],
+        out_shape=[pltpu.VMEM((frames, rows, width), F32), pltpu.VMEM(block.shape, BF16)],
         scratch_shapes=[
-            pltpu.VMEM((width, width), BF16),
+            pltpu.VMEM(sampled.shape, jnp.int32),
             pltpu.VMEM((frames, width, width), BF16),
             pltpu.VMEM((ahead + 1, frames, coils, tile, width), BF16),
             pltpu.VMEM((ahead + 1, coils, tile, width), BF16),
             pltpu.SemaphoreType.DMA,
-            pltpu.SemaphoreType.DMA((ahead + 1,)),
+            pltpu.SemaphoreType.DMA,
+            pltpu.SemaphoreType.DMA((ahead + 1, frames)),
             pltpu.SemaphoreType.DMA((ahead + 1,)),
         ],
         cost_estimate=cost(2 * frames * coils * rows * width * width, 2 * kspace.size),
-        compiler_params=grant(24),
+        compiler_params=grant(32),
         name="data_term",
-    )(sampled, remote(block), remote(kspace), remote(sens))
+    )(remote(sampled), remote(block), remote(kspace), remote(sens))
 
 
 def normal_term(part, image, sens, normal, data, tile):
@@ -317,20 +325,20 @@
         jnp.broadcast_to(temporal[None], (frame_size, per, 2 * rank)), "frame", 0, 0, tiled=True
     )
     block = jnp.asarray(dft_block(width // 2))
-    normal, spatial2 = prepare(sampled, block, spatial2)
-
-    image = pl.pallas_call(
+    image, spatial2 = pl.pallas_call(
         functools.partial(image_kernel, total, rows, rank),
-        in_specs=[VMEM, VMEM],
-        out_specs=VMEM,
-        out_shape=pltpu.VMEM((total * rows, width), BF16),
+        in_specs=[VMEM, HBM],
+        out_specs=[VMEM, VMEM],
+        out_shape=[pltpu.VMEM((total * rows, width), BF16), pltpu.VMEM(spatial2.shape, BF16)],
+        scratch_shapes=[pltpu.SemaphoreType.DMA],
         compiler_params=grant(12),
         name="image_rows",
-    )(local(factors), spatial2)
+    )(local(factors), remote(spatial2))
     image, sampled = lax.optimization_barrier((image, sampled))
     image = lax.all_to_all(image.reshape(frame_size, per, rows, width), "frame", 0, 0, tiled=True)
-    data = data_term(sampled, block, kspace, sensitivity, 32, 3)
-    image, data = lax.optimization_barrier((image, data))
+    data, block = data_term(sampled, block, kspace, sensitivity, 64, 2)
+    image, data, block = lax.optimization_barrier((image, data, block))
+    normal = prepare(sampled, block)
     regroup = rows % 16 != 0
     if regroup:
         image = image.transpose(1, 0, 2, 3).reshape(per, half_rows // 16, 16, width).transpose(1, 0, 2, 3)

time: 68.1 us -> 68.1 us (level)
  blocking collectives: 15.2 us -> 28.7 us
  starting transfers between devices: 14.7 us -> 7.39 us
  waiting for transfers between devices: 9.84 us -> 5.43 us
  local copies, waits for them, and re-layouts: 3.65 us -> 0.66 us
  Pallas kernels: 23.3 us -> 24.7 us
    all_to_all x0 -> x1, blocking collectives: none -> 13.6 us  [on_device(): lax.all_to_all(jnp.broadcast_to(temporal[None], (frame_size, per, 2 * ran...]
    all_to_all x1 -> x0, starting transfers between devices: 7.31 us -> none  [on_device(): lax.all_to_all(jnp.broadcast_to(temporal[None], (frame_size, per, 2 * ran...]
    all_to_all x1 -> x0, waiting for transfers between devices: 3.64 us -> none  [on_device(): lax.all_to_all(jnp.broadcast_to(temporal[None], (frame_size, per, 2 * ran...]
    unnamed x6 -> x2, local copies, waits for them, and re-layouts: 2.4 us -> 0.01 us
    ppermute x1, waiting for transfers between devices: 1.51 us -> 0.74 us  [on_device(): image_other = lax.ppermute(image, 'coil', swap)]
    pallas_call x1, Pallas kernels: 1.64 us -> 2.35 us  [on_device(): pl.pallas_call(functools.partial(image_kernel, total, rows, rank), in_spe...]
  transfers between devices with their start and end apart: 5 -> 4, of which waited for: 3 -> 2; matrix products, arithmetic and copies ran while one was open for 0% -> 0% of each run, Pallas kernels for 23% -> 24%
where the time goes in v3:
time: 68.1 us; the launch traced here: 67.7 us
  blocking collectives  28.7 us (42%)
  Pallas kernels  24.7 us (36%)
  starting transfers between devices  7.39 us (11%)
  waiting for transfers between devices  5.43 us (8%)
  between operations  0.74 us (1%)
    all_to_all x1, blocking collectives, on_device(): lax.all_to_all(grad, 'frame', 0, 0, tiled=True).reshape(total * rows, width)  15.1 us
    all_to_all x1, blocking collectives, on_device(): lax.all_to_all(jnp.broadcast_to(temporal[None], (frame_size, per, 2 * ran...  13.6 us
    pallas_call x1, Pallas kernels, data_term(): pl.pallas_call(functools.partial(data_kernel, tile, ahead), in_specs=[HBM...  9.1 us
    pallas_call x2, Pallas kernels, normal_term(): pl.pallas_call(functools.partial(normal_kernel, tile), in_specs=[SMEM, VM...  8.86 us
    all_to_all x1, waiting for transfers between devices, on_device(): partial = lax.all_to_all(partial, ('frame', 'coil'), 0, 0, tiled=True)  4.69 us
    all_to_all x1, starting transfers between devices, on_device(): partial = lax.all_to_all(partial, ('frame', 'coil'), 0, 0, tiled=True)  3.69 us
    all_to_all x1, starting transfers between devices, on_device(): lax.all_to_all(image.reshape(frame_size, per, rows, width), 'frame', 0, 0...  3.42 us
    pallas_call x1, Pallas kernels, on_device(): pl.pallas_call(functools.partial(image_kernel, total, rows, rank), in_spe...  2.35 us
  transfers between devices with their start and end apart: 4, of which 2 were waited for; matrix products, arithmetic and copies ran while one was open for 0% of the time, Pallas kernels for 24%

profile of v3, /device:TPU:0, one launch (start us, length us, event | category | flops | bytes accessed | tf_op | source)
XLA Modules:
  0.0 67.7 jit_solution(15178551947215229633)
XLA Ops:
  0.6 0.7 broadcast_in_dim.2
  1.3 13.6 %all_to_all.20.factors_ref = bf16[8,2,64]{2,1,0:T(2,128)(2,1)S(1)} all-to-all(bf16[8,2,64]{2,1,0:T(2,128)(2,1)S(1)} %broadcast_in_dim.2), channel_id=1, replica_groups=mesh['cuts'=2,'frame'=8,'coil'=2] {'frame'}, dimensions={0} | all-to-all | bytes 4096 | tf_op jit(solution)/shard_map/all_to_all | solution.py:324
  14.9 0.0 copy-start
  14.9 2.3 %image_rows.1 = (bf16[256,512]{1,0:T(8,128)(2,1)}, bf16[512,512]{1,0:T(8,128)(2,1)S(1)}) custom-call(bf16[8,2,64]{2,1,0:T(2,128)(2,1)S(1)} %all_to_all.20.factors_ref, bf16[512,512]{1,0:T(8,128)(2,1)} %bitcast.9), custom_call_target="tpu_custom_call" | custom-call | tf_op jit(solution)/shard_map/image_rows/pallas_call | solution.py:328
  17.2 3.4 %all-to-all-start.1 = ((bf16[8,2,16,512]{3,2,1,0:T(8,128)(2,1)}), bf16[8,2,16,512]{3,2,1,0:T(8,128)(2,1)S(1)}, u32[]{:S(2)}, u32[]{:S(2)}) async-start(bf16[8,2,16,512]{3,2,1,0:T(8,128)(2,1)} %bitcast.2), calls=%async_computation.1 | async-start | bytes 524288 | tf_op jit(solution)/shard_map/all_to_all | solution.py:338
  20.7 9.1 %data_term.1 = (f32[2,256,512]{2,1,0:T(8,128)S(1)}, bf16[512,512]{1,0:T(8,128)(2,1)S(1)}) custom-call(s32[2,256]{1,0:T(2,128)} %sampled_ref.1, bf16[512,512]{1,0:T(8,128)(2,1)} %constant.20.clone.block_ref, bf16[2,16,256,512]{3,2,1,0:T(8,128)(2,1)} %kspace_ref.1, bf16[16,256,512]{2,1,0:T(8,128)(2,1)} %sens_ref.5), custom_call_target="tpu_custom_call" | custom-call | flops 4294967296 | bytes 8388608 | tf_op jit(solution)/shard_map/data_term/pallas_call | solution.py:275
  29.8 0.0 all-to-all-done.1.image_ref
  29.8 0.1 collective-permute-start
  29.9 0.0 copy-done
  29.9 0.8 %prepare.1.normal_ref = bf16[2,512,512]{2,1,0:T(8,128)(2,1)S(1)} custom-call(s32[2,256]{1,0:T(2,128)S(1)} %copy-done, bf16[512,512]{1,0:T(8,128)(2,1)S(1)} %get-tuple-element.17.block_ref), custom_call_target="tpu_custom_call" | custom-call | flops 536870912 | bytes 1048576 | tf_op jit(solution)/shard_map/prepare/pallas_call | solution.py:262
  30.6 0.7 %collective-permute-done.image_ref = bf16[8,2,16,512]{3,2,1,0:T(8,128)(2,1)S(1)} collective-permute-done((bf16[8,2,16,512]{3,2,1,0:T(8,128)(2,1)S(1)}, bf16[8,2,16,512]{3,2,1,0:T(8,128)(2,1)S(1)}, u32[]{:S(2)}, u32[]{:S(2)}) %collective-permute-start) | collective-permute-done | bytes 262176 | tf_op jit(solution)/shard_map/ppermute | solution.py:345
  31.4 4.4 %normal_term.3 = f32[8,2,16,512]{3,2,1,0:T(8,128)S(1)} custom-call(s32[1]{0:T(128)} %bitcast.3.part_ref, bf16[8,2,16,512]{3,2,1,0:T(8,128)(2,1)S(1)} %collective-permute-done.image_ref, bf16[16,256,512]{2,1,0:T(8,128)(2,1)} %sens_ref.5, bf16[2,512,512]{2,1,0:T(8,128)(2,1)S(1)} %prepare.1.normal_ref, f32[2,256,512]{2,1,0:T(8,128)S(1)} %get-tuple-element.18.data_ref), custom_call_target="tpu_custom_call" | custom-call | flops 2147483648 | bytes 2097152 | tf_op jit(solution)/shard_map/normal_term/pallas_call | solution.py:300
  35.8 0.2 collective-permute-start.1
  36.0 4.4 %normal_term.2 = f32[8,2,16,512]{3,2,1,0:T(8,128)S(1)} custom-call(s32[1]{0:T(128)} %bitcast.part_ref, bf16[8,2,16,512]{3,2,1,0:T(8,128)(2,1)S(1)} %all-to-all-done.1.image_ref, bf16[16,256,512]{2,1,0:T(8,128)(2,1)} %sens_ref.5, bf16[2,512,512]{2,1,0:T(8,128)(2,1)S(1)} %prepare.1.normal_ref, f32[2,256,512]{2,1,0:T(8,128)S(1)} %get-tuple-element.18.data_ref), custom_call_target="tpu_custom_call" | custom-call | flops 2147483648 | bytes 2097152 | tf_op jit(solution)/shard_map/normal_term/pallas_call | solution.py:300
  40.5 0.0 collective-permute-done.1
  40.5 0.1 add_convert_fusion
  40.6 15.1 %all_to_all.21 = bf16[8,2,16,512]{3,2,1,0:T(8,128)(2,1)S(1)} all-to-all(bf16[8,2,16,512]{3,2,1,0:T(8,128)(2,1)S(1)} %add_convert_fusion), channel_id=1, replica_groups=mesh['cuts'=2,'frame'=8,'coil'=2] {'frame'}, dimensions={0} | all-to-all | bytes 524288 | tf_op jit(solution)/shard_map/all_to_all | solution.py:352
  55.7 1.2 %temporal_rows.1 = f32[16,1,128]{2,1,0:T(1,128)} custom-call(bf16[512,512]{1,0:T(8,128)(2,1)S(1)} %get-tuple-element.19.spatial_ref, bf16[256,512]{1,0:T(8,128)(2,1)S(1)} %bitcast.6), custom_call_target="tpu_custom_call" | custom-call | tf_op jit(solution)/shard_map/temporal_rows/pallas_call | solution.py:355
  56.9 3.7 %all-to-all-start.3 = ((f32[16,1,128]{2,1,0:T(1,128)}), f32[16,1,128]{2,1,0:T(1,128)S(1)}, u32[]{:S(2)}, u32[]{:S(2)}) async-start(f32[16,1,128]{2,1,0:T(1,128)} %temporal_rows.1), calls=%async_computation.3 | async-start | bytes 16384 | tf_op jit(solution)/shard_map/all_to_all | solution.py:363
  60.6 1.7 %spatial_rows.1 = f32[512,512]{1,0:T(8,128)} custom-call(bf16[8,2,64]{2,1,0:T(2,128)(2,1)S(1)} %all_to_all.20.factors_ref, bf16[256,512]{1,0:T(8,128)(2,1)S(1)} %bitcast.7), custom_call_target="tpu_custom_call" | custom-call | tf_op jit(solution)/shard_map/spatial_rows/pallas_call | solution.py:364
  62.4 4.7 %all-to-all-done.3.parts_ref = f32[16,1,128]{2,1,0:T(1,128)S(1)} async-done(((f32[16,1,128]{2,1,0:T(1,128)}), f32[16,1,128]{2,1,0:T(1,128)S(1)}, u32[]{:S(2)}, u32[]{:S(2)}) %all-to-all-start.3) | async-done | bytes 8224 | tf_op jit(solution)/shard_map/all_to_all | solution.py:363
  67.1 0.6 temporal_sum.1
Async XLA Ops:
  14.9 15.0 %copy-start = (s32[2,256]{1,0:T(2,128)S(1)}, s32[2,256]{1,0:T(2,128)}, u32[]{:S(2)}) copy-start(s32[2,256]{1,0:T(2,128)} %sampled_ref.1) | copy-start | bytes 6148
  17.2 12.5 %all-to-all-start.1 = ((bf16[8,2,16,512]{3,2,1,0:T(8,128)(2,1)}), bf16[8,2,16,512]{3,2,1,0:T(8,128)(2,1)S(1)}, u32[]{:S(2)}, u32[]{:S(2)}) async-start(bf16[8,2,16,512]{3,2,1,0:T(8,128)(2,1)} %bitcast.2), calls=%async_computation.1 | async-start | bytes 524288 | tf_op jit(solution)/shard_map/all_to_all | solution.py:338
  29.8 1.6 %collective-permute-start = (bf16[8,2,16,512]{3,2,1,0:T(8,128)(2,1)S(1)}, bf16[8,2,16,512]{3,2,1,0:T(8,128)(2,1)S(1)}, u32[]{:S(2)}, u32[]{:S(2)}) collective-permute-start(bf16[8,2,16,512]{3,2,1,0:T(8,128)(2,1)S(1)} %all-to-all-done.1.image_ref), channel_id=1, source_target_pairs={{0,1},{1,0},{2,3},{3,2},{4,5},{5,4},{6,7},{7,6},{8,9},{9,8},{10,11... | collective-permute-start | bytes 786440 | tf_op jit(solution)/shard_map/ppermute | solution.py:345
  35.8 4.7 %collective-permute-start.1 = (f32[8,2,16,512]{3,2,1,0:T(8,128)S(1)}, f32[8,2,16,512]{3,2,1,0:T(8,128)S(1)}, u32[]{:S(2)}, u32[]{:S(2)}) collective-permute-start(f32[8,2,16,512]{3,2,1,0:T(8,128)S(1)} %normal_term.3), channel_id=1, source_target_pairs={{0,1},{1,0},{2,3},{3,2},{4,5},{5,4},{6,7},{7,6},{8,9},{9,8},{10,11... | collective-permute-start | bytes 1572872 | tf_op jit(solution)/shard_map/ppermute | solution.py:347
  56.9 10.1 %all-to-all-start.3 = ((f32[16,1,128]{2,1,0:T(1,128)}), f32[16,1,128]{2,1,0:T(1,128)S(1)}, u32[]{:S(2)}, u32[]{:S(2)}) async-start(f32[16,1,128]{2,1,0:T(1,128)} %temporal_rows.1), calls=%async_computation.3 | async-start | bytes 16384 | tf_op jit(solution)/shard_map/all_to_all | solution.py:363

commit v4 on v2

--- a/solution.py
+++ b/solution.py
@@ -13,13 +13,12 @@
 BF16 = jnp.bfloat16
 
 
-def dft_block(length):
+def dft_half(length):
     index = np.arange(length)
     angles = (index[:, None] * index[None, :] % length) * (2.0 * math.pi / length)
     cosine = np.cos(angles) / math.sqrt(length)
     sine_part = -np.sin(angles) / math.sqrt(length)
-    block = np.block([[cosine, sine_part], [-sine_part, cosine]])
-    return block.astype(np.float32).astype(BF16)
+    return np.concatenate([cosine, sine_part], 1).astype(np.float32).astype(BF16)
 
 
 def dot(a, b):
@@ -131,88 +130,127 @@
     )
 
 
-def masked(block, sampled_ref, t):
-    keep = sampled_ref[t : t + 1, :].astype(F32)
-    return (block.astype(F32) * jnp.concatenate([keep, keep], 1)).astype(BF16)
-
-
-def prepare_kernel(sampled_ref, block_ref, spatial_ref, normal_ref, staged_ref, sem):
-    staging = pltpu.make_async_copy(spatial_ref, staged_ref, sem)
+def stage_kernel(sampled_ref, block_ref, spatial_ref, mask_out, block_out, spatial_out, sems):
+    copies = [
+        pltpu.make_async_copy(sampled_ref, mask_out, sems.at[0]),
+        pltpu.make_async_copy(block_ref, block_out, sems.at[1]),
+        pltpu.make_async_copy(spatial_ref, spatial_out, sems.at[2]),
+    ]
+    for copy in copies:
+        copy.start()
+    for copy in copies:
+        copy.wait()
+
+
+def data_kernel(tile, ahead, starts_ref, mask_ref, block_ref, kspace_ref, sens_ref,
+                first_ref, normal_ref, other_ref, own_ref,
+                back, kspace_held, sens_held, own_held, kspace_sem, sens_sem, first_sem, own_sem):
+    frames, coils, rows, width = kspace_ref.shape
+    groups, _, per, _ = own_ref.shape
+    half = width // 2
+    steps = rows // tile
+    part_steps = steps // 2
+    step_groups = tile // per
+
+    def fetch(step):
+        slot = lax.rem(step, ahead + 1)
+        start = starts_ref[1 - step // part_steps] + lax.rem(step, part_steps) * tile
+        place = pl.ds(pl.multiple_of(start, tile), tile)
+        copies = [pltpu.make_async_copy(sens_ref.at[:, place], sens_held.at[slot], sens_sem.at[slot])]
+        for t in range(frames):
+            source = kspace_ref.at[t, :, place]
+            copies.append(
+                pltpu.make_async_copy(source, kspace_held.at[slot, t], kspace_sem.at[slot, t])
+            )
+        return copies
+
+    for step in range(min(ahead, steps)):
+        for copy in fetch(step):
+            copy.start()
+    start = pl.ds(pl.multiple_of(starts_ref[0], tile), tile)
+    staging = pltpu.make_async_copy(sens_ref.at[:, start], first_ref, first_sem)
     staging.start()
     block = block_ref[...]
-    for t in range(sampled_ref.shape[0]):
-        normal_ref[t] = dot_t(masked(block, sampled_ref, t), block).astype(BF16)
+    for t in range(frames):
+        keep = mask_ref[t : t + 1, :].astype(F32)
+        cosine = (block[:, :half].astype(F32) * keep).astype(BF16).T
+        sine_part = (block[:, half:].astype(F32) * keep).astype(BF16).T
+        back[t, :half, :half] = cosine
+        back[t, :half, half:] = -sine_part
+        back[t, half:, :half] = sine_part
+        back[t, half:, half:] = cosine
+        normal_ref[t] = dot(block, back[t]).astype(BF16)
+
+    def part(first_step, store):
+        @pl.loop(0, part_steps)
+        def _(k):
+            step = first_step + k
+
+            @pl.when(step + ahead < steps)
+            def _():
+                for copy in fetch(step + ahead):
+                    copy.start()
+
+            copies = fetch(step)
+            copies[0].wait()
+            slot = lax.rem(step, ahead + 1)
+            sens = sens_held[slot].astype(F32)
+            sens_r, sens_i = sens[..., :half], sens[..., half:]
+            for t in range(frames):
+                copies[1 + t].wait()
+                adjoint = dot(kspace_held[slot, t].reshape(coils * tile, width), back[t])
+                store(k, t, *conj_sum(adjoint.reshape(coils, tile, width), sens_r, sens_i))
+
+    def store_own(k, t, real, imag):
+        group = pl.ds(k * step_groups, step_groups)
+        own_held[group, t, :, :half] = real.reshape(step_groups, per, half)
+        own_held[group, t, :, half:] = imag.reshape(step_groups, per, half)
+
+    def store_other(k, t, real, imag):
+        place = pl.ds(k * tile, tile)
+        other_ref[t, place, :half] = real
+        other_ref[t, place, half:] = imag
+
+    part(0, store_own)
+    leaving = pltpu.make_async_copy(own_held, own_ref, own_sem)
+    leaving.start()
+    part(part_steps, store_other)
     staging.wait()
-
-
-def data_kernel(tile, ahead, sampled_ref, block_ref, kspace_ref, sens_ref, out_ref,
-                block_held, back_held, kspace_held, sens_held, block_sem, kspace_sem, sens_sem):
-    frames, coils, rows, width = kspace_ref.shape
-    half = width // 2
-    steps = rows // tile
-
-    def fetch(step):
-        slot = lax.rem(step, ahead + 1)
-        place = pl.ds(step * tile, tile)
-        return (
-            pltpu.make_async_copy(kspace_ref.at[:, :, place], kspace_held.at[slot], kspace_sem.at[slot]),
-            pltpu.make_async_copy(sens_ref.at[:, place], sens_held.at[slot], sens_sem.at[slot]),
-        )
-
-    def begin(step):
-        for copy in fetch(step):
-            copy.start()
-
-    table = pltpu.make_async_copy(block_ref, block_held, block_sem)
-    table.start()
-    for step in range(min(ahead, steps)):
-        begin(step)
-    table.wait()
-    block = block_held[...]
-    for t in range(frames):
-        back_held[t] = masked(block, sampled_ref, t).T
-
-    @pl.loop(0, steps)
-    def _(step):
-        @pl.when(step + ahead < steps)
-        def _():
-            begin(step + ahead)
-
-        for copy in fetch(step):
-            copy.wait()
-        place = pl.ds(step * tile, tile)
-        slot = lax.rem(step, ahead + 1)
-        sens = sens_held[slot].astype(F32)
-        sens_r, sens_i = sens[..., :half], sens[..., half:]
-        for t in range(frames):
-            adjoint = dot(kspace_held[slot, t].reshape(coils * tile, width), back_held[t])
-            real, imag = conj_sum(adjoint.reshape(coils, tile, width), sens_r, sens_i)
-            out_ref[t, place, :half] = real
-            out_ref[t, place, half:] = imag
-
-
-def normal_kernel(tile, part_ref, image_ref, sens_ref, normal_ref, data_ref, out_ref, sens_held, sem):
+    leaving.wait()
+
+
+def normal_kernel(other, starts_ref, image_ref, first_ref, sens_ref, normal_ref, *rest):
+    if other:
+        data_ref, out_ref, next_ref, table, sens_held, sem, next_sem = rest
+    else:
+        out_ref, table, sens_held, sem = rest
     groups, frames, per, width = image_ref.shape
-    coils = sens_ref.shape[0]
+    coils, tile, _ = first_ref.shape
     half = width // 2
     step_groups = tile // per
     steps = groups // step_groups
 
-    def spot(step):
-        return pl.ds(pl.multiple_of(part_ref[0] * (groups * per) + step * tile, tile), tile)
+    def spot(step, which):
+        return pl.ds(pl.multiple_of(starts_ref[which] + step * tile, tile), tile)
 
     def fetch(step):
-        return pltpu.make_async_copy(sens_ref.at[:, spot(step)], sens_held.at[step], sem.at[step])
-
-    for step in range(steps):
+        source = sens_ref.at[:, spot(step, 0 if other else 1)]
+        return pltpu.make_async_copy(source, sens_held.at[step - 1], sem.at[step - 1])
+
+    for step in range(1, steps):
         fetch(step).start()
-
-    @pl.loop(0, steps)
-    def _(step):
-        place = spot(step)
+    if other:
+        staging = pltpu.make_async_copy(sens_ref.at[:, spot(0, 1)], next_ref, next_sem)
+        staging.start()
+    for t in range(frames):
+        table[t, :half] = normal_ref[t]
+        table[t, half:, :half] = -normal_ref[t, :, half:]
+        table[t, half:, half:] = normal_ref[t, :, :half]
+
+    def work(step, sens):
+        place = pl.ds(step * tile, tile)
         group = pl.ds(step * step_groups, step_groups)
-        fetch(step).wait()
-        sens = sens_held[step].astype(F32)
+        sens = sens.astype(F32)
         sens_r, sens_i = sens[..., :half], sens[..., half:]
         for t in range(frames):
             image = image_ref[group, t].reshape(tile, width).astype(F32)
@@ -220,11 +258,23 @@
             coil_r = (sens_r * image_r - sens_i * image_i).astype(BF16)
             coil_i = (sens_r * image_i + sens_i * image_r).astype(BF16)
             coil = jnp.concatenate([coil_r, coil_i], -1).reshape(coils * tile, width)
-            adjoint = dot(coil, normal_ref[t])
+            adjoint = dot(coil, table[t])
             real, imag = conj_sum(adjoint.reshape(coils, tile, width), sens_r, sens_i)
-            shape = (step_groups, per, half)
-            out_ref[group, t, :, :half] = (real - data_ref[t, place, :half]).reshape(shape)
-            out_ref[group, t, :, half:] = (imag - data_ref[t, place, half:]).reshape(shape)
+            if other:
+                real = real - data_ref[t, place, :half]
+                imag = imag - data_ref[t, place, half:]
+            out_ref[group, t, :, :half] = real.reshape(step_groups, per, half)
+            out_ref[group, t, :, half:] = imag.reshape(step_groups, per, half)
+
+    work(0, first_ref[...])
+
+    @pl.loop(1, steps)
+    def _(step):
+        fetch(step).wait()
+        work(step, sens_held[step - 1])
+
+    if other:
+        staging.wait()
 
 
 def cost(flops, moved):
@@ -249,58 +299,78 @@
     return pltpu.CompilerParams(vmem_limit_bytes=mib * MIB)
 
 
-def prepare(sampled, block, spatial):
-    frames = sampled.shape[0]
+def stage(sampled, block, spatial):
     return pl.pallas_call(
-        prepare_kernel,
-        in_specs=[VMEM, VMEM, HBM],
-        out_specs=[VMEM, VMEM],
-        out_shape=[pltpu.VMEM((frames, *block.shape), BF16), pltpu.VMEM(spatial.shape, BF16)],
-        scratch_shapes=[pltpu.SemaphoreType.DMA],
-        cost_estimate=cost(2 * frames * block.shape[0] ** 3, 4 * block.size),
+        stage_kernel,
+        in_specs=[HBM, HBM, HBM],
+        out_specs=[VMEM, VMEM, VMEM],
+        out_shape=[
+            pltpu.VMEM(sampled.shape, jnp.int32),
+            pltpu.VMEM(block.shape, BF16),
+            pltpu.VMEM(spatial.shape, BF16),
+        ],
+        scratch_shapes=[pltpu.SemaphoreType.DMA((3,))],
+        cost_estimate=cost(0, 8 * block.size),
         compiler_params=grant(12),
-        name="prepare",
-    )(sampled, block, remote(spatial))
-
-
-def data_term(sampled, block, kspace, sens, tile, ahead):
+        name="stage",
+    )(remote(sampled), remote(block), remote(spatial))
+
+
+def data_term(starts, mask, block, kspace, sens, per, tile, ahead):
     frames, coils, rows, width = kspace.shape
+    own = (rows // 2 // per, frames, per, width)
     return pl.pallas_call(
         functools.partial(data_kernel, tile, ahead),
-        in_specs=[VMEM, HBM, HBM, HBM],
-        out_specs=VMEM,
-        out_shape=pltpu.VMEM((frames, rows, width), F32),
+        in_specs=[SMEM, VMEM, VMEM, HBM, HBM],
+        out_specs=[VMEM, VMEM, VMEM, HBM],
+        out_shape=[
+            pltpu.VMEM((coils, tile, width), BF16),
+            pltpu.VMEM((frames, width // 2, width), BF16),
+            pltpu.VMEM((frames, rows // 2, width), F32),
+            pltpu.HBM(own, F32),
+        ],
         scratch_shapes=[
-            pltpu.VMEM((width, width), BF16),
             pltpu.VMEM((frames, width, width), BF16),
             pltpu.VMEM((ahead + 1, frames, coils, tile, width), BF16),
             pltpu.VMEM((ahead + 1, coils, tile, width), BF16),
+            pltpu.VMEM(own, F32),
+            pltpu.SemaphoreType.DMA((ahead + 1, frames)),
+            pltpu.SemaphoreType.DMA((ahead + 1,)),
             pltpu.SemaphoreType.DMA,
-            pltpu.SemaphoreType.DMA((ahead + 1,)),
-            pltpu.SemaphoreType.DMA((ahead + 1,)),
+            pltpu.SemaphoreType.DMA,
         ],
         cost_estimate=cost(2 * frames * coils * rows * width * width, 2 * kspace.size),
-        compiler_params=grant(24),
+        compiler_params=grant(32),
         name="data_term",
-    )(sampled, remote(block), remote(kspace), remote(sens))
-
-
-def normal_term(part, image, sens, normal, data, tile):
+    )(starts, mask, block, remote(kspace), remote(sens))
+
+
+def normal_term(starts, image, first, sens, normal, data=None):
     groups, frames, per, width = image.shape
-    coils = sens.shape[0]
+    coils, tile, _ = first.shape
     steps = groups * per // tile
+    other = data is not None
+    outs = [pltpu.VMEM((groups, frames, per, width), F32)]
+    scratch = [
+        pltpu.VMEM((frames, width, width), BF16),
+        pltpu.VMEM((steps - 1, coils, tile, width), BF16),
+        pltpu.SemaphoreType.DMA((steps - 1,)),
+    ]
+    if other:
+        outs.append(pltpu.VMEM(first.shape, BF16))
+        scratch.append(pltpu.SemaphoreType.DMA)
     return pl.pallas_call(
-        functools.partial(normal_kernel, tile),
-        in_specs=[SMEM, VMEM, HBM, VMEM, VMEM],
-        out_specs=VMEM,
-        out_shape=pltpu.VMEM((groups, frames, per, width), F32),
-        scratch_shapes=[pltpu.VMEM((steps, coils, tile, width), BF16), pltpu.SemaphoreType.DMA((steps,))],
+        functools.partial(normal_kernel, other),
+        in_specs=[SMEM, VMEM, VMEM, HBM, VMEM] + [VMEM] * other,
+        out_specs=[VMEM] * len(outs),
+        out_shape=outs,
+        scratch_shapes=scratch,
         cost_estimate=cost(
             2 * frames * coils * groups * per * width * width, coils * groups * per * width * 2
         ),
         compiler_params=grant(20),
-        name="normal_term",
-    )(part, image, remote(sens), normal, data)
+        name="normal_other" if other else "normal_own",
+    )(starts, image, first, remote(sens), normal, *([data] if other else []))
 
 
 def on_device(frame_size, coil_size, spatial, temporal, kspace, sampled, sensitivity):
@@ -309,16 +379,14 @@
     total = per * frame_size
     half_rows = rows * frame_size
     swap = [(i, (i + 1) % coil_size) for i in range(coil_size)]
-    own = lax.axis_index("coil")
-    other = (own + 1) % coil_size
+    own = lax.axis_index("coil") * half_rows
+    starts = jnp.stack([(own + half_rows) % (coil_size * half_rows), own])
     spatial2 = spatial.reshape(rows * rank, width)
 
     factors = lax.all_to_all(
         jnp.broadcast_to(temporal[None], (frame_size, per, 2 * rank)), "frame", 0, 0, tiled=True
     )
-    block = jnp.asarray(dft_block(width // 2))
-    normal, spatial2 = prepare(sampled, block, spatial2)
-
+    mask, block, near = stage(sampled, jnp.asarray(dft_half(width // 2)), spatial2)
     image = pl.pallas_call(
         functools.partial(image_kernel, total, rows, rank),
         in_specs=[VMEM, VMEM],
@@ -326,19 +394,21 @@
         out_shape=pltpu.VMEM((total * rows, width), BF16),
         compiler_params=grant(12),
         name="image_rows",
-    )(local(factors), spatial2)
-    image, sampled = lax.optimization_barrier((image, sampled))
+    )(local(factors), near)
+    image, kspace = lax.optimization_barrier((image, kspace))
     image = lax.all_to_all(image.reshape(frame_size, per, rows, width), "frame", 0, 0, tiled=True)
-    data = data_term(sampled, block, kspace, sensitivity, 32, 3)
-    image, data = lax.optimization_barrier((image, data))
     regroup = rows % 16 != 0
+    first, normal, data_other, data_own = data_term(
+        starts, mask, block, kspace, sensitivity, 16 if regroup else rows, 32, 3
+    )
+    image, normal = lax.optimization_barrier((image, normal))
     if regroup:
         image = image.transpose(1, 0, 2, 3).reshape(per, half_rows // 16, 16, width).transpose(1, 0, 2, 3)
     image_other = lax.ppermute(image, "coil", swap)
-    send = normal_term(other.reshape(1), local(image_other), sensitivity, normal, data, 32)
+    send, first = normal_term(starts, local(image_other), first, sensitivity, normal, data_other)
     received = lax.ppermute(send, "coil", swap)
-    keep_own = normal_term(own.reshape(1), local(image), sensitivity, normal, data, 32)
-    grad = (keep_own + received).astype(BF16)
+    (keep_own,) = normal_term(starts, local(image), first, sensitivity, normal)
+    grad = (keep_own + received - data_own).astype(BF16)
     if regroup:
         grad = grad.transpose(1, 0, 2, 3).reshape(per, frame_size, rows, width).transpose(1, 0, 2, 3)
     grad = lax.all_to_all(grad, "frame", 0, 0, tiled=True).reshape(total * rows, width)
@@ -351,7 +421,7 @@
         out_shape=pltpu.VMEM((frame_size * coil_size, 1, per * 2 * rank), F32),
         compiler_params=grant(12),
         name="temporal_rows",
-    )(spatial2, grad)
+    )(local(spatial2), grad)
     partial = lax.all_to_all(partial, ("frame", "coil"), 0, 0, tiled=True)
     spatial_grad = pl.pallas_call(
         functools.partial(spatial_kernel, total, rows, rank),

time: 68.1 us -> 68.5 us (level)
  local copies, waits for them, and re-layouts: 3.65 us -> 1.26 us
  waiting for transfers between devices: 9.84 us -> 11.5 us
  Pallas kernels: 23.3 us -> 24.6 us
    unnamed x6 -> x4, local copies, waits for them, and re-layouts: 2.4 us -> 0.01 us
    all_to_all x1, waiting for transfers between devices: 3.64 us -> 5.25 us  [on_device(): lax.all_to_all(jnp.broadcast_to(temporal[None], (frame_size, per, 2 * ran...]
    pallas_call x4, Pallas kernels: 18.1 us -> 19.3 us  [the longest x1 10.1 us: data_term(): pl.pallas_call(functools.partial(data_kernel, tile, ahead), in_specs=[SME...]
  transfers between devices with their start and end apart: 5 -> 5, of which waited for: 3 -> 3; matrix products, arithmetic and copies ran while one was open for 0% -> 0% of each run, Pallas kernels for 23% -> 25%
where the time goes in v4:
time: 68.5 us; the launch traced here: 68.1 us
  Pallas kernels  24.6 us (36%)
  blocking collectives  15.2 us (22%)
  starting transfers between devices  14.7 us (21%)
  waiting for transfers between devices  11.5 us (17%)
  local copies, waits for them, and re-layouts  1.26 us (2%)
  between operations  0.73 us (1%)
    all_to_all x1, blocking collectives, on_device(): lax.all_to_all(grad, 'frame', 0, 0, tiled=True).reshape(total * rows, width)  15.2 us
    pallas_call x1, Pallas kernels, data_term(): pl.pallas_call(functools.partial(data_kernel, tile, ahead), in_specs=[SME...  10.1 us
    pallas_call x2, Pallas kernels, normal_term(): pl.pallas_call(functools.partial(normal_kernel, other), in_specs=[SMEM, V...  8 us
    all_to_all x1, starting transfers between devices, on_device(): lax.all_to_all(jnp.broadcast_to(temporal[None], (frame_size, per, 2 * ran...  7.31 us
    all_to_all x1, waiting for transfers between devices, on_device(): lax.all_to_all(jnp.broadcast_to(temporal[None], (frame_size, per, 2 * ran...  5.25 us
    all_to_all x1, waiting for transfers between devices, on_device(): partial = lax.all_to_all(partial, ('frame', 'coil'), 0, 0, tiled=True)  4.68 us
    all_to_all x1, starting transfers between devices, on_device(): partial = lax.all_to_all(partial, ('frame', 'coil'), 0, 0, tiled=True)  3.69 us
    all_to_all x1, starting transfers between devices, on_device(): lax.all_to_all(image.reshape(frame_size, per, rows, width), 'frame', 0, 0...  3.41 us
  transfers between devices with their start and end apart: 5, of which 3 were waited for; matrix products, arithmetic and copies ran while one was open for 0% of the time, Pallas kernels for 25%

profile of v4, /device:TPU:0, one launch (start us, length us, event | category | flops | bytes accessed | tf_op | source)
XLA Modules:
  0.0 68.1 jit_solution(3173626134001751926)
XLA Ops:
  0.6 1.2 %broadcast_in_dim.2 = bf16[8,2,64]{2,1,0:T(2,128)(2,1)} broadcast(bf16[2,64]{1,0:T(2,128)(2,1)} %param.7), dimensions={1,2} | broadcast | bytes 2304 | tf_op jit(solution)/shard_map/broadcast_in_dim | solution.py:387
  1.9 7.3 %all-to-all-start = ((bf16[8,2,64]{2,1,0:T(2,128)(2,1)}), bf16[8,2,64]{2,1,0:T(2,128)(2,1)S(1)}, u32[]{:S(2)}, u32[]{:S(2)}) async-start(bf16[8,2,64]{2,1,0:T(2,128)(2,1)} %broadcast_in_dim.2), calls=%async_computation | async-start | bytes 8192 | tf_op jit(solution)/shard_map/all_to_all | solution.py:386
  9.2 1.2 %stage.1 = (s32[2,256]{1,0:T(2,128)S(1)}, bf16[256,512]{1,0:T(8,128)(2,1)S(1)}, bf16[512,512]{1,0:T(8,128)(2,1)S(1)}) custom-call(s32[2,256]{1,0:T(2,128)} %sampled_ref.1, bf16[256,512]{1,0:T(8,128)(2,1)} %constant.21.clone.block_ref, bf16[512,512]{1,0:T(8,128)(2,1)} %bitcast.8), custom_call_target="tpu_custom_call" | custom-call | bytes 1048576 | tf_op jit(solution)/shard_map/stage/pallas_call | solution.py:303
  10.4 5.2 %all-to-all-done.factors_ref = bf16[8,2,64]{2,1,0:T(2,128)(2,1)S(1)} async-done(((bf16[8,2,64]{2,1,0:T(2,128)(2,1)}), bf16[8,2,64]{2,1,0:T(2,128)(2,1)S(1)}, u32[]{:S(2)}, u32[]{:S(2)}) %all-to-all-start) | async-done | bytes 2080 | tf_op jit(solution)/shard_map/all_to_all | solution.py:386
  15.6 1.6 %image_rows.1 = bf16[256,512]{1,0:T(8,128)(2,1)} custom-call(bf16[8,2,64]{2,1,0:T(2,128)(2,1)S(1)} %all-to-all-done.factors_ref, bf16[512,512]{1,0:T(8,128)(2,1)S(1)} %get-tuple-element.15.spatial_ref), custom_call_target="tpu_custom_call" | custom-call | tf_op jit(solution)/shard_map/image_rows/pallas_call | solution.py:390
  17.2 3.4 %all-to-all-start.1 = ((bf16[8,2,16,512]{3,2,1,0:T(8,128)(2,1)}), bf16[8,2,16,512]{3,2,1,0:T(8,128)(2,1)S(1)}, u32[]{:S(2)}, u32[]{:S(2)}) async-start(bf16[8,2,16,512]{3,2,1,0:T(8,128)(2,1)} %bitcast.3), calls=%async_computation.1 | async-start | bytes 524288 | tf_op jit(solution)/shard_map/all_to_all | solution.py:399
  20.7 0.1 pad_add_fusion.starts_ref
  20.7 10.1 %data_term.1 = (bf16[16,32,512]{2,1,0:T(8,128)(2,1)S(1)}, bf16[2,256,512]{2,1,0:T(8,128)(2,1)S(1)}, f32[2,128,512]{2,1,0:T(8,128)S(1)}, f32[8,2,16,512]{3,2,1,0:T(8,128)}) custom-call(s32[2]{0:T(128)S(1)} %pad_add_fusion.starts_ref, s32[2,256]{1,0:T(2,128)S(1)} %get-tuple-element.17.mask_ref, bf16[256,512]{1,0:T(8,128)(2,1)S(1)} %get-tuple-element.18.block_ref, ...), custom_call_target="tpu_custom_call" | custom-call | flops 4294967296 | bytes 8388608 | tf_op jit(solution)/shard_map/data_term/pallas_call | solution.py:322
  30.9 0.0 copy-start.1
  30.9 0.0 all-to-all-done.1.image_ref
  30.9 0.1 collective-permute-start
  31.0 1.5 %collective-permute-done.image_ref = bf16[8,2,16,512]{3,2,1,0:T(8,128)(2,1)S(1)} collective-permute-done((bf16[8,2,16,512]{3,2,1,0:T(8,128)(2,1)S(1)}, bf16[8,2,16,512]{3,2,1,0:T(8,128)(2,1)S(1)}, u32[]{:S(2)}, u32[]{:S(2)}) %collective-permute-start) | collective-permute-done | bytes 262176 | tf_op jit(solution)/shard_map/ppermute | solution.py:407
  32.5 0.0 copy-start
  32.5 4.0 %normal_other.1 = (f32[8,2,16,512]{3,2,1,0:T(8,128)S(1)}, bf16[16,32,512]{2,1,0:T(8,128)(2,1)S(1)}) custom-call(s32[2]{0:T(128)S(1)} %pad_add_fusion.starts_ref, bf16[8,2,16,512]{3,2,1,0:T(8,128)(2,1)S(1)} %collective-permute-done.image_ref, bf16[16,32,512]{2,1,0:T(8,128)(2,1)S(1)} %get-tuple-element.22.first_ref, bf16[16,256,512]{2,1,0:T(8,128)(2,1)} %sens_ref.5, ...), custom_call_target="tpu_custom_call" | custom-call | flops 2147483648 | bytes 2097152 | tf_op jit(solution)/shard_map/normal_other/pallas_call | solution.py:362
  36.6 0.2 collective-permute-start.1
  36.8 4.0 %normal_own.1 = f32[8,2,16,512]{3,2,1,0:T(8,128)S(1)} custom-call(s32[2]{0:T(128)S(1)} %pad_add_fusion.starts_ref, bf16[8,2,16,512]{3,2,1,0:T(8,128)(2,1)S(1)} %all-to-all-done.1.image_ref, bf16[16,32,512]{2,1,0:T(8,128)(2,1)S(1)} %get-tuple-element.25.first_ref, bf16[16,256,512]{2,1,0:T(8,128)(2,1)} %sens_ref.5, ...), custom_call_target="tpu_custom_call" | custom-call | flops 2147483648 | bytes 2097152 | tf_op jit(solution)/shard_map/normal_own/pallas_call | solution.py:362
  40.7 0.0 collective-permute-done.1
  40.7 0.0 copy-done.1
  40.8 0.2 subtract_convert_fusion
  41.0 15.2 %all_to_all.20 = bf16[8,2,16,512]{3,2,1,0:T(8,128)(2,1)S(1)} all-to-all(bf16[8,2,16,512]{3,2,1,0:T(8,128)(2,1)S(1)} %subtract_convert_fusion), channel_id=1, replica_groups=mesh['cuts'=2,'frame'=8,'coil'=2] {'frame'}, dimensions={0} | all-to-all | bytes 524288 | tf_op jit(solution)/shard_map/all_to_all | solution.py:414
  56.1 0.0 copy-done
  56.1 1.2 %temporal_rows.1 = f32[16,1,128]{2,1,0:T(1,128)} custom-call(bf16[512,512]{1,0:T(8,128)(2,1)S(1)} %bitcast.9, bf16[256,512]{1,0:T(8,128)(2,1)S(1)} %bitcast.6), custom_call_target="tpu_custom_call" | custom-call | tf_op jit(solution)/shard_map/temporal_rows/pallas_call | solution.py:417
  57.3 3.7 %all-to-all-start.3 = ((f32[16,1,128]{2,1,0:T(1,128)}), f32[16,1,128]{2,1,0:T(1,128)S(1)}, u32[]{:S(2)}, u32[]{:S(2)}) async-start(f32[16,1,128]{2,1,0:T(1,128)} %temporal_rows.1), calls=%async_computation.3 | async-start | bytes 16384 | tf_op jit(solution)/shard_map/all_to_all | solution.py:425
  61.0 1.7 %spatial_rows.1 = f32[512,512]{1,0:T(8,128)} custom-call(bf16[8,2,64]{2,1,0:T(2,128)(2,1)S(1)} %all-to-all-done.factors_ref, bf16[256,512]{1,0:T(8,128)(2,1)S(1)} %bitcast.7), custom_call_target="tpu_custom_call" | custom-call | tf_op jit(solution)/shard_map/spatial_rows/pallas_call | solution.py:426
  62.8 4.7 %all-to-all-done.3.parts_ref = f32[16,1,128]{2,1,0:T(1,128)S(1)} async-done(((f32[16,1,128]{2,1,0:T(1,128)}), f32[16,1,128]{2,1,0:T(1,128)S(1)}, u32[]{:S(2)}, u32[]{:S(2)}) %all-to-all-start.3) | async-done | bytes 8224 | tf_op jit(solution)/shard_map/all_to_all | solution.py:425
  67.5 0.6 temporal_sum.1
Async XLA Ops:
  1.9 13.7 %all-to-all-start = ((bf16[8,2,64]{2,1,0:T(2,128)(2,1)}), bf16[8,2,64]{2,1,0:T(2,128)(2,1)S(1)}, u32[]{:S(2)}, u32[]{:S(2)}) async-start(bf16[8,2,64]{2,1,0:T(2,128)(2,1)} %broadcast_in_dim.2), calls=%async_computation | async-start | bytes 8192 | tf_op jit(solution)/shard_map/all_to_all | solution.py:386
  17.2 13.7 %all-to-all-start.1 = ((bf16[8,2,16,512]{3,2,1,0:T(8,128)(2,1)}), bf16[8,2,16,512]{3,2,1,0:T(8,128)(2,1)S(1)}, u32[]{:S(2)}, u32[]{:S(2)}) async-start(bf16[8,2,16,512]{3,2,1,0:T(8,128)(2,1)} %bitcast.3), calls=%async_computation.1 | async-start | bytes 524288 | tf_op jit(solution)/shard_map/all_to_all | solution.py:399
  30.9 9.9 %copy-start.1 = (f32[8,2,16,512]{3,2,1,0:T(8,128)S(1)}, f32[8,2,16,512]{3,2,1,0:T(8,128)}, u32[]{:S(2)}) copy-start(f32[8,2,16,512]{3,2,1,0:T(8,128)} %get-tuple-element.27) | copy-start | bytes 1572868
  30.9 1.6 %collective-permute-start = (bf16[8,2,16,512]{3,2,1,0:T(8,128)(2,1)S(1)}, bf16[8,2,16,512]{3,2,1,0:T(8,128)(2,1)S(1)}, u32[]{:S(2)}, u32[]{:S(2)}) collective-permute-start(bf16[8,2,16,512]{3,2,1,0:T(8,128)(2,1)S(1)} %all-to-all-done.1.image_ref), channel_id=1, source_target_pairs={{0,1},{1,0},{2,3},{3,2},{4,5},{5,4},{6,7},{7,6},{8,9},{9,8},{10,11... | collective-permute-start | bytes 786440 | tf_op jit(solution)/shard_map/ppermute | solution.py:407
  32.5 23.6 %copy-start = (bf16[16,32,512]{2,1,0:T(8,128)(2,1)S(1)}, bf16[16,32,512]{2,1,0:T(8,128)(2,1)}, u32[]{:S(2)}) copy-start(bf16[16,32,512]{2,1,0:T(8,128)(2,1)} %param.6) | copy-start | bytes 1572868
  36.6 4.2 %collective-permute-start.1 = (f32[8,2,16,512]{3,2,1,0:T(8,128)S(1)}, f32[8,2,16,512]{3,2,1,0:T(8,128)S(1)}, u32[]{:S(2)}, u32[]{:S(2)}) collective-permute-start(f32[8,2,16,512]{3,2,1,0:T(8,128)S(1)} %get-tuple-element.26), channel_id=1, source_target_pairs={{0,1},{1,0},{2,3},{3,2},{4,5},{5,4},{6,7},{7,6},{8,9},{9,8},{10,11... | collective-permute-start | bytes 1572872 | tf_op jit(solution)/shard_map/ppermute | solution.py:409
  57.3 10.1 %all-to-all-start.3 = ((f32[16,1,128]{2,1,0:T(1,128)}), f32[16,1,128]{2,1,0:T(1,128)S(1)}, u32[]{:S(2)}, u32[]{:S(2)}) async-start(f32[16,1,128]{2,1,0:T(1,128)} %temporal_rows.1), calls=%async_computation.3 | async-start | bytes 16384 | tf_op jit(solution)/shard_map/all_to_all | solution.py:425

commit v5 on v4

--- a/solution.py
+++ b/solution.py
@@ -130,11 +130,16 @@
     )
 
 
-def stage_kernel(sampled_ref, block_ref, spatial_ref, mask_out, block_out, spatial_out, sems):
+def stage_kernel(starts_ref, sampled_ref, block_ref, spatial_ref, sens_ref, kspace_ref,
+                 mask_out, block_out, spatial_out, sens_out, kspace_out, sems):
+    tile = sens_out.shape[1]
+    start = pl.ds(pl.multiple_of(starts_ref[0], tile), tile)
     copies = [
-        pltpu.make_async_copy(sampled_ref, mask_out, sems.at[0]),
-        pltpu.make_async_copy(block_ref, block_out, sems.at[1]),
-        pltpu.make_async_copy(spatial_ref, spatial_out, sems.at[2]),
+        pltpu.make_async_copy(spatial_ref, spatial_out, sems.at[0]),
+        pltpu.make_async_copy(sampled_ref, mask_out, sems.at[1]),
+        pltpu.make_async_copy(block_ref, block_out, sems.at[2]),
+        pltpu.make_async_copy(sens_ref.at[:, start], sens_out, sems.at[3]),
+        pltpu.make_async_copy(kspace_ref.at[:, :, start], kspace_out, sems.at[4]),
     ]
     for copy in copies:
         copy.start()
@@ -142,34 +147,38 @@
         copy.wait()
 
 
-def data_kernel(tile, ahead, starts_ref, mask_ref, block_ref, kspace_ref, sens_ref,
-                first_ref, normal_ref, other_ref, own_ref,
-                back, kspace_held, sens_held, own_held, kspace_sem, sens_sem, first_sem, own_sem):
+def data_plan(rows, tile):
+    own = [(1, 0, tile)]
+    own += [(1, at, min(2 * tile, rows - at)) for at in range(tile, rows, 2 * tile)]
+    other = [(0, tile, tile)] if rows > tile else []
+    other += [(0, at, min(2 * tile, rows - at)) for at in range(2 * tile, rows, 2 * tile)]
+    return [(0, 0, tile)] + own + other
+
+
+def data_kernel(plan, starts_ref, mask_ref, block_ref, first_ref, kspace_first_ref, kspace_ref, sens_ref,
+                normal_ref, other_ref, own_ref, back, own_held, own_sem, *held):
     frames, coils, rows, width = kspace_ref.shape
     groups, _, per, _ = own_ref.shape
     half = width // 2
-    steps = rows // tile
-    part_steps = steps // 2
-    step_groups = tile // per
+    pieces = [held[4 * k : 4 * k + 4] for k in range(len(plan) - 1)]
 
     def fetch(step):
-        slot = lax.rem(step, ahead + 1)
-        start = starts_ref[1 - step // part_steps] + lax.rem(step, part_steps) * tile
-        place = pl.ds(pl.multiple_of(start, tile), tile)
-        copies = [pltpu.make_async_copy(sens_ref.at[:, place], sens_held.at[slot], sens_sem.at[slot])]
+        part, at, size = plan[step]
+        kspace_held, sens_held, kspace_sem, sens_sem = pieces[step - 1]
+        place = pl.ds(pl.multiple_of(starts_ref[part] + at, plan[0][2]), size)
+        copies = [pltpu.make_async_copy(sens_ref.at[:, place], sens_held, sens_sem)]
         for t in range(frames):
-            source = kspace_ref.at[t, :, place]
             copies.append(
-                pltpu.make_async_copy(source, kspace_held.at[slot, t], kspace_sem.at[slot, t])
+                pltpu.make_async_copy(kspace_ref.at[t, :, place], kspace_held.at[t], kspace_sem.at[t])
             )
         return copies
 
-    for step in range(min(ahead, steps)):
-        for copy in fetch(step):
-            copy.start()
-    start = pl.ds(pl.multiple_of(starts_ref[0], tile), tile)
-    staging = pltpu.make_async_copy(sens_ref.at[:, start], first_ref, first_sem)
-    staging.start()
+    def begin(step):
+        if step < len(plan):
+            for copy in fetch(step):
+                copy.start()
+
+    begin(1)
     block = block_ref[...]
     for t in range(frames):
         keep = mask_ref[t : t + 1, :].astype(F32)
@@ -180,42 +189,34 @@
         back[t, half:, :half] = sine_part
         back[t, half:, half:] = cosine
         normal_ref[t] = dot(block, back[t]).astype(BF16)
-
-    def part(first_step, store):
-        @pl.loop(0, part_steps)
-        def _(k):
-            step = first_step + k
-
-            @pl.when(step + ahead < steps)
-            def _():
-                for copy in fetch(step + ahead):
-                    copy.start()
-
+    begin(2)
+    own_left = sum(part == 1 for part, _, _ in plan)
+    leaving = pltpu.make_async_copy(own_held, own_ref, own_sem)
+    for step, (part, at, size) in enumerate(plan):
+        if step:
+            begin(step + 2)
             copies = fetch(step)
             copies[0].wait()
-            slot = lax.rem(step, ahead + 1)
-            sens = sens_held[slot].astype(F32)
-            sens_r, sens_i = sens[..., :half], sens[..., half:]
-            for t in range(frames):
+            kspace_held, sens_held = pieces[step - 1][:2]
+        else:
+            kspace_held, sens_held = kspace_first_ref, first_ref
+        sens = sens_held[...].astype(F32)
+        sens_r, sens_i = sens[..., :half], sens[..., half:]
+        for t in range(frames):
+            if step:
                 copies[1 + t].wait()
-                adjoint = dot(kspace_held[slot, t].reshape(coils * tile, width), back[t])
-                store(k, t, *conj_sum(adjoint.reshape(coils, tile, width), sens_r, sens_i))
-
-    def store_own(k, t, real, imag):
-        group = pl.ds(k * step_groups, step_groups)
-        own_held[group, t, :, :half] = real.reshape(step_groups, per, half)
-        own_held[group, t, :, half:] = imag.reshape(step_groups, per, half)
-
-    def store_other(k, t, real, imag):
-        place = pl.ds(k * tile, tile)
-        other_ref[t, place, :half] = real
-        other_ref[t, place, half:] = imag
-
-    part(0, store_own)
-    leaving = pltpu.make_async_copy(own_held, own_ref, own_sem)
-    leaving.start()
-    part(part_steps, store_other)
-    staging.wait()
+            adjoint = dot(kspace_held[t].reshape(coils * size, width), back[t])
+            real, imag = conj_sum(adjoint.reshape(coils, size, width), sens_r, sens_i)
+            if part:
+                group = slice(at // per, (at + size) // per)
+                own_held[group, t, :, :half] = real.reshape(size // per, per, half)
+                own_held[group, t, :, half:] = imag.reshape(size // per, per, half)
+            else:
+                other_ref[t, at : at + size, :half] = real
+                other_ref[t, at : at + size, half:] = imag
+        own_left -= part
+        if part and own_left == 0:
+            leaving.start()
     leaving.wait()
 
 
@@ -299,50 +300,52 @@
     return pltpu.CompilerParams(vmem_limit_bytes=mib * MIB)
 
 
-def stage(sampled, block, spatial):
+def stage(starts, sampled, block, spatial, sens, kspace, tile):
+    frames, coils, _, width = kspace.shape
     return pl.pallas_call(
         stage_kernel,
-        in_specs=[HBM, HBM, HBM],
-        out_specs=[VMEM, VMEM, VMEM],
+        in_specs=[SMEM] + [HBM] * 5,
+        out_specs=[VMEM] * 5,
         out_shape=[
             pltpu.VMEM(sampled.shape, jnp.int32),
             pltpu.VMEM(block.shape, BF16),
             pltpu.VMEM(spatial.shape, BF16),
+            pltpu.VMEM((coils, tile, width), BF16),
+            pltpu.VMEM((frames, coils, tile, width), BF16),
         ],
-        scratch_shapes=[pltpu.SemaphoreType.DMA((3,))],
+        scratch_shapes=[pltpu.SemaphoreType.DMA((5,))],
         cost_estimate=cost(0, 8 * block.size),
         compiler_params=grant(12),
         name="stage",
-    )(remote(sampled), remote(block), remote(spatial))
-
-
-def data_term(starts, mask, block, kspace, sens, per, tile, ahead):
+    )(starts, remote(sampled), remote(block), remote(spatial), remote(sens), remote(kspace))
+
+
+def data_term(starts, mask, block, first, kspace_first, kspace, sens, per):
     frames, coils, rows, width = kspace.shape
     own = (rows // 2 // per, frames, per, width)
+    plan = data_plan(rows // 2, first.shape[1])
+    scratch = [pltpu.VMEM((frames, width, width), BF16), pltpu.VMEM(own, F32), pltpu.SemaphoreType.DMA]
+    for _, _, size in plan[1:]:
+        scratch += [
+            pltpu.VMEM((frames, coils, size, width), BF16),
+            pltpu.VMEM((coils, size, width), BF16),
+            pltpu.SemaphoreType.DMA((frames,)),
+            pltpu.SemaphoreType.DMA,
+        ]
     return pl.pallas_call(
-        functools.partial(data_kernel, tile, ahead),
-        in_specs=[SMEM, VMEM, VMEM, HBM, HBM],
-        out_specs=[VMEM, VMEM, VMEM, HBM],
+        functools.partial(data_kernel, plan),
+        in_specs=[SMEM] + [VMEM] * 4 + [HBM] * 2,
+        out_specs=[VMEM, VMEM, HBM],
         out_shape=[
-            pltpu.VMEM((coils, tile, width), BF16),
             pltpu.VMEM((frames, width // 2, width), BF16),
             pltpu.VMEM((frames, rows // 2, width), F32),
             pltpu.HBM(own, F32),
         ],
-        scratch_shapes=[
-            pltpu.VMEM((frames, width, width), BF16),
-            pltpu.VMEM((ahead + 1, frames, coils, tile, width), BF16),
-            pltpu.VMEM((ahead + 1, coils, tile, width), BF16),
-            pltpu.VMEM(own, F32),
-            pltpu.SemaphoreType.DMA((ahead + 1, frames)),
-            pltpu.SemaphoreType.DMA((ahead + 1,)),
-            pltpu.SemaphoreType.DMA,
-            pltpu.SemaphoreType.DMA,
-        ],
+        scratch_shapes=scratch,
         cost_estimate=cost(2 * frames * coils * rows * width * width, 2 * kspace.size),
-        compiler_params=grant(32),
+        compiler_params=grant(36),
         name="data_term",
-    )(starts, mask, block, remote(kspace), remote(sens))
+    )(starts, mask, block, first, kspace_first, remote(kspace), remote(sens))
 
 
 def normal_term(starts, image, first, sens, normal, data=None):
@@ -386,7 +389,9 @@
     factors = lax.all_to_all(
         jnp.broadcast_to(temporal[None], (frame_size, per, 2 * rank)), "frame", 0, 0, tiled=True
     )
-    mask, block, near = stage(sampled, jnp.asarray(dft_half(width // 2)), spatial2)
+    mask, block, near, first, kspace_first = stage(
+        starts, sampled, jnp.asarray(dft_half(width // 2)), spatial2, sensitivity, kspace, 32
+    )
     image = pl.pallas_call(
         functools.partial(image_kernel, total, rows, rank),
         in_specs=[VMEM, VMEM],
@@ -398,8 +403,8 @@
     image, kspace = lax.optimization_barrier((image, kspace))
     image = lax.all_to_all(image.reshape(frame_size, per, rows, width), "frame", 0, 0, tiled=True)
     regroup = rows % 16 != 0
-    first, normal, data_other, data_own = data_term(
-        starts, mask, block, kspace, sensitivity, 16 if regroup else rows, 32, 3
+    normal, data_other, data_own = data_term(
+        starts, mask, block, first, kspace_first, kspace, sensitivity, 16 if regroup else rows
     )
     image, normal = lax.optimization_barrier((image, normal))
     if regroup:

time: 68.5 us -> 67.7 us (0.988)
  waiting for transfers between devices: 11.5 us -> 10.3 us
    all_to_all x1, waiting for transfers between devices: 5.25 us -> 4.11 us  [on_device(): lax.all_to_all(jnp.broadcast_to(temporal[None], (frame_size, per, 2 * ran...]
  transfers between devices with their start and end apart: 5 -> 5, of which waited for: 3 -> 3; matrix products, arithmetic and copies ran while one was open for 0% -> 0% of each run, Pallas kernels for 25% -> 26%
where the time goes in v5:
time: 67.7 us; the launch traced here: 67.3 us
  Pallas kernels  24.8 us (37%)
  blocking collectives  15.2 us (22%)
  starting transfers between devices  14.7 us (22%)
  waiting for transfers between devices  10.3 us (15%)
  local copies, waits for them, and re-layouts  1.26 us (2%)
  between operations  0.73 us (1%)
    all_to_all x1, blocking collectives, on_device(): lax.all_to_all(grad, 'frame', 0, 0, tiled=True).reshape(total * rows, width)  15.2 us
    pallas_call x1, Pallas kernels, data_term(): pl.pallas_call(functools.partial(data_kernel, plan), in_specs=[SMEM] + [V...  9.36 us
    pallas_call x2, Pallas kernels, normal_term(): pl.pallas_call(functools.partial(normal_kernel, other), in_specs=[SMEM, V...  8 us
    all_to_all x1, starting transfers between devices, on_device(): lax.all_to_all(jnp.broadcast_to(temporal[None], (frame_size, per, 2 * ran...  7.31 us
    all_to_all x1, waiting for transfers between devices, on_device(): partial = lax.all_to_all(partial, ('frame', 'coil'), 0, 0, tiled=True)  4.68 us
    all_to_all x1, waiting for transfers between devices, on_device(): lax.all_to_all(jnp.broadcast_to(temporal[None], (frame_size, per, 2 * ran...  4.11 us
    all_to_all x1, starting transfers between devices, on_device(): partial = lax.all_to_all(partial, ('frame', 'coil'), 0, 0, tiled=True)  3.69 us
    all_to_all x1, starting transfers between devices, on_device(): lax.all_to_all(image.reshape(frame_size, per, rows, width), 'frame', 0, 0...  3.41 us
  transfers between devices with their start and end apart: 5, of which 3 were waited for; matrix products, arithmetic and copies ran while one was open for 0% of the time, Pallas kernels for 26%

profile of v5, /device:TPU:0, one launch (start us, length us, event | category | flops | bytes accessed | tf_op | source)
XLA Modules:
  0.0 67.3 jit_solution(1619531642916383074)
XLA Ops:
  0.6 1.2 %broadcast_in_dim.2 = bf16[8,2,64]{2,1,0:T(2,128)(2,1)} broadcast(bf16[2,64]{1,0:T(2,128)(2,1)} %param.7), dimensions={1,2} | broadcast | bytes 2304 | tf_op jit(solution)/shard_map/broadcast_in_dim | solution.py:390
  1.9 7.3 %all-to-all-start = ((bf16[8,2,64]{2,1,0:T(2,128)(2,1)}), bf16[8,2,64]{2,1,0:T(2,128)(2,1)S(1)}, u32[]{:S(2)}, u32[]{:S(2)}) async-start(bf16[8,2,64]{2,1,0:T(2,128)(2,1)} %broadcast_in_dim.2), calls=%async_computation | async-start | bytes 8192 | tf_op jit(solution)/shard_map/all_to_all | solution.py:389
  9.2 0.1 pad_add_fusion.starts_ref
  9.3 2.2 %stage.1 = (s32[2,256]{1,0:T(2,128)S(1)}, bf16[256,512]{1,0:T(8,128)(2,1)S(1)}, bf16[512,512]{1,0:T(8,128)(2,1)S(1)}, bf16[16,32,512]{2,1,0:T(8,128)(2,1)S(1)}, bf16[2,16,32,512]{3,2,1,0:T(8,128)(2,1)S(1)}) custom-call(s32[2]{0:T(128)S(1)} %pad_add_fusion.starts_ref, s32[2,256]{1,0:T(2,128)} %sampled_ref.1, bf16[256,512]{1,0:T(8,128)(2,1)} %constant.21.clone.block_ref, ...), custom_call_target="tpu_custom_call" | custom-call | bytes 1048576 | tf_op jit(solution)/shard_map/stage/pallas_call | solution.py:305
  11.5 4.1 %all-to-all-done.factors_ref = bf16[8,2,64]{2,1,0:T(2,128)(2,1)S(1)} async-done(((bf16[8,2,64]{2,1,0:T(2,128)(2,1)}), bf16[8,2,64]{2,1,0:T(2,128)(2,1)S(1)}, u32[]{:S(2)}, u32[]{:S(2)}) %all-to-all-start) | async-done | bytes 2080 | tf_op jit(solution)/shard_map/all_to_all | solution.py:389
  15.6 1.6 %image_rows.1 = bf16[256,512]{1,0:T(8,128)(2,1)} custom-call(bf16[8,2,64]{2,1,0:T(2,128)(2,1)S(1)} %all-to-all-done.factors_ref, bf16[512,512]{1,0:T(8,128)(2,1)S(1)} %get-tuple-element.16.spatial_ref), custom_call_target="tpu_custom_call" | custom-call | tf_op jit(solution)/shard_map/image_rows/pallas_call | solution.py:395
  17.2 3.4 %all-to-all-start.1 = ((bf16[8,2,16,512]{3,2,1,0:T(8,128)(2,1)}), bf16[8,2,16,512]{3,2,1,0:T(8,128)(2,1)S(1)}, u32[]{:S(2)}, u32[]{:S(2)}) async-start(bf16[8,2,16,512]{3,2,1,0:T(8,128)(2,1)} %bitcast.3), calls=%async_computation.1 | async-start | bytes 524288 | tf_op jit(solution)/shard_map/all_to_all | solution.py:404
  20.7 9.4 %data_term.1 = (bf16[2,256,512]{2,1,0:T(8,128)(2,1)S(1)}, f32[2,128,512]{2,1,0:T(8,128)S(1)}, f32[8,2,16,512]{3,2,1,0:T(8,128)}) custom-call(s32[2]{0:T(128)S(1)} %pad_add_fusion.starts_ref, s32[2,256]{1,0:T(2,128)S(1)} %get-tuple-element.18.mask_ref, bf16[256,512]{1,0:T(8,128)(2,1)S(1)} %get-tuple-element.19.block_ref, ...), custom_call_target="tpu_custom_call" | custom-call | flops 4294967296 | bytes 8388608 | tf_op jit(solution)/shard_map/data_term/pallas_call | solution.py:335
  30.0 0.0 copy-start.1
  30.1 0.0 all-to-all-done.1.image_ref
  30.1 0.1 collective-permute-start
  30.1 1.5 %collective-permute-done.image_ref = bf16[8,2,16,512]{3,2,1,0:T(8,128)(2,1)S(1)} collective-permute-done((bf16[8,2,16,512]{3,2,1,0:T(8,128)(2,1)S(1)}, bf16[8,2,16,512]{3,2,1,0:T(8,128)(2,1)S(1)}, u32[]{:S(2)}, u32[]{:S(2)}) %collective-permute-start) | collective-permute-done | bytes 262176 | tf_op jit(solution)/shard_map/ppermute | solution.py:412
  31.7 0.0 copy-start
  31.7 4.0 %normal_other.1 = (f32[8,2,16,512]{3,2,1,0:T(8,128)S(1)}, bf16[16,32,512]{2,1,0:T(8,128)(2,1)S(1)}) custom-call(s32[2]{0:T(128)S(1)} %pad_add_fusion.starts_ref, bf16[8,2,16,512]{3,2,1,0:T(8,128)(2,1)S(1)} %collective-permute-done.image_ref, bf16[16,32,512]{2,1,0:T(8,128)(2,1)S(1)} %get-tuple-element.20.first_ref, bf16[16,256,512]{2,1,0:T(8,128)(2,1)} %sens_ref.7, ...), custom_call_target="tpu_custom_call" | custom-call | flops 2147483648 | bytes 2097152 | tf_op jit(solution)/shard_map/normal_other/pallas_call | solution.py:365
  35.7 0.2 collective-permute-start.1
  35.9 4.0 %normal_own.1 = f32[8,2,16,512]{3,2,1,0:T(8,128)S(1)} custom-call(s32[2]{0:T(128)S(1)} %pad_add_fusion.starts_ref, bf16[8,2,16,512]{3,2,1,0:T(8,128)(2,1)S(1)} %all-to-all-done.1.image_ref, bf16[16,32,512]{2,1,0:T(8,128)(2,1)S(1)} %get-tuple-element.27.first_ref, bf16[16,256,512]{2,1,0:T(8,128)(2,1)} %sens_ref.7, ...), custom_call_target="tpu_custom_call" | custom-call | flops 2147483648 | bytes 2097152 | tf_op jit(solution)/shard_map/normal_own/pallas_call | solution.py:365
  39.9 0.0 collective-permute-done.1
  39.9 0.0 copy-done.1
  39.9 0.2 subtract_convert_fusion
  40.1 15.2 %all_to_all.20 = bf16[8,2,16,512]{3,2,1,0:T(8,128)(2,1)S(1)} all-to-all(bf16[8,2,16,512]{3,2,1,0:T(8,128)(2,1)S(1)} %subtract_convert_fusion), channel_id=1, replica_groups=mesh['cuts'=2,'frame'=8,'coil'=2] {'frame'}, dimensions={0} | all-to-all | bytes 524288 | tf_op jit(solution)/shard_map/all_to_all | solution.py:419
  55.3 0.0 copy-done
  55.3 1.2 %temporal_rows.1 = f32[16,1,128]{2,1,0:T(1,128)} custom-call(bf16[512,512]{1,0:T(8,128)(2,1)S(1)} %bitcast.9, bf16[256,512]{1,0:T(8,128)(2,1)S(1)} %bitcast.6), custom_call_target="tpu_custom_call" | custom-call | tf_op jit(solution)/shard_map/temporal_rows/pallas_call | solution.py:422
  56.5 3.7 %all-to-all-start.3 = ((f32[16,1,128]{2,1,0:T(1,128)}), f32[16,1,128]{2,1,0:T(1,128)S(1)}, u32[]{:S(2)}, u32[]{:S(2)}) async-start(f32[16,1,128]{2,1,0:T(1,128)} %temporal_rows.1), calls=%async_computation.3 | async-start | bytes 16384 | tf_op jit(solution)/shard_map/all_to_all | solution.py:430
  60.2 1.7 %spatial_rows.1 = f32[512,512]{1,0:T(8,128)} custom-call(bf16[8,2,64]{2,1,0:T(2,128)(2,1)S(1)} %all-to-all-done.factors_ref, bf16[256,512]{1,0:T(8,128)(2,1)S(1)} %bitcast.7), custom_call_target="tpu_custom_call" | custom-call | tf_op jit(solution)/shard_map/spatial_rows/pallas_call | solution.py:431
  62.0 4.7 %all-to-all-done.3.parts_ref = f32[16,1,128]{2,1,0:T(1,128)S(1)} async-done(((f32[16,1,128]{2,1,0:T(1,128)}), f32[16,1,128]{2,1,0:T(1,128)S(1)}, u32[]{:S(2)}, u32[]{:S(2)}) %all-to-all-start.3) | async-done | bytes 8224 | tf_op jit(solution)/shard_map/all_to_all | solution.py:430
  66.6 0.6 temporal_sum.1
Async XLA Ops:
  1.9 13.7 %all-to-all-start = ((bf16[8,2,64]{2,1,0:T(2,128)(2,1)}), bf16[8,2,64]{2,1,0:T(2,128)(2,1)S(1)}, u32[]{:S(2)}, u32[]{:S(2)}) async-start(bf16[8,2,64]{2,1,0:T(2,128)(2,1)} %broadcast_in_dim.2), calls=%async_computation | async-start | bytes 8192 | tf_op jit(solution)/shard_map/all_to_all | solution.py:389
  17.2 12.8 %all-to-all-start.1 = ((bf16[8,2,16,512]{3,2,1,0:T(8,128)(2,1)}), bf16[8,2,16,512]{3,2,1,0:T(8,128)(2,1)S(1)}, u32[]{:S(2)}, u32[]{:S(2)}) async-start(bf16[8,2,16,512]{3,2,1,0:T(8,128)(2,1)} %bitcast.3), calls=%async_computation.1 | async-start | bytes 524288 | tf_op jit(solution)/shard_map/all_to_all | solution.py:404
  30.0 9.9 %copy-start.1 = (f32[8,2,16,512]{3,2,1,0:T(8,128)S(1)}, f32[8,2,16,512]{3,2,1,0:T(8,128)}, u32[]{:S(2)}) copy-start(f32[8,2,16,512]{3,2,1,0:T(8,128)} %get-tuple-element.29) | copy-start | bytes 1572868
  30.1 1.6 %collective-permute-start = (bf16[8,2,16,512]{3,2,1,0:T(8,128)(2,1)S(1)}, bf16[8,2,16,512]{3,2,1,0:T(8,128)(2,1)S(1)}, u32[]{:S(2)}, u32[]{:S(2)}) collective-permute-start(bf16[8,2,16,512]{3,2,1,0:T(8,128)(2,1)S(1)} %all-to-all-done.1.image_ref), channel_id=1, source_target_pairs={{0,1},{1,0},{2,3},{3,2},{4,5},{5,4},{6,7},{7,6},{8,9},{9,8},{10,11... | collective-permute-start | bytes 786440 | tf_op jit(solution)/shard_map/ppermute | solution.py:412
  31.7 23.6 %copy-start = (bf16[16,32,512]{2,1,0:T(8,128)(2,1)S(1)}, bf16[16,32,512]{2,1,0:T(8,128)(2,1)}, u32[]{:S(2)}) copy-start(bf16[16,32,512]{2,1,0:T(8,128)(2,1)} %param.6) | copy-start | bytes 1572868
  35.7 4.2 %collective-permute-start.1 = (f32[8,2,16,512]{3,2,1,0:T(8,128)S(1)}, f32[8,2,16,512]{3,2,1,0:T(8,128)S(1)}, u32[]{:S(2)}, u32[]{:S(2)}) collective-permute-start(f32[8,2,16,512]{3,2,1,0:T(8,128)S(1)} %get-tuple-element.28), channel_id=1, source_target_pairs={{0,1},{1,0},{2,3},{3,2},{4,5},{5,4},{6,7},{7,6},{8,9},{9,8},{10,11... | collective-permute-start | bytes 1572872 | tf_op jit(solution)/shard_map/ppermute | solution.py:414
  56.5 10.1 %all-to-all-start.3 = ((f32[16,1,128]{2,1,0:T(1,128)}), f32[16,1,128]{2,1,0:T(1,128)S(1)}, u32[]{:S(2)}, u32[]{:S(2)}) async-start(f32[16,1,128]{2,1,0:T(1,128)} %temporal_rows.1), calls=%async_computation.3 | async-start | bytes 16384 | tf_op jit(solution)/shard_map/all_to_all | solution.py:430

commit v6 on v5

--- a/solution.py
+++ b/solution.py
@@ -132,14 +132,13 @@
 
 def stage_kernel(starts_ref, sampled_ref, block_ref, spatial_ref, sens_ref, kspace_ref,
                  mask_out, block_out, spatial_out, sens_out, kspace_out, sems):
-    tile = sens_out.shape[1]
-    start = pl.ds(pl.multiple_of(starts_ref[0], tile), tile)
+    start = pl.multiple_of(starts_ref[0], sens_out.shape[1])
     copies = [
         pltpu.make_async_copy(spatial_ref, spatial_out, sems.at[0]),
         pltpu.make_async_copy(sampled_ref, mask_out, sems.at[1]),
         pltpu.make_async_copy(block_ref, block_out, sems.at[2]),
-        pltpu.make_async_copy(sens_ref.at[:, start], sens_out, sems.at[3]),
-        pltpu.make_async_copy(kspace_ref.at[:, :, start], kspace_out, sems.at[4]),
+        pltpu.make_async_copy(sens_ref.at[:, pl.ds(start, sens_out.shape[1])], sens_out, sems.at[3]),
+        pltpu.make_async_copy(kspace_ref.at[0, :, pl.ds(start, kspace_out.shape[1])], kspace_out, sems.at[4]),
     ]
     for copy in copies:
         copy.start()
@@ -148,18 +147,16 @@
 
 
 def data_plan(rows, tile):
-    own = [(1, 0, tile)]
-    own += [(1, at, min(2 * tile, rows - at)) for at in range(tile, rows, 2 * tile)]
-    other = [(0, tile, tile)] if rows > tile else []
-    other += [(0, at, min(2 * tile, rows - at)) for at in range(2 * tile, rows, 2 * tile)]
-    return [(0, 0, tile)] + own + other
+    own = [(1, at, tile) for at in range(0, rows // 2, tile)] + [(1, rows // 2, rows // 2)]
+    return [(0, 0, tile)] + own + [(0, tile, rows - tile)]
 
 
 def data_kernel(plan, starts_ref, mask_ref, block_ref, first_ref, kspace_first_ref, kspace_ref, sens_ref,
-                normal_ref, other_ref, own_ref, back, own_held, own_sem, *held):
+                normal_ref, other_ref, own_ref, back, own_held, own_sem, late_held, late_sem, *held):
     frames, coils, rows, width = kspace_ref.shape
     groups, _, per, _ = own_ref.shape
     half = width // 2
+    quarter = half // 2
     pieces = [held[4 * k : 4 * k + 4] for k in range(len(plan) - 1)]
 
     def fetch(step):
@@ -178,6 +175,14 @@
             for copy in fetch(step):
                 copy.start()
 
+    late = []
+    for t in range(1, frames):
+        place = pl.ds(pl.multiple_of(starts_ref[0], plan[0][2]), plan[0][2])
+        late.append(
+            pltpu.make_async_copy(kspace_ref.at[t, :, place], late_held.at[t - 1], late_sem.at[t - 1])
+        )
+    for copy in late:
+        copy.start()
     begin(1)
     block = block_ref[...]
     for t in range(frames):
@@ -188,24 +193,33 @@
         back[t, :half, half:] = -sine_part
         back[t, half:, :half] = sine_part
         back[t, half:, half:] = cosine
-        normal_ref[t] = dot(block, back[t]).astype(BF16)
-    begin(2)
+        near = dot(block[:quarter], back[t])
+        for k in range(2):
+            for part in range(2):
+                at = part * half
+                low, high = near[:, at : at + quarter], near[:, at + quarter : at + half]
+                table = (0.5 * (low + high if k == 0 else low - high)).astype(BF16)
+                normal_ref[t, k, :, part * quarter : (part + 1) * quarter] = table
+        if t == 0:
+            begin(2)
     own_left = sum(part == 1 for part, _, _ in plan)
     leaving = pltpu.make_async_copy(own_held, own_ref, own_sem)
     for step, (part, at, size) in enumerate(plan):
         if step:
             begin(step + 2)
-            copies = fetch(step)
-            copies[0].wait()
+            for copy in fetch(step):
+                copy.wait()
             kspace_held, sens_held = pieces[step - 1][:2]
         else:
-            kspace_held, sens_held = kspace_first_ref, first_ref
+            kspace_held = [kspace_first_ref] + [late_held.at[t] for t in range(frames - 1)]
+            sens_held = first_ref.at[:, :size]
         sens = sens_held[...].astype(F32)
         sens_r, sens_i = sens[..., :half], sens[..., half:]
         for t in range(frames):
-            if step:
-                copies[1 + t].wait()
-            adjoint = dot(kspace_held[t].reshape(coils * size, width), back[t])
+            if step == 0 and t:
+                late[t - 1].wait()
+            kspace = kspace_held[t][...] if step == 0 else kspace_held[t]
+            adjoint = dot(kspace.reshape(coils * size, width), back[t])
             real, imag = conj_sum(adjoint.reshape(coils, size, width), sens_r, sens_i)
             if part:
                 group = slice(at // per, (at + size) // per)
@@ -228,6 +242,7 @@
     groups, frames, per, width = image_ref.shape
     coils, tile, _ = first_ref.shape
     half = width // 2
+    quarter = half // 2
     step_groups = tile // per
     steps = groups // step_groups
 
@@ -244,9 +259,11 @@
         staging = pltpu.make_async_copy(sens_ref.at[:, spot(0, 1)], next_ref, next_sem)
         staging.start()
     for t in range(frames):
-        table[t, :half] = normal_ref[t]
-        table[t, half:, :half] = -normal_ref[t, :, half:]
-        table[t, half:, half:] = normal_ref[t, :, :half]
+        for k in range(2):
+            near = normal_ref[t, k]
+            table[t, k, :quarter] = near
+            table[t, k, quarter:, :quarter] = -near[:, quarter:]
+            table[t, k, quarter:, quarter:] = near[:, :quarter]
 
     def work(step, sens):
         place = pl.ds(step * tile, tile)
@@ -256,16 +273,24 @@
         for t in range(frames):
             image = image_ref[group, t].reshape(tile, width).astype(F32)
             image_r, image_i = image[:, :half], image[:, half:]
-            coil_r = (sens_r * image_r - sens_i * image_i).astype(BF16)
-            coil_i = (sens_r * image_i + sens_i * image_r).astype(BF16)
-            coil = jnp.concatenate([coil_r, coil_i], -1).reshape(coils * tile, width)
-            adjoint = dot(coil, table[t])
-            real, imag = conj_sum(adjoint.reshape(coils, tile, width), sens_r, sens_i)
-            if other:
-                real = real - data_ref[t, place, :half]
-                imag = imag - data_ref[t, place, half:]
-            out_ref[group, t, :, :half] = real.reshape(step_groups, per, half)
-            out_ref[group, t, :, half:] = imag.reshape(step_groups, per, half)
+            coil_r = sens_r * image_r - sens_i * image_i
+            coil_i = sens_r * image_i + sens_i * image_r
+            low_r, high_r = coil_r[..., :quarter], coil_r[..., quarter:]
+            low_i, high_i = coil_i[..., :quarter], coil_i[..., quarter:]
+            plus = jnp.concatenate([low_r + high_r, low_i + high_i], -1).astype(BF16)
+            minus = jnp.concatenate([low_r - high_r, low_i - high_i], -1).astype(BF16)
+            plus = dot(plus.reshape(coils * tile, half), table[t, 0]).reshape(coils, tile, half)
+            minus = dot(minus.reshape(coils * tile, half), table[t, 1]).reshape(coils, tile, half)
+            for k, both in enumerate((plus + minus, plus - minus)):
+                lanes = slice(k * quarter, (k + 1) * quarter)
+                real, imag = conj_sum(both, sens_r[..., lanes], sens_i[..., lanes])
+                low = slice(k * quarter, (k + 1) * quarter)
+                high = slice(half + k * quarter, half + (k + 1) * quarter)
+                if other:
+                    real = real - data_ref[t, place, low]
+                    imag = imag - data_ref[t, place, high]
+                out_ref[group, t, :, low] = real.reshape(step_groups, per, quarter)
+                out_ref[group, t, :, high] = imag.reshape(step_groups, per, quarter)
 
     work(0, first_ref[...])
 
@@ -301,7 +326,7 @@
 
 
 def stage(starts, sampled, block, spatial, sens, kspace, tile):
-    frames, coils, _, width = kspace.shape
+    _, coils, _, width = kspace.shape
     return pl.pallas_call(
         stage_kernel,
         in_specs=[SMEM] + [HBM] * 5,
@@ -310,8 +335,8 @@
             pltpu.VMEM(sampled.shape, jnp.int32),
             pltpu.VMEM(block.shape, BF16),
             pltpu.VMEM(spatial.shape, BF16),
+            pltpu.VMEM((coils, 2 * tile, width), BF16),
             pltpu.VMEM((coils, tile, width), BF16),
-            pltpu.VMEM((frames, coils, tile, width), BF16),
         ],
         scratch_shapes=[pltpu.SemaphoreType.DMA((5,))],
         cost_estimate=cost(0, 8 * block.size),
@@ -323,8 +348,14 @@
 def data_term(starts, mask, block, first, kspace_first, kspace, sens, per):
     frames, coils, rows, width = kspace.shape
     own = (rows // 2 // per, frames, per, width)
-    plan = data_plan(rows // 2, first.shape[1])
-    scratch = [pltpu.VMEM((frames, width, width), BF16), pltpu.VMEM(own, F32), pltpu.SemaphoreType.DMA]
+    plan = data_plan(rows // 2, kspace_first.shape[1])
+    scratch = [
+        pltpu.VMEM((frames, width, width), BF16),
+        pltpu.VMEM(own, F32),
+        pltpu.SemaphoreType.DMA,
+        pltpu.VMEM((max(frames - 1, 1), coils, plan[0][2], width), BF16),
+        pltpu.SemaphoreType.DMA((max(frames - 1, 1),)),
+    ]
     for _, _, size in plan[1:]:
         scratch += [
             pltpu.VMEM((frames, coils, size, width), BF16),
@@ -337,7 +368,7 @@
         in_specs=[SMEM] + [VMEM] * 4 + [HBM] * 2,
         out_specs=[VMEM, VMEM, HBM],
         out_shape=[
-            pltpu.VMEM((frames, width // 2, width), BF16),
+            pltpu.VMEM((frames, 2, width // 4, width // 2), BF16),
             pltpu.VMEM((frames, rows // 2, width), F32),
             pltpu.HBM(own, F32),
         ],
@@ -355,7 +386,7 @@
     other = data is not None
     outs = [pltpu.VMEM((groups, frames, per, width), F32)]
     scratch = [
-        pltpu.VMEM((frames, width, width), BF16),
+        pltpu.VMEM((frames, 2, width // 2, width // 2), BF16),
         pltpu.VMEM((steps - 1, coils, tile, width), BF16),
         pltpu.SemaphoreType.DMA((steps - 1,)),
     ]

time: 67.7 us -> 65.4 us (0.966)
  Pallas kernels: 24.8 us -> 22.5 us
    pallas_call x1, Pallas kernels: 9.36 us -> 7.84 us  [data_term(): pl.pallas_call(functools.partial(data_kernel, plan), in_specs=[SMEM] + [V...]
    pallas_call x2, Pallas kernels: 8 us -> 7.19 us  [normal_term(): pl.pallas_call(functools.partial(normal_kernel, other), in_specs=[SMEM, V...]
  transfers between devices with their start and end apart: 5 -> 5, of which waited for: 3 -> 4; matrix products, arithmetic and copies ran while one was open for 0% -> 0% of each run, Pallas kernels for 26% -> 24%
where the time goes in v6:
time: 65.4 us; the launch traced here: 65 us
  Pallas kernels  22.5 us (34%)
  blocking collectives  15 us (23%)
  starting transfers between devices  14.6 us (22%)
  waiting for transfers between devices  10.7 us (16%)
  local copies, waits for them, and re-layouts  1.26 us (2%)
  between operations  0.71 us (1%)
    all_to_all x1, blocking collectives, on_device(): lax.all_to_all(grad, 'frame', 0, 0, tiled=True).reshape(total * rows, width)  15 us
    pallas_call x1, Pallas kernels, data_term(): pl.pallas_call(functools.partial(data_kernel, plan), in_specs=[SMEM] + [V...  7.84 us
    all_to_all x1, starting transfers between devices, on_device(): lax.all_to_all(jnp.broadcast_to(temporal[None], (frame_size, per, 2 * ran...  7.31 us
    pallas_call x2, Pallas kernels, normal_term(): pl.pallas_call(functools.partial(normal_kernel, other), in_specs=[SMEM, V...  7.19 us
    all_to_all x1, waiting for transfers between devices, on_device(): partial = lax.all_to_all(partial, ('frame', 'coil'), 0, 0, tiled=True)  4.68 us
    all_to_all x1, waiting for transfers between devices, on_device(): lax.all_to_all(jnp.broadcast_to(temporal[None], (frame_size, per, 2 * ran...  4.14 us
    all_to_all x1, starting transfers between devices, on_device(): partial = lax.all_to_all(partial, ('frame', 'coil'), 0, 0, tiled=True)  3.69 us
    all_to_all x1, starting transfers between devices, on_device(): lax.all_to_all(image.reshape(frame_size, per, rows, width), 'frame', 0, 0...  3.41 us
  transfers between devices with their start and end apart: 5, of which 4 were waited for; matrix products, arithmetic and copies ran while one was open for 0% of the time, Pallas kernels for 24%

profile of v6, /device:TPU:0, one launch (start us, length us, event | category | flops | bytes accessed | tf_op | source)
XLA Modules:
  0.0 65.0 jit_solution(3564878154973685205)
XLA Ops:
  0.6 1.2 %broadcast_in_dim.2 = bf16[8,2,64]{2,1,0:T(2,128)(2,1)} broadcast(bf16[2,64]{1,0:T(2,128)(2,1)} %param.7), dimensions={1,2} | broadcast | bytes 2304 | tf_op jit(solution)/shard_map/broadcast_in_dim | solution.py:421
  1.9 7.3 %all-to-all-start = ((bf16[8,2,64]{2,1,0:T(2,128)(2,1)}), bf16[8,2,64]{2,1,0:T(2,128)(2,1)S(1)}, u32[]{:S(2)}, u32[]{:S(2)}) async-start(bf16[8,2,64]{2,1,0:T(2,128)(2,1)} %broadcast_in_dim.2), calls=%async_computation | async-start | bytes 8192 | tf_op jit(solution)/shard_map/all_to_all | solution.py:420
  9.2 0.1 pad_add_fusion.starts_ref
  9.3 2.2 %stage.1 = (s32[2,256]{1,0:T(2,128)S(1)}, bf16[256,512]{1,0:T(8,128)(2,1)S(1)}, bf16[512,512]{1,0:T(8,128)(2,1)S(1)}, bf16[16,64,512]{2,1,0:T(8,128)(2,1)S(1)}, bf16[16,32,512]{2,1,0:T(8,128)(2,1)S(1)}) custom-call(s32[2]{0:T(128)S(1)} %pad_add_fusion.starts_ref, s32[2,256]{1,0:T(2,128)} %sampled_ref.1, bf16[256,512]{1,0:T(8,128)(2,1)} %constant.21.clone.block_ref, ...), custom_call_target="tpu_custom_call" | custom-call | bytes 1048576 | tf_op jit(solution)/shard_map/stage/pallas_call | solution.py:330
  11.5 4.1 %all-to-all-done.factors_ref = bf16[8,2,64]{2,1,0:T(2,128)(2,1)S(1)} async-done(((bf16[8,2,64]{2,1,0:T(2,128)(2,1)}), bf16[8,2,64]{2,1,0:T(2,128)(2,1)S(1)}, u32[]{:S(2)}, u32[]{:S(2)}) %all-to-all-start) | async-done | bytes 2080 | tf_op jit(solution)/shard_map/all_to_all | solution.py:420
  15.6 1.6 %image_rows.1 = bf16[256,512]{1,0:T(8,128)(2,1)} custom-call(bf16[8,2,64]{2,1,0:T(2,128)(2,1)S(1)} %all-to-all-done.factors_ref, bf16[512,512]{1,0:T(8,128)(2,1)S(1)} %get-tuple-element.16.spatial_ref), custom_call_target="tpu_custom_call" | custom-call | tf_op jit(solution)/shard_map/image_rows/pallas_call | solution.py:426
  17.2 3.4 %all-to-all-start.1 = ((bf16[8,2,16,512]{3,2,1,0:T(8,128)(2,1)}), bf16[8,2,16,512]{3,2,1,0:T(8,128)(2,1)S(1)}, u32[]{:S(2)}, u32[]{:S(2)}) async-start(bf16[8,2,16,512]{3,2,1,0:T(8,128)(2,1)} %bitcast.3), calls=%async_computation.1 | async-start | bytes 524288 | tf_op jit(solution)/shard_map/all_to_all | solution.py:435
  20.7 7.8 %data_term.1 = (bf16[2,2,128,256]{3,2,1,0:T(8,128)(2,1)S(1)}, f32[2,128,512]{2,1,0:T(8,128)S(1)}, f32[8,2,16,512]{3,2,1,0:T(8,128)}) custom-call(s32[2]{0:T(128)S(1)} %pad_add_fusion.starts_ref, s32[2,256]{1,0:T(2,128)S(1)} %get-tuple-element.18.mask_ref, bf16[256,512]{1,0:T(8,128)(2,1)S(1)} %get-tuple-element.19.block_ref, ...), custom_call_target="tpu_custom_call" | custom-call | flops 4294967296 | bytes 8388608 | tf_op jit(solution)/shard_map/data_term/pallas_call | solution.py:366
  28.5 0.0 copy-start.1
  28.5 0.3 all-to-all-done.1.image_ref
  28.8 0.0 collective-permute-start
  28.8 1.5 %collective-permute-done.image_ref = bf16[8,2,16,512]{3,2,1,0:T(8,128)(2,1)S(1)} collective-permute-done((bf16[8,2,16,512]{3,2,1,0:T(8,128)(2,1)S(1)}, bf16[8,2,16,512]{3,2,1,0:T(8,128)(2,1)S(1)}, u32[]{:S(2)}, u32[]{:S(2)}) %collective-permute-start) | collective-permute-done | bytes 262176 | tf_op jit(solution)/shard_map/ppermute | solution.py:443
  30.4 0.0 copy-start
  30.4 3.6 %normal_other.1 = (f32[8,2,16,512]{3,2,1,0:T(8,128)S(1)}, bf16[16,64,512]{2,1,0:T(8,128)(2,1)S(1)}) custom-call(s32[2]{0:T(128)S(1)} %pad_add_fusion.starts_ref, bf16[8,2,16,512]{3,2,1,0:T(8,128)(2,1)S(1)} %collective-permute-done.image_ref, bf16[16,64,512]{2,1,0:T(8,128)(2,1)S(1)} %get-tuple-element.20.first_ref, bf16[16,256,512]{2,1,0:T(8,128)(2,1)} %sens_ref.7, ...), custom_call_target="tpu_custom_call" | custom-call | flops 2147483648 | bytes 2097152 | tf_op jit(solution)/shard_map/normal_other/pallas_call | solution.py:396
  34.0 0.2 collective-permute-start.1
  34.2 3.6 %normal_own.1 = f32[8,2,16,512]{3,2,1,0:T(8,128)S(1)} custom-call(s32[2]{0:T(128)S(1)} %pad_add_fusion.starts_ref, bf16[8,2,16,512]{3,2,1,0:T(8,128)(2,1)S(1)} %all-to-all-done.1.image_ref, bf16[16,64,512]{2,1,0:T(8,128)(2,1)S(1)} %get-tuple-element.27.first_ref, bf16[16,256,512]{2,1,0:T(8,128)(2,1)} %sens_ref.7, ...), custom_call_target="tpu_custom_call" | custom-call | flops 2147483648 | bytes 2097152 | tf_op jit(solution)/shard_map/normal_own/pallas_call | solution.py:396
  37.8 0.0 collective-permute-done.1
  37.8 0.0 copy-done.1
  37.8 0.2 subtract_convert_fusion
  38.0 15.0 %all_to_all.20 = bf16[8,2,16,512]{3,2,1,0:T(8,128)(2,1)S(1)} all-to-all(bf16[8,2,16,512]{3,2,1,0:T(8,128)(2,1)S(1)} %subtract_convert_fusion), channel_id=1, replica_groups=mesh['cuts'=2,'frame'=8,'coil'=2] {'frame'}, dimensions={0} | all-to-all | bytes 524288 | tf_op jit(solution)/shard_map/all_to_all | solution.py:450
  53.0 0.0 copy-done
  53.0 1.2 %temporal_rows.1 = f32[16,1,128]{2,1,0:T(1,128)} custom-call(bf16[512,512]{1,0:T(8,128)(2,1)S(1)} %bitcast.9, bf16[256,512]{1,0:T(8,128)(2,1)S(1)} %bitcast.6), custom_call_target="tpu_custom_call" | custom-call | tf_op jit(solution)/shard_map/temporal_rows/pallas_call | solution.py:453
  54.2 3.7 %all-to-all-start.3 = ((f32[16,1,128]{2,1,0:T(1,128)}), f32[16,1,128]{2,1,0:T(1,128)S(1)}, u32[]{:S(2)}, u32[]{:S(2)}) async-start(f32[16,1,128]{2,1,0:T(1,128)} %temporal_rows.1), calls=%async_computation.3 | async-start | bytes 16384 | tf_op jit(solution)/shard_map/all_to_all | solution.py:461
  57.9 1.7 %spatial_rows.1 = f32[512,512]{1,0:T(8,128)} custom-call(bf16[8,2,64]{2,1,0:T(2,128)(2,1)S(1)} %all-to-all-done.factors_ref, bf16[256,512]{1,0:T(8,128)(2,1)S(1)} %bitcast.7), custom_call_target="tpu_custom_call" | custom-call | tf_op jit(solution)/shard_map/spatial_rows/pallas_call | solution.py:462
  59.6 4.7 %all-to-all-done.3.parts_ref = f32[16,1,128]{2,1,0:T(1,128)S(1)} async-done(((f32[16,1,128]{2,1,0:T(1,128)}), f32[16,1,128]{2,1,0:T(1,128)S(1)}, u32[]{:S(2)}, u32[]{:S(2)}) %all-to-all-start.3) | async-done | bytes 8224 | tf_op jit(solution)/shard_map/all_to_all | solution.py:461
  64.3 0.6 temporal_sum.1
Async XLA Ops:
  1.9 13.7 %all-to-all-start = ((bf16[8,2,64]{2,1,0:T(2,128)(2,1)}), bf16[8,2,64]{2,1,0:T(2,128)(2,1)S(1)}, u32[]{:S(2)}, u32[]{:S(2)}) async-start(bf16[8,2,64]{2,1,0:T(2,128)(2,1)} %broadcast_in_dim.2), calls=%async_computation | async-start | bytes 8192 | tf_op jit(solution)/shard_map/all_to_all | solution.py:420
  17.2 11.6 %all-to-all-start.1 = ((bf16[8,2,16,512]{3,2,1,0:T(8,128)(2,1)}), bf16[8,2,16,512]{3,2,1,0:T(8,128)(2,1)S(1)}, u32[]{:S(2)}, u32[]{:S(2)}) async-start(bf16[8,2,16,512]{3,2,1,0:T(8,128)(2,1)} %bitcast.3), calls=%async_computation.1 | async-start | bytes 524288 | tf_op jit(solution)/shard_map/all_to_all | solution.py:435
  28.5 9.3 %copy-start.1 = (f32[8,2,16,512]{3,2,1,0:T(8,128)S(1)}, f32[8,2,16,512]{3,2,1,0:T(8,128)}, u32[]{:S(2)}) copy-start(f32[8,2,16,512]{3,2,1,0:T(8,128)} %get-tuple-element.29) | copy-start | bytes 1572868
  28.8 1.5 %collective-permute-start = (bf16[8,2,16,512]{3,2,1,0:T(8,128)(2,1)S(1)}, bf16[8,2,16,512]{3,2,1,0:T(8,128)(2,1)S(1)}, u32[]{:S(2)}, u32[]{:S(2)}) collective-permute-start(bf16[8,2,16,512]{3,2,1,0:T(8,128)(2,1)S(1)} %all-to-all-done.1.image_ref), channel_id=1, source_target_pairs={{0,1},{1,0},{2,3},{3,2},{4,5},{5,4},{6,7},{7,6},{8,9},{9,8},{10,11... | collective-permute-start | bytes 786440 | tf_op jit(solution)/shard_map/ppermute | solution.py:443
  30.4 22.6 %copy-start = (bf16[16,32,512]{2,1,0:T(8,128)(2,1)S(1)}, bf16[16,32,512]{2,1,0:T(8,128)(2,1)}, u32[]{:S(2)}) copy-start(bf16[16,32,512]{2,1,0:T(8,128)(2,1)} %param.6) | copy-start | bytes 1572868
  34.0 3.8 %collective-permute-start.1 = (f32[8,2,16,512]{3,2,1,0:T(8,128)S(1)}, f32[8,2,16,512]{3,2,1,0:T(8,128)S(1)}, u32[]{:S(2)}, u32[]{:S(2)}) collective-permute-start(f32[8,2,16,512]{3,2,1,0:T(8,128)S(1)} %get-tuple-element.28), channel_id=1, source_target_pairs={{0,1},{1,0},{2,3},{3,2},{4,5},{5,4},{6,7},{7,6},{8,9},{9,8},{10,11... | collective-permute-start | bytes 1572872 | tf_op jit(solution)/shard_map/ppermute | solution.py:445
  54.2 10.1 %all-to-all-start.3 = ((f32[16,1,128]{2,1,0:T(1,128)}), f32[16,1,128]{2,1,0:T(1,128)S(1)}, u32[]{:S(2)}, u32[]{:S(2)}) async-start(f32[16,1,128]{2,1,0:T(1,128)} %temporal_rows.1), calls=%async_computation.3 | async-start | bytes 16384 | tf_op jit(solution)/shard_map/all_to_all | solution.py:461

commit v7 on v6

--- a/solution.py
+++ b/solution.py
@@ -132,7 +132,7 @@
 
 def stage_kernel(starts_ref, sampled_ref, block_ref, spatial_ref, sens_ref, kspace_ref,
                  mask_out, block_out, spatial_out, sens_out, kspace_out, sems):
-    start = pl.multiple_of(starts_ref[0], sens_out.shape[1])
+    start = pl.multiple_of(starts_ref[1], sens_out.shape[1])
     copies = [
         pltpu.make_async_copy(spatial_ref, spatial_out, sems.at[0]),
         pltpu.make_async_copy(sampled_ref, mask_out, sems.at[1]),
@@ -147,8 +147,8 @@
 
 
 def data_plan(rows, tile):
-    own = [(1, at, tile) for at in range(0, rows // 2, tile)] + [(1, rows // 2, rows // 2)]
-    return [(0, 0, tile)] + own + [(0, tile, rows - tile)]
+    own = [(1, at, tile) for at in range(0, rows // 2, tile)]
+    return own + [(0, 0, tile), (1, rows // 2, rows // 2), (0, tile, rows - tile)]
 
 
 def data_kernel(plan, starts_ref, mask_ref, block_ref, first_ref, kspace_first_ref, kspace_ref, sens_ref,
@@ -177,7 +177,7 @@
 
     late = []
     for t in range(1, frames):
-        place = pl.ds(pl.multiple_of(starts_ref[0], plan[0][2]), plan[0][2])
+        place = pl.ds(pl.multiple_of(starts_ref[plan[0][0]], plan[0][2]), plan[0][2])
         late.append(
             pltpu.make_async_copy(kspace_ref.at[t, :, place], late_held.at[t - 1], late_sem.at[t - 1])
         )
@@ -234,29 +234,31 @@
     leaving.wait()
 
 
-def normal_kernel(other, starts_ref, image_ref, first_ref, sens_ref, normal_ref, *rest):
-    if other:
-        data_ref, out_ref, next_ref, table, sens_held, sem, next_sem = rest
+def normal_kernel(part, begin, end, following, starts_ref, image_ref, first_ref, sens_ref, normal_ref, *rest):
+    data_ref = rest[0] if part == 0 else None
+    rest = list(rest[1:]) if part == 0 or begin else list(rest)
+    if following:
+        out_ref, next_ref, table, sens_held, sem, next_sem = rest
     else:
         out_ref, table, sens_held, sem = rest
-    groups, frames, per, width = image_ref.shape
+    _, frames, per, width = image_ref.shape
     coils, tile, _ = first_ref.shape
     half = width // 2
     quarter = half // 2
     step_groups = tile // per
-    steps = groups // step_groups
-
-    def spot(step, which):
-        return pl.ds(pl.multiple_of(starts_ref[which] + step * tile, tile), tile)
+    steps = (end - begin) // tile
+
+    def spot(which, at):
+        return pl.ds(pl.multiple_of(starts_ref[which] + at, tile), tile)
 
     def fetch(step):
-        source = sens_ref.at[:, spot(step, 0 if other else 1)]
+        source = sens_ref.at[:, spot(part, begin + step * tile)]
         return pltpu.make_async_copy(source, sens_held.at[step - 1], sem.at[step - 1])
 
     for step in range(1, steps):
         fetch(step).start()
-    if other:
-        staging = pltpu.make_async_copy(sens_ref.at[:, spot(0, 1)], next_ref, next_sem)
+    if following:
+        staging = pltpu.make_async_copy(sens_ref.at[:, spot(*following)], next_ref, next_sem)
         staging.start()
     for t in range(frames):
         for k in range(2):
@@ -266,8 +268,8 @@
             table[t, k, quarter:, quarter:] = near[:, :quarter]
 
     def work(step, sens):
-        place = pl.ds(step * tile, tile)
-        group = pl.ds(step * step_groups, step_groups)
+        place = pl.ds(begin + step * tile, tile)
+        group = pl.ds(begin // per + step * step_groups, step_groups)
         sens = sens.astype(F32)
         sens_r, sens_i = sens[..., :half], sens[..., half:]
         for t in range(frames):
@@ -286,7 +288,7 @@
                 real, imag = conj_sum(both, sens_r[..., lanes], sens_i[..., lanes])
                 low = slice(k * quarter, (k + 1) * quarter)
                 high = slice(half + k * quarter, half + (k + 1) * quarter)
-                if other:
+                if part == 0:
                     real = real - data_ref[t, place, low]
                     imag = imag - data_ref[t, place, high]
                 out_ref[group, t, :, low] = real.reshape(step_groups, per, quarter)
@@ -299,7 +301,7 @@
         fetch(step).wait()
         work(step, sens_held[step - 1])
 
-    if other:
+    if following:
         staging.wait()
 
 
@@ -379,32 +381,33 @@
     )(starts, mask, block, first, kspace_first, remote(kspace), remote(sens))
 
 
-def normal_term(starts, image, first, sens, normal, data=None):
+def normal_term(part, begin, end, following, starts, image, first, sens, normal, more=()):
     groups, frames, per, width = image.shape
     coils, tile, _ = first.shape
-    steps = groups * per // tile
-    other = data is not None
+    steps = (end - begin) // tile
+    spare = max(steps - 1, 1)
     outs = [pltpu.VMEM((groups, frames, per, width), F32)]
     scratch = [
         pltpu.VMEM((frames, 2, width // 2, width // 2), BF16),
-        pltpu.VMEM((steps - 1, coils, tile, width), BF16),
-        pltpu.SemaphoreType.DMA((steps - 1,)),
+        pltpu.VMEM((spare, coils, tile, width), BF16),
+        pltpu.SemaphoreType.DMA((spare,)),
     ]
-    if other:
+    if following:
         outs.append(pltpu.VMEM(first.shape, BF16))
         scratch.append(pltpu.SemaphoreType.DMA)
     return pl.pallas_call(
-        functools.partial(normal_kernel, other),
-        in_specs=[SMEM, VMEM, VMEM, HBM, VMEM] + [VMEM] * other,
+        functools.partial(normal_kernel, part, begin, end, following),
+        in_specs=[SMEM, VMEM, VMEM, HBM, VMEM] + [VMEM] * len(more),
         out_specs=[VMEM] * len(outs),
         out_shape=outs,
         scratch_shapes=scratch,
+        input_output_aliases={5: 0} if part and begin else {},
         cost_estimate=cost(
-            2 * frames * coils * groups * per * width * width, coils * groups * per * width * 2
+            frames * coils * (end - begin) * width * width, coils * (end - begin) * width * 2
         ),
-        compiler_params=grant(20),
-        name="normal_other" if other else "normal_own",
-    )(starts, image, first, remote(sens), normal, *([data] if other else []))
+        compiler_params=grant(32),
+        name="normal_term",
+    )(starts, image, first, remote(sens), normal, *more)
 
 
 def on_device(frame_size, coil_size, spatial, temporal, kspace, sampled, sensitivity):
@@ -441,9 +444,17 @@
     if regroup:
         image = image.transpose(1, 0, 2, 3).reshape(per, half_rows // 16, 16, width).transpose(1, 0, 2, 3)
     image_other = lax.ppermute(image, "coil", swap)
-    send, first = normal_term(starts, local(image_other), first, sensitivity, normal, data_other)
+    middle = half_rows // 2
+    image = local(image)
+    keep_own, first = normal_term(1, 0, middle, (0, 0), starts, image, first, sensitivity, normal)
+    image_other, keep_own = lax.optimization_barrier((image_other, keep_own))
+    send, first = normal_term(
+        0, 0, half_rows, (1, middle), starts, local(image_other), first, sensitivity, normal, (data_other,)
+    )
     received = lax.ppermute(send, "coil", swap)
-    (keep_own,) = normal_term(starts, local(image), first, sensitivity, normal)
+    (keep_own,) = normal_term(
+        1, middle, half_rows, None, starts, image, first, sensitivity, normal, (keep_own,)
+    )
     grad = (keep_own + received - data_own).astype(BF16)
     if regroup:
         grad = grad.transpose(1, 0, 2, 3).reshape(per, frame_size, rows, width).transpose(1, 0, 2, 3)

time: 65.4 us -> 64 us (0.979)
  waiting for transfers between devices: 10.7 us -> 9.47 us
  blocking collectives: 15 us -> 14.2 us
    ppermute x1, waiting for transfers between devices: 1.53 us -> 0.01 us  [on_device(): image_other = lax.ppermute(image, 'coil', swap)]
    all_to_all x1, blocking collectives: 15 us -> 14.2 us  [on_device(): lax.all_to_all(grad, 'frame', 0, 0, tiled=True).reshape(total * rows, width)]
    pallas_call x2 -> x3, Pallas kernels: 7.19 us -> 7.72 us  [normal_term(): pl.pallas_call(functools.partial(normal_kernel, part, begin, end, followi...]
  transfers between devices with their start and end apart: 5 -> 5, of which waited for: 4 -> 3; matrix products, arithmetic and copies ran while one was open for 0% -> 0% of each run, Pallas kernels for 24% -> 24%
where the time goes in v7:
time: 64 us; the launch traced here: 63.6 us
  Pallas kernels  22.7 us (35%)
  starting transfers between devices  15 us (23%)
  blocking collectives  14.2 us (22%)
  waiting for transfers between devices  9.47 us (15%)
  local copies, waits for them, and re-layouts  1.26 us (2%)
  between operations  0.73 us (1%)
    all_to_all x1, blocking collectives, on_device(): lax.all_to_all(grad, 'frame', 0, 0, tiled=True).reshape(total * rows, width)  14.2 us
    pallas_call x3, Pallas kernels, normal_term(): pl.pallas_call(functools.partial(normal_kernel, part, begin, end, followi...  7.72 us
    pallas_call x1, Pallas kernels, data_term(): pl.pallas_call(functools.partial(data_kernel, plan), in_specs=[SMEM] + [V...  7.5 us
    all_to_all x1, starting transfers between devices, on_device(): lax.all_to_all(jnp.broadcast_to(temporal[None], (frame_size, per, 2 * ran...  7.31 us
    all_to_all x1, waiting for transfers between devices, on_device(): partial = lax.all_to_all(partial, ('frame', 'coil'), 0, 0, tiled=True)  4.67 us
    all_to_all x1, waiting for transfers between devices, on_device(): lax.all_to_all(jnp.broadcast_to(temporal[None], (frame_size, per, 2 * ran...  4.14 us
    all_to_all x1, starting transfers between devices, on_device(): partial = lax.all_to_all(partial, ('frame', 'coil'), 0, 0, tiled=True)  3.69 us
    all_to_all x1, starting transfers between devices, on_device(): lax.all_to_all(image.reshape(frame_size, per, rows, width), 'frame', 0, 0...  3.41 us
  transfers between devices with their start and end apart: 5, of which 3 were waited for; matrix products, arithmetic and copies ran while one was open for 0% of the time, Pallas kernels for 24%

profile of v7, /device:TPU:0, one launch (start us, length us, event | category | flops | bytes accessed | tf_op | source)
XLA Modules:
  0.0 63.6 jit_solution(15467097476568754496)
XLA Ops:
  0.6 1.2 %broadcast_in_dim.2 = bf16[8,2,64]{2,1,0:T(2,128)(2,1)} broadcast(bf16[2,64]{1,0:T(2,128)(2,1)} %param.7), dimensions={1,2} | broadcast | bytes 2304 | tf_op jit(solution)/shard_map/broadcast_in_dim | solution.py:424
  1.9 7.3 %all-to-all-start = ((bf16[8,2,64]{2,1,0:T(2,128)(2,1)}), bf16[8,2,64]{2,1,0:T(2,128)(2,1)S(1)}, u32[]{:S(2)}, u32[]{:S(2)}) async-start(bf16[8,2,64]{2,1,0:T(2,128)(2,1)} %broadcast_in_dim.2), calls=%async_computation | async-start | bytes 8192 | tf_op jit(solution)/shard_map/all_to_all | solution.py:423
  9.2 0.1 pad_add_fusion.starts_ref
  9.3 2.2 %stage.1 = (s32[2,256]{1,0:T(2,128)S(1)}, bf16[256,512]{1,0:T(8,128)(2,1)S(1)}, bf16[512,512]{1,0:T(8,128)(2,1)S(1)}, bf16[16,64,512]{2,1,0:T(8,128)(2,1)S(1)}, bf16[16,32,512]{2,1,0:T(8,128)(2,1)S(1)}) custom-call(s32[2]{0:T(128)S(1)} %pad_add_fusion.starts_ref, s32[2,256]{1,0:T(2,128)} %sampled_ref.1, bf16[256,512]{1,0:T(8,128)(2,1)} %constant.21.clone.block_ref, ...), custom_call_target="tpu_custom_call" | custom-call | bytes 1048576 | tf_op jit(solution)/shard_map/stage/pallas_call | solution.py:332
  11.5 4.1 %all-to-all-done.factors_ref = bf16[8,2,64]{2,1,0:T(2,128)(2,1)S(1)} async-done(((bf16[8,2,64]{2,1,0:T(2,128)(2,1)}), bf16[8,2,64]{2,1,0:T(2,128)(2,1)S(1)}, u32[]{:S(2)}, u32[]{:S(2)}) %all-to-all-start) | async-done | bytes 2080 | tf_op jit(solution)/shard_map/all_to_all | solution.py:423
  15.6 1.6 %image_rows.1 = bf16[256,512]{1,0:T(8,128)(2,1)} custom-call(bf16[8,2,64]{2,1,0:T(2,128)(2,1)S(1)} %all-to-all-done.factors_ref, bf16[512,512]{1,0:T(8,128)(2,1)S(1)} %get-tuple-element.20.spatial_ref), custom_call_target="tpu_custom_call" | custom-call | tf_op jit(solution)/shard_map/image_rows/pallas_call | solution.py:429
  17.2 3.4 %all-to-all-start.1 = ((bf16[8,2,16,512]{3,2,1,0:T(8,128)(2,1)}), bf16[8,2,16,512]{3,2,1,0:T(8,128)(2,1)S(1)}, u32[]{:S(2)}, u32[]{:S(2)}) async-start(bf16[8,2,16,512]{3,2,1,0:T(8,128)(2,1)} %bitcast.3), calls=%async_computation.1 | async-start | bytes 524288 | tf_op jit(solution)/shard_map/all_to_all | solution.py:438
  20.7 7.5 %data_term.1 = (bf16[2,2,128,256]{3,2,1,0:T(8,128)(2,1)S(1)}, f32[2,128,512]{2,1,0:T(8,128)S(1)}, f32[8,2,16,512]{3,2,1,0:T(8,128)}) custom-call(s32[2]{0:T(128)S(1)} %pad_add_fusion.starts_ref, s32[2,256]{1,0:T(2,128)S(1)} %get-tuple-element.22.mask_ref, bf16[256,512]{1,0:T(8,128)(2,1)S(1)} %get-tuple-element.23.block_ref, ...), custom_call_target="tpu_custom_call" | custom-call | flops 4294967296 | bytes 8388608 | tf_op jit(solution)/shard_map/data_term/pallas_call | solution.py:368
  28.2 0.7 %all-to-all-done.1.image_ref = bf16[8,2,16,512]{3,2,1,0:T(8,128)(2,1)S(1)} async-done(((bf16[8,2,16,512]{3,2,1,0:T(8,128)(2,1)}), bf16[8,2,16,512]{3,2,1,0:T(8,128)(2,1)S(1)}, u32[]{:S(2)}, u32[]{:S(2)}) %all-to-all-start.1) | async-done | bytes 262176 | tf_op jit(solution)/shard_map/all_to_all | solution.py:438
  28.8 0.0 copy-start.1
  28.8 0.0 collective-permute-start
  28.8 2.1 %normal_term.3 = (f32[8,2,16,512]{3,2,1,0:T(8,128)S(1)}, bf16[16,64,512]{2,1,0:T(8,128)(2,1)S(1)}) custom-call(s32[2]{0:T(128)S(1)} %pad_add_fusion.starts_ref, bf16[8,2,16,512]{3,2,1,0:T(8,128)(2,1)S(1)} %all-to-all-done.1.image_ref, bf16[16,64,512]{2,1,0:T(8,128)(2,1)S(1)} %get-tuple-element.24.first_ref, bf16[16,256,512]{2,1,0:T(8,128)(2,1)} %sens_ref.9, ...), custom_call_target="tpu_custom_call" | custom-call | flops 536870912 | bytes 1048576 | tf_op jit(solution)/shard_map/normal_term/pallas_call | solution.py:398
  30.9 0.0 copy-start
  30.9 0.0 collective-permute-done.image_ref
  30.9 3.6 %normal_term.4 = (f32[8,2,16,512]{3,2,1,0:T(8,128)S(1)}, bf16[16,64,512]{2,1,0:T(8,128)(2,1)S(1)}) custom-call(s32[2]{0:T(128)S(1)} %pad_add_fusion.starts_ref, bf16[8,2,16,512]{3,2,1,0:T(8,128)(2,1)S(1)} %collective-permute-done.image_ref, bf16[16,64,512]{2,1,0:T(8,128)(2,1)S(1)} %get-tuple-element.32.first_ref, bf16[16,256,512]{2,1,0:T(8,128)(2,1)} %sens_ref.9, ...), custom_call_target="tpu_custom_call" | custom-call | flops 1073741824 | bytes 2097152 | tf_op jit(solution)/shard_map/normal_term/pallas_call | solution.py:398
  34.5 0.6 collective-permute-start.1
  35.1 2.1 %normal_term.5 = f32[8,2,16,512]{3,2,1,0:T(8,128)S(1)} custom-call(s32[2]{0:T(128)S(1)} %pad_add_fusion.starts_ref, bf16[8,2,16,512]{3,2,1,0:T(8,128)(2,1)S(1)} %all-to-all-done.1.image_ref, bf16[16,64,512]{2,1,0:T(8,128)(2,1)S(1)} %get-tuple-element.34.first_ref, bf16[16,256,512]{2,1,0:T(8,128)(2,1)} %sens_ref.9, ...), custom_call_target="tpu_custom_call", output_to_operand_aliasing={{}: (5, {})} | custom-call | flops 536870912 | bytes 1048576 | tf_op jit(solution)/shard_map/normal_term/pallas_call | solution.py:398
  37.2 0.0 collective-permute-done.1
  37.2 0.0 copy-done.1
  37.2 0.2 subtract_convert_fusion
  37.4 14.2 %all_to_all.20 = bf16[8,2,16,512]{3,2,1,0:T(8,128)(2,1)S(1)} all-to-all(bf16[8,2,16,512]{3,2,1,0:T(8,128)(2,1)S(1)} %subtract_convert_fusion), channel_id=1, replica_groups=mesh['cuts'=2,'frame'=8,'coil'=2] {'frame'}, dimensions={0} | all-to-all | bytes 524288 | tf_op jit(solution)/shard_map/all_to_all | solution.py:461
  51.6 0.0 copy-done
  51.6 1.2 %temporal_rows.1 = f32[16,1,128]{2,1,0:T(1,128)} custom-call(bf16[512,512]{1,0:T(8,128)(2,1)S(1)} %bitcast.9, bf16[256,512]{1,0:T(8,128)(2,1)S(1)} %bitcast.6), custom_call_target="tpu_custom_call" | custom-call | tf_op jit(solution)/shard_map/temporal_rows/pallas_call | solution.py:464
  52.9 3.7 %all-to-all-start.3 = ((f32[16,1,128]{2,1,0:T(1,128)}), f32[16,1,128]{2,1,0:T(1,128)S(1)}, u32[]{:S(2)}, u32[]{:S(2)}) async-start(f32[16,1,128]{2,1,0:T(1,128)} %temporal_rows.1), calls=%async_computation.3 | async-start | bytes 16384 | tf_op jit(solution)/shard_map/all_to_all | solution.py:472
  56.6 1.7 %spatial_rows.1 = f32[512,512]{1,0:T(8,128)} custom-call(bf16[8,2,64]{2,1,0:T(2,128)(2,1)S(1)} %all-to-all-done.factors_ref, bf16[256,512]{1,0:T(8,128)(2,1)S(1)} %bitcast.7), custom_call_target="tpu_custom_call" | custom-call | tf_op jit(solution)/shard_map/spatial_rows/pallas_call | solution.py:473
  58.3 4.7 %all-to-all-done.3.parts_ref = f32[16,1,128]{2,1,0:T(1,128)S(1)} async-done(((f32[16,1,128]{2,1,0:T(1,128)}), f32[16,1,128]{2,1,0:T(1,128)S(1)}, u32[]{:S(2)}, u32[]{:S(2)}) %all-to-all-start.3) | async-done | bytes 8224 | tf_op jit(solution)/shard_map/all_to_all | solution.py:472
  63.0 0.6 %temporal_sum.1 = f32[2,64]{1,0:T(2,128)} custom-call(f32[16,1,128]{2,1,0:T(1,128)S(1)} %all-to-all-done.3.parts_ref), custom_call_target="tpu_custom_call" | custom-call | tf_op jit(solution)/shard_map/temporal_sum/pallas_call | solution.py:481
Async XLA Ops:
  1.9 13.7 %all-to-all-start = ((bf16[8,2,64]{2,1,0:T(2,128)(2,1)}), bf16[8,2,64]{2,1,0:T(2,128)(2,1)S(1)}, u32[]{:S(2)}, u32[]{:S(2)}) async-start(bf16[8,2,64]{2,1,0:T(2,128)(2,1)} %broadcast_in_dim.2), calls=%async_computation | async-start | bytes 8192 | tf_op jit(solution)/shard_map/all_to_all | solution.py:423
  17.2 11.6 %all-to-all-start.1 = ((bf16[8,2,16,512]{3,2,1,0:T(8,128)(2,1)}), bf16[8,2,16,512]{3,2,1,0:T(8,128)(2,1)S(1)}, u32[]{:S(2)}, u32[]{:S(2)}) async-start(bf16[8,2,16,512]{3,2,1,0:T(8,128)(2,1)} %bitcast.3), calls=%async_computation.1 | async-start | bytes 524288 | tf_op jit(solution)/shard_map/all_to_all | solution.py:438
  28.8 8.4 %copy-start.1 = (f32[8,2,16,512]{3,2,1,0:T(8,128)S(1)}, f32[8,2,16,512]{3,2,1,0:T(8,128)}, u32[]{:S(2)}) copy-start(f32[8,2,16,512]{3,2,1,0:T(8,128)} %get-tuple-element.37) | copy-start | bytes 1572868
  28.8 2.1 %collective-permute-start = (bf16[8,2,16,512]{3,2,1,0:T(8,128)(2,1)S(1)}, bf16[8,2,16,512]{3,2,1,0:T(8,128)(2,1)S(1)}, u32[]{:S(2)}, u32[]{:S(2)}) collective-permute-start(bf16[8,2,16,512]{3,2,1,0:T(8,128)(2,1)S(1)} %all-to-all-done.1.image_ref), channel_id=1, source_target_pairs={{0,1},{1,0},{2,3},{3,2},{4,5},{5,4},{6,7},{7,6},{8,9},{9,8},{10,11... | collective-permute-start | bytes 786440 | tf_op jit(solution)/shard_map/ppermute | solution.py:446
  30.9 20.7 %copy-start = (bf16[16,32,512]{2,1,0:T(8,128)(2,1)S(1)}, bf16[16,32,512]{2,1,0:T(8,128)(2,1)}, u32[]{:S(2)}) copy-start(bf16[16,32,512]{2,1,0:T(8,128)(2,1)} %param.6) | copy-start | bytes 1572868
  34.5 2.7 %collective-permute-start.1 = (f32[8,2,16,512]{3,2,1,0:T(8,128)S(1)}, f32[8,2,16,512]{3,2,1,0:T(8,128)S(1)}, u32[]{:S(2)}, u32[]{:S(2)}) collective-permute-start(f32[8,2,16,512]{3,2,1,0:T(8,128)S(1)} %get-tuple-element.36), channel_id=1, source_target_pairs={{0,1},{1,0},{2,3},{3,2},{4,5},{5,4},{6,7},{7,6},{8,9},{9,8},{10,11... | collective-permute-start | bytes 1572872 | tf_op jit(solution)/shard_map/ppermute | solution.py:454
  52.9 10.1 %all-to-all-start.3 = ((f32[16,1,128]{2,1,0:T(1,128)}), f32[16,1,128]{2,1,0:T(1,128)S(1)}, u32[]{:S(2)}, u32[]{:S(2)}) async-start(f32[16,1,128]{2,1,0:T(1,128)} %temporal_rows.1), calls=%async_computation.3 | async-start | bytes 16384 | tf_op jit(solution)/shard_map/all_to_all | solution.py:472

commit v8 on v7

--- a/solution.py
+++ b/solution.py
@@ -60,6 +60,59 @@
     mid_col = product.shape[1] // 2
     image_ref[:, :mid_col] = (product[:half, :mid_col] - product[half:, mid_col:]).astype(BF16)
     image_ref[:, mid_col:] = (product[:half, mid_col:] + product[half:, :mid_col]).astype(BF16)
+
+
+def image_block_kernel(total, rows, rank, factors_ref, spatial_ref, image_ref, wide, held, sems):
+    groups, per, lanes = factors_ref.shape
+    width = rows * rank
+    half = total * rows
+    source = iota((lanes, 2 * width), 1)
+    source = source // width * rank + source % rank
+    tile = jnp.where(iota((lanes, 2 * width), 0) == source, 1.0, 0.0).astype(BF16)
+    same = iota((rows, width), 0) == iota((rows, width), 1) // rank
+    factors = factors_ref[...].astype(F32)
+    for t in range(per):
+        lines = dot(factors[:, t].astype(BF16), tile)
+        for group in range(groups):
+            for part in range(2):
+                line = lines[group : group + 1, part * width : (part + 1) * width]
+                at = part * half + (group * per + t) * rows
+                wide[at : at + rows] = jnp.where(same, line, 0.0).astype(BF16)
+    spatial = spatial_ref[...]
+    mid = spatial.shape[1] // 2
+    copies = []
+    for piece in range(2):
+        place = slice(piece * half // 2, (piece + 1) * half // 2)
+        real = dot(wide[place], spatial)
+        imag = dot(wide[half + place.start : half + place.stop], spatial)
+        held[place, :mid] = (real[:, :mid] - imag[:, mid:]).astype(BF16)
+        held[place, mid:] = (real[:, mid:] + imag[:, :mid]).astype(BF16)
+        copies.append(pltpu.make_async_copy(held.at[place], image_ref.at[place], sems.at[piece]))
+        copies[-1].start()
+    for copy in copies:
+        copy.wait()
+
+
+def image_rows(total, rows, rank, factors, spatial):
+    shape = (total * rows, spatial.shape[1])
+    if rows % 16:
+        body, outs, space, scratch = image_kernel, pltpu.VMEM(shape, BF16), VMEM, []
+    else:
+        body, outs, space = image_block_kernel, pltpu.HBM(shape, BF16), HBM
+        scratch = [
+            pltpu.VMEM((2 * total * rows, rows * rank), BF16),
+            pltpu.VMEM(shape, BF16),
+            pltpu.SemaphoreType.DMA((2,)),
+        ]
+    return pl.pallas_call(
+        functools.partial(body, total, rows, rank),
+        in_specs=[VMEM, VMEM],
+        out_specs=space,
+        out_shape=outs,
+        scratch_shapes=scratch,
+        compiler_params=grant(12),
+        name="image_rows",
+    )(local(factors), spatial)
 
 
 def both_parts(grad):
@@ -426,14 +479,7 @@
     mask, block, near, first, kspace_first = stage(
         starts, sampled, jnp.asarray(dft_half(width // 2)), spatial2, sensitivity, kspace, 32
     )
-    image = pl.pallas_call(
-        functools.partial(image_kernel, total, rows, rank),
-        in_specs=[VMEM, VMEM],
-        out_specs=VMEM,
-        out_shape=pltpu.VMEM((total * rows, width), BF16),
-        compiler_params=grant(12),
-        name="image_rows",
-    )(local(factors), near)
+    image = image_rows(total, rows, rank, factors, near)
     image, kspace = lax.optimization_barrier((image, kspace))
     image = lax.all_to_all(image.reshape(frame_size, per, rows, width), "frame", 0, 0, tiled=True)
     regroup = rows % 16 != 0

time: 64 us -> 63.7 us (level)
  transfers between devices with their start and end apart: 5 -> 5, of which waited for: 3 -> 3; matrix products, arithmetic and copies ran while one was open for 0% -> 0% of each run, Pallas kernels for 24% -> 25%
where the time goes in v8:
time: 63.7 us; the launch traced here: 63.3 us
  Pallas kernels  22.3 us (35%)
  starting transfers between devices  15 us (24%)
  blocking collectives  14.2 us (22%)
  waiting for transfers between devices  9.47 us (15%)
  local copies, waits for them, and re-layouts  1.26 us (2%)
  between operations  0.74 us (1%)
    all_to_all x1, blocking collectives, on_device(): lax.all_to_all(grad, 'frame', 0, 0, tiled=True).reshape(total * rows, width)  14.2 us
    pallas_call x3, Pallas kernels, normal_term(): pl.pallas_call(functools.partial(normal_kernel, part, begin, end, followi...  7.79 us
    pallas_call x1, Pallas kernels, data_term(): pl.pallas_call(functools.partial(data_kernel, plan), in_specs=[SMEM] + [V...  7.5 us
    all_to_all x1, starting transfers between devices, on_device(): lax.all_to_all(jnp.broadcast_to(temporal[None], (frame_size, per, 2 * ran...  7.31 us
    all_to_all x1, waiting for transfers between devices, on_device(): partial = lax.all_to_all(partial, ('frame', 'coil'), 0, 0, tiled=True)  4.67 us
    all_to_all x1, waiting for transfers between devices, on_device(): lax.all_to_all(jnp.broadcast_to(temporal[None], (frame_size, per, 2 * ran...  4.14 us
    all_to_all x1, starting transfers between devices, on_device(): partial = lax.all_to_all(partial, ('frame', 'coil'), 0, 0, tiled=True)  3.69 us
    all_to_all x1, starting transfers between devices, on_device(): lax.all_to_all(image.reshape(frame_size, per, rows, width), 'frame', 0, 0...  3.42 us
  transfers between devices with their start and end apart: 5, of which 3 were waited for; matrix products, arithmetic and copies ran while one was open for 0% of the time, Pallas kernels for 25%

profile of v8, /device:TPU:0, one launch (start us, length us, event | category | flops | bytes accessed | tf_op | source)
XLA Modules:
  0.0 63.3 jit_solution(3407641015983854640)
XLA Ops:
  0.6 1.2 %broadcast_in_dim.2 = bf16[8,2,64]{2,1,0:T(2,128)(2,1)} broadcast(bf16[2,64]{1,0:T(2,128)(2,1)} %param.7), dimensions={1,2} | broadcast | bytes 2304 | tf_op jit(solution)/shard_map/broadcast_in_dim | solution.py:477
  1.9 7.3 %all-to-all-start = ((bf16[8,2,64]{2,1,0:T(2,128)(2,1)}), bf16[8,2,64]{2,1,0:T(2,128)(2,1)S(1)}, u32[]{:S(2)}, u32[]{:S(2)}) async-start(bf16[8,2,64]{2,1,0:T(2,128)(2,1)} %broadcast_in_dim.2), calls=%async_computation | async-start | bytes 8192 | tf_op jit(solution)/shard_map/all_to_all | solution.py:476
  9.2 0.1 pad_add_fusion.starts_ref
  9.3 2.2 %stage.1 = (s32[2,256]{1,0:T(2,128)S(1)}, bf16[256,512]{1,0:T(8,128)(2,1)S(1)}, bf16[512,512]{1,0:T(8,128)(2,1)S(1)}, bf16[16,64,512]{2,1,0:T(8,128)(2,1)S(1)}, bf16[16,32,512]{2,1,0:T(8,128)(2,1)S(1)}) custom-call(s32[2]{0:T(128)S(1)} %pad_add_fusion.starts_ref, s32[2,256]{1,0:T(2,128)} %sampled_ref.1, bf16[256,512]{1,0:T(8,128)(2,1)} %constant.21.clone.block_ref, ...), custom_call_target="tpu_custom_call" | custom-call | bytes 1048576 | tf_op jit(solution)/shard_map/stage/pallas_call | solution.py:385
  11.5 4.1 %all-to-all-done.factors_ref = bf16[8,2,64]{2,1,0:T(2,128)(2,1)S(1)} async-done(((bf16[8,2,64]{2,1,0:T(2,128)(2,1)}), bf16[8,2,64]{2,1,0:T(2,128)(2,1)S(1)}, u32[]{:S(2)}, u32[]{:S(2)}) %all-to-all-start) | async-done | bytes 2080 | tf_op jit(solution)/shard_map/all_to_all | solution.py:476
  15.6 1.2 %image_rows.1 = bf16[256,512]{1,0:T(8,128)(2,1)} custom-call(bf16[8,2,64]{2,1,0:T(2,128)(2,1)S(1)} %all-to-all-done.factors_ref, bf16[512,512]{1,0:T(8,128)(2,1)S(1)} %get-tuple-element.20.spatial_ref), custom_call_target="tpu_custom_call" | custom-call | tf_op jit(solution)/shard_map/image_rows/pallas_call | solution.py:107
  16.9 3.4 %all-to-all-start.1 = ((bf16[8,2,16,512]{3,2,1,0:T(8,128)(2,1)}), bf16[8,2,16,512]{3,2,1,0:T(8,128)(2,1)S(1)}, u32[]{:S(2)}, u32[]{:S(2)}) async-start(bf16[8,2,16,512]{3,2,1,0:T(8,128)(2,1)} %bitcast.11), calls=%async_computation.1 | async-start | bytes 524288 | tf_op jit(solution)/shard_map/all_to_all | solution.py:484
  20.3 7.5 %data_term.1 = (bf16[2,2,128,256]{3,2,1,0:T(8,128)(2,1)S(1)}, f32[2,128,512]{2,1,0:T(8,128)S(1)}, f32[8,2,16,512]{3,2,1,0:T(8,128)}) custom-call(s32[2]{0:T(128)S(1)} %pad_add_fusion.starts_ref, s32[2,256]{1,0:T(2,128)S(1)} %get-tuple-element.22.mask_ref, bf16[256,512]{1,0:T(8,128)(2,1)S(1)} %get-tuple-element.23.block_ref, ...), custom_call_target="tpu_custom_call" | custom-call | flops 4294967296 | bytes 8388608 | tf_op jit(solution)/shard_map/data_term/pallas_call | solution.py:421
  27.8 0.7 %all-to-all-done.1.image_ref = bf16[8,2,16,512]{3,2,1,0:T(8,128)(2,1)S(1)} async-done(((bf16[8,2,16,512]{3,2,1,0:T(8,128)(2,1)}), bf16[8,2,16,512]{3,2,1,0:T(8,128)(2,1)S(1)}, u32[]{:S(2)}, u32[]{:S(2)}) %all-to-all-start.1) | async-done | bytes 262176 | tf_op jit(solution)/shard_map/all_to_all | solution.py:484
  28.4 0.0 copy-start.1
  28.4 0.0 collective-permute-start
  28.5 2.1 %normal_term.3 = (f32[8,2,16,512]{3,2,1,0:T(8,128)S(1)}, bf16[16,64,512]{2,1,0:T(8,128)(2,1)S(1)}) custom-call(s32[2]{0:T(128)S(1)} %pad_add_fusion.starts_ref, bf16[8,2,16,512]{3,2,1,0:T(8,128)(2,1)S(1)} %all-to-all-done.1.image_ref, bf16[16,64,512]{2,1,0:T(8,128)(2,1)S(1)} %get-tuple-element.24.first_ref, bf16[16,256,512]{2,1,0:T(8,128)(2,1)} %sens_ref.9, ...), custom_call_target="tpu_custom_call" | custom-call | flops 536870912 | bytes 1048576 | tf_op jit(solution)/shard_map/normal_term/pallas_call | solution.py:451
  30.5 0.0 copy-start
  30.6 0.0 collective-permute-done.image_ref
  30.6 3.6 %normal_term.4 = (f32[8,2,16,512]{3,2,1,0:T(8,128)S(1)}, bf16[16,64,512]{2,1,0:T(8,128)(2,1)S(1)}) custom-call(s32[2]{0:T(128)S(1)} %pad_add_fusion.starts_ref, bf16[8,2,16,512]{3,2,1,0:T(8,128)(2,1)S(1)} %collective-permute-done.image_ref, bf16[16,64,512]{2,1,0:T(8,128)(2,1)S(1)} %get-tuple-element.32.first_ref, bf16[16,256,512]{2,1,0:T(8,128)(2,1)} %sens_ref.9, ...), custom_call_target="tpu_custom_call" | custom-call | flops 1073741824 | bytes 2097152 | tf_op jit(solution)/shard_map/normal_term/pallas_call | solution.py:451
  34.2 0.6 collective-permute-start.1
  34.8 2.1 %normal_term.5 = f32[8,2,16,512]{3,2,1,0:T(8,128)S(1)} custom-call(s32[2]{0:T(128)S(1)} %pad_add_fusion.starts_ref, bf16[8,2,16,512]{3,2,1,0:T(8,128)(2,1)S(1)} %all-to-all-done.1.image_ref, bf16[16,64,512]{2,1,0:T(8,128)(2,1)S(1)} %get-tuple-element.34.first_ref, bf16[16,256,512]{2,1,0:T(8,128)(2,1)} %sens_ref.9, ...), custom_call_target="tpu_custom_call", output_to_operand_aliasing={{}: (5, {})} | custom-call | flops 536870912 | bytes 1048576 | tf_op jit(solution)/shard_map/normal_term/pallas_call | solution.py:451
  36.9 0.0 collective-permute-done.1
  36.9 0.0 copy-done.1
  36.9 0.2 subtract_convert_fusion
  37.1 14.2 %all_to_all.20 = bf16[8,2,16,512]{3,2,1,0:T(8,128)(2,1)S(1)} all-to-all(bf16[8,2,16,512]{3,2,1,0:T(8,128)(2,1)S(1)} %subtract_convert_fusion), channel_id=1, replica_groups=mesh['cuts'=2,'frame'=8,'coil'=2] {'frame'}, dimensions={0} | all-to-all | bytes 524288 | tf_op jit(solution)/shard_map/all_to_all | solution.py:507
  51.3 0.0 copy-done
  51.3 1.2 %temporal_rows.1 = f32[16,1,128]{2,1,0:T(1,128)} custom-call(bf16[512,512]{1,0:T(8,128)(2,1)S(1)} %bitcast.9, bf16[256,512]{1,0:T(8,128)(2,1)S(1)} %bitcast.6), custom_call_target="tpu_custom_call" | custom-call | tf_op jit(solution)/shard_map/temporal_rows/pallas_call | solution.py:510
  52.5 3.7 %all-to-all-start.3 = ((f32[16,1,128]{2,1,0:T(1,128)}), f32[16,1,128]{2,1,0:T(1,128)S(1)}, u32[]{:S(2)}, u32[]{:S(2)}) async-start(f32[16,1,128]{2,1,0:T(1,128)} %temporal_rows.1), calls=%async_computation.3 | async-start | bytes 16384 | tf_op jit(solution)/shard_map/all_to_all | solution.py:518
  56.2 1.7 %spatial_rows.1 = f32[512,512]{1,0:T(8,128)} custom-call(bf16[8,2,64]{2,1,0:T(2,128)(2,1)S(1)} %all-to-all-done.factors_ref, bf16[256,512]{1,0:T(8,128)(2,1)S(1)} %bitcast.7), custom_call_target="tpu_custom_call" | custom-call | tf_op jit(solution)/shard_map/spatial_rows/pallas_call | solution.py:519
  58.0 4.7 %all-to-all-done.3.parts_ref = f32[16,1,128]{2,1,0:T(1,128)S(1)} async-done(((f32[16,1,128]{2,1,0:T(1,128)}), f32[16,1,128]{2,1,0:T(1,128)S(1)}, u32[]{:S(2)}, u32[]{:S(2)}) %all-to-all-start.3) | async-done | bytes 8224 | tf_op jit(solution)/shard_map/all_to_all | solution.py:518
  62.7 0.6 %temporal_sum.1 = f32[2,64]{1,0:T(2,128)} custom-call(f32[16,1,128]{2,1,0:T(1,128)S(1)} %all-to-all-done.3.parts_ref), custom_call_target="tpu_custom_call" | custom-call | tf_op jit(solution)/shard_map/temporal_sum/pallas_call | solution.py:527
Async XLA Ops:
  1.9 13.7 %all-to-all-start = ((bf16[8,2,64]{2,1,0:T(2,128)(2,1)}), bf16[8,2,64]{2,1,0:T(2,128)(2,1)S(1)}, u32[]{:S(2)}, u32[]{:S(2)}) async-start(bf16[8,2,64]{2,1,0:T(2,128)(2,1)} %broadcast_in_dim.2), calls=%async_computation | async-start | bytes 8192 | tf_op jit(solution)/shard_map/all_to_all | solution.py:476
  16.9 11.6 %all-to-all-start.1 = ((bf16[8,2,16,512]{3,2,1,0:T(8,128)(2,1)}), bf16[8,2,16,512]{3,2,1,0:T(8,128)(2,1)S(1)}, u32[]{:S(2)}, u32[]{:S(2)}) async-start(bf16[8,2,16,512]{3,2,1,0:T(8,128)(2,1)} %bitcast.11), calls=%async_computation.1 | async-start | bytes 524288 | tf_op jit(solution)/shard_map/all_to_all | solution.py:484
  28.4 8.4 %copy-start.1 = (f32[8,2,16,512]{3,2,1,0:T(8,128)S(1)}, f32[8,2,16,512]{3,2,1,0:T(8,128)}, u32[]{:S(2)}) copy-start(f32[8,2,16,512]{3,2,1,0:T(8,128)} %get-tuple-element.37) | copy-start | bytes 1572868
  28.4 2.1 %collective-permute-start = (bf16[8,2,16,512]{3,2,1,0:T(8,128)(2,1)S(1)}, bf16[8,2,16,512]{3,2,1,0:T(8,128)(2,1)S(1)}, u32[]{:S(2)}, u32[]{:S(2)}) collective-permute-start(bf16[8,2,16,512]{3,2,1,0:T(8,128)(2,1)S(1)} %all-to-all-done.1.image_ref), channel_id=1, source_target_pairs={{0,1},{1,0},{2,3},{3,2},{4,5},{5,4},{6,7},{7,6},{8,9},{9,8},{10,11... | collective-permute-start | bytes 786440 | tf_op jit(solution)/shard_map/ppermute | solution.py:492
  30.5 20.8 %copy-start = (bf16[16,32,512]{2,1,0:T(8,128)(2,1)S(1)}, bf16[16,32,512]{2,1,0:T(8,128)(2,1)}, u32[]{:S(2)}) copy-start(bf16[16,32,512]{2,1,0:T(8,128)(2,1)} %param.6) | copy-start | bytes 1572868
  34.2 2.7 %collective-permute-start.1 = (f32[8,2,16,512]{3,2,1,0:T(8,128)S(1)}, f32[8,2,16,512]{3,2,1,0:T(8,128)S(1)}, u32[]{:S(2)}, u32[]{:S(2)}) collective-permute-start(f32[8,2,16,512]{3,2,1,0:T(8,128)S(1)} %get-tuple-element.36), channel_id=1, source_target_pairs={{0,1},{1,0},{2,3},{3,2},{4,5},{5,4},{6,7},{7,6},{8,9},{9,8},{10,11... | collective-permute-start | bytes 1572872 | tf_op jit(solution)/shard_map/ppermute | solution.py:500
  52.5 10.1 %all-to-all-start.3 = ((f32[16,1,128]{2,1,0:T(1,128)}), f32[16,1,128]{2,1,0:T(1,128)S(1)}, u32[]{:S(2)}, u32[]{:S(2)}) async-start(f32[16,1,128]{2,1,0:T(1,128)} %temporal_rows.1), calls=%async_computation.3 | async-start | bytes 16384 | tf_op jit(solution)/shard_map/all_to_all | solution.py:518

commit v9 on v8

v9 whole, which is shorter than its diff:
```python
import functools
import math

import jax
import jax.numpy as jnp
import numpy as np
from jax import lax
from jax.experimental import pallas as pl
from jax.experimental.pallas import tpu as pltpu
from jax.sharding import PartitionSpec as P


F32 = jnp.float32
BF16 = jnp.bfloat16


def dft_tables(length):
    index = np.arange(length)
    angles = (index[:, None] * index[None, :] % length) * (2.0 * math.pi / length)
    cosine = np.cos(angles) / math.sqrt(length)
    sine_part = -np.sin(angles) / math.sqrt(length)
    block = np.block([[cosine, sine_part], [-sine_part, cosine]]).astype(np.float32)
    middle = length // 2
    left, right = [], []
    for odd in range(2):
        lines = np.concatenate([index[odd::2], length + index[odd::2]])
        near = np.concatenate([index[:middle], length + index[:middle]])
        left.append(block[:middle][:, lines])
        right.append(block.T[lines][:, near])
    order = np.concatenate([index[0::2], index[1::2]])
    picks = (index[:, None] == order[None, :]).astype(np.float32)
    return [np.asarray(a).astype(BF16) for a in (block[:length], np.stack(left), np.stack(right), picks)]


def dot(a, b):
    return jnp.dot(a, b, preferred_element_type=F32)


def dot_t(a, b):
    return lax.dot_general(a, b, (((1,), (1,)), ((), ())), preferred_element_type=F32)


def iota(shape, axis):
    return lax.broadcasted_iota(jnp.int32, shape, axis)


def spread(factors_ref, total, rows, rank):
    groups, per, lanes = factors_ref.shape
    height = 2 * total * rows
    frame = iota((height, groups), 0) // rows % total
    factors = factors_ref[...].astype(F32)
    picked = jnp.zeros((height, lanes), F32)
    for t in range(per):
        pick = jnp.where(frame == iota((height, groups), 1) * per + t, 1.0, 0.0).astype(BF16)
        picked = picked + dot(pick, factors[:, t].astype(BF16))
    mine = iota((height, lanes), 1) // rank == iota((height, lanes), 0) // (total * rows)
    return jnp.where(mine, picked, 0.0).astype(BF16)


def image_kernel(total, rows, rank, factors_ref, spatial_ref, image_ref):
    mid = spread(factors_ref, total, rows, rank)
    lanes = mid.shape[1]
    width = rows * rank
    tile = jnp.where(iota((lanes, width), 0) % rank == iota((lanes, width), 1) % rank, 1.0, 0.0)
    wide = dot(mid, tile.astype(BF16))
    height = wide.shape[0]
    same = iota((height, width), 0) % rows == iota((height, width), 1) // rank
    wide = jnp.where(same, wide, 0.0).astype(BF16)
    product = dot(wide, spatial_ref[...])
    half = height // 2
    mid_col = product.shape[1] // 2
    image_ref[:, :mid_col] = (product[:half, :mid_col] - product[half:, mid_col:]).astype(BF16)
    image_ref[:, mid_col:] = (product[:half, mid_col:] + product[half:, :mid_col]).astype(BF16)


def image_block_kernel(total, rows, rank, factors_ref, spatial_ref, image_ref, wide, held, sems):
    groups, per, lanes = factors_ref.shape
    width = rows * rank
    half = total * rows
    source = iota((lanes, 2 * width), 1)
    source = source // width * rank + source % rank
    tile = jnp.where(iota((lanes, 2 * width), 0) == source, 1.0, 0.0).astype(BF16)
    same = iota((rows, width), 0) == iota((rows, width), 1) // rank
    factors = factors_ref[...].astype(F32)
    for t in range(per):
        lines = dot(factors[:, t].astype(BF16), tile)
        for group in range(groups):
            for part in range(2):
                line = lines[group : group + 1, part * width : (part + 1) * width]
                at = part * half + (group * per + t) * rows
                wide[at : at + rows] = jnp.where(same, line, 0.0).astype(BF16)
    spatial = spatial_ref[...]
    mid = spatial.shape[1] // 2
    copies = []
    for piece in range(2):
        place = slice(piece * half // 2, (piece + 1) * half // 2)
        real = dot(wide[place], spatial)
        imag = dot(wide[half + place.start : half + place.stop], spatial)
        held[place, :mid] = (real[:, :mid] - imag[:, mid:]).astype(BF16)
        held[place, mid:] = (real[:, mid:] + imag[:, :mid]).astype(BF16)
        copies.append(pltpu.make_async_copy(held.at[place], image_ref.at[place], sems.at[piece]))
        copies[-1].start()
    for copy in copies:
        copy.wait()


def image_rows(total, rows, rank, factors, spatial):
    shape = (total * rows, spatial.shape[1])
    if rows % 16:
        body, outs, space, scratch = image_kernel, pltpu.VMEM(shape, BF16), VMEM, []
    else:
        body, outs, space = image_block_kernel, pltpu.HBM(shape, BF16), HBM
        scratch = [
            pltpu.VMEM((2 * total * rows, rows * rank), BF16),
            pltpu.VMEM(shape, BF16),
            pltpu.SemaphoreType.DMA((2,)),
        ]
    return pl.pallas_call(
        functools.partial(body, total, rows, rank),
        in_specs=[VMEM, VMEM],
        out_specs=space,
        out_shape=outs,
        scratch_shapes=scratch,
        compiler_params=grant(12),
        name="image_rows",
    )(local(factors), spatial)


def both_parts(grad):
    half = grad.shape[1] // 2
    turned = jnp.concatenate([grad[:, half:], -grad[:, :half]], 1)
    return jnp.concatenate([grad, turned], 0)


def spatial_kernel(total, rows, rank, factors_ref, grad_ref, out_ref):
    mid = spread(factors_ref, total, rows, rank)
    lanes = mid.shape[1]
    width = rows * rank
    tile = jnp.where(iota((width, lanes), 0) % rank == iota((width, lanes), 1) % rank, 1.0, 0.0)
    wide = dot_t(tile.astype(BF16), mid)
    height = mid.shape[0]
    same = iota((width, height), 1) % rows == iota((width, height), 0) // rank
    wide = jnp.where(same, wide, 0.0).astype(BF16)
    out_ref[...] = dot(wide, both_parts(grad_ref[...]))


def temporal_kernel(total, rows, rank, spatial_ref, grad_ref, out_ref):
    product = dot_t(both_parts(grad_ref[...]), spatial_ref[...])
    height, width = product.shape
    same = iota((height, width), 0) % rows == iota((height, width), 1) // rank
    product = jnp.where(same, product, 0.0)
    lanes = 128
    fold = product[:, :lanes]
    for start in range(lanes, width, lanes):
        fold = fold + product[:, start : start + lanes]
    if rows % 8 == 0:
        fold = jnp.sum(fold.reshape(2 * total, rows, lanes), axis=1)
    else:
        pick = iota((2 * total, height), 0) == iota((2 * total, height), 1) // rows
        fold = jnp.dot(
            jnp.where(pick, 1.0, 0.0), fold, precision=lax.Precision.HIGHEST, preferred_element_type=F32
        )
    shift = lanes // 2
    while shift >= rank:
        fold = fold + pltpu.roll(fold, shift, 1)
        shift //= 2
    lane = iota((total, lanes), 1)
    both = jnp.where(lane // rank % 2 == 0, fold[:total], fold[total:])
    groups, _, span = out_ref.shape
    per = span // (2 * rank)
    copies = groups * per // total
    place = iota((1, span), 1) // (2 * rank)
    for group in range(groups // copies):
        line = both[group * per : group * per + 1, :span]
        for t in range(1, per):
            line = jnp.where(place == t, both[group * per + t : group * per + t + 1, :span], line)
        for copy in range(copies):
            out_ref[group * copies + copy] = line


def sum_kernel(parts_ref, out_ref):
    line = jnp.sum(parts_ref[...], axis=0)
    per, span = out_ref.shape
    for t in range(per):
        out_ref[t : t + 1, :] = line[:, t * span : (t + 1) * span]


def conj_sum(adjoint, sens_r, sens_i):
    half = sens_r.shape[-1]
    back_r, back_i = adjoint[..., :half], adjoint[..., half:]
    return (
        jnp.sum(sens_r * back_r + sens_i * back_i, axis=0),
        jnp.sum(sens_r * back_i - sens_i * back_r, axis=0),
    )


def data_plan(rows, tile):
    own = [(1, at, tile) for at in range(0, rows // 2, tile)]
    return own + [(0, 0, tile), (1, rows // 2, rows // 2), (0, tile, rows - tile)]


def data_kernel(plan, starts_ref, sampled_ref, block_ref, spatial_ref, kspace_ref, sens_ref,
                other_ref, own_ref, spatial_out, mask, block, back, sems, *held):
    frames, coils, _, width = kspace_ref.shape
    _, _, per, _ = own_ref.shape
    half = width // 2
    pieces = [held[4 * k : 4 * k + 4] for k in range(len(plan))]

    def begin(step):
        if step < len(plan):
            for copy in fetch(step):
                copy.start()

    def fetch(step):
        part, at, size = plan[step]
        kspace_held, sens_held, kspace_sem, sens_sem = pieces[step]
        place = pl.ds(pl.multiple_of(starts_ref[part] + at, plan[0][2]), size)
        return (
            pltpu.make_async_copy(sens_ref.at[:, place], sens_held, sens_sem),
            pltpu.make_async_copy(kspace_ref.at[:, :, place], kspace_held, kspace_sem),
        )

    tables = [
        pltpu.make_async_copy(sampled_ref, mask, sems.at[0]),
        pltpu.make_async_copy(block_ref, block, sems.at[1]),
    ]
    staging = [pltpu.make_async_copy(spatial_ref, spatial_out, sems.at[2])]
    for copy in tables:
        copy.start()
    begin(0)
    for copy in tables:
        copy.wait()
    begin(1)
    for t in range(frames):
        keep = mask[t : t + 1, :].astype(F32)
        cosine = (block[:, :half].astype(F32) * keep).astype(BF16).T
        sine_part = (block[:, half:].astype(F32) * keep).astype(BF16).T
        back[t, :half, :half] = cosine
        back[t, :half, half:] = -sine_part
        back[t, half:, :half] = sine_part
        back[t, half:, half:] = cosine
    for step, (part, at, size) in enumerate(plan):
        begin(step + 2)
        if step == 1:
            for copy in staging:
                copy.start()
        for copy in fetch(step):
            copy.wait()
        kspace_held, sens_held = pieces[step][:2]
        sens = sens_held[...].astype(F32)
        sens_r, sens_i = sens[..., :half], sens[..., half:]
        out_ref = own_ref if part else other_ref
        group = slice(at // per, (at + size) // per)
        for t in range(frames):
            adjoint = dot(kspace_held[t].reshape(coils * size, width), back[t])
            real, imag = conj_sum(adjoint.reshape(coils, size, width), sens_r, sens_i)
            out_ref[group, t, :, :half] = real.reshape(size // per, per, half)
            out_ref[group, t, :, half:] = imag.reshape(size // per, per, half)
    for copy in staging:
        copy.wait()


def normal_kernel(starts_ref, message_ref, own_ref, other_ref, sens_ref, left_ref, right_ref, picks_ref,
                  own_out, other_out, masks, table, wide, held, sems):
    groups, per, _ = message_ref.shape
    _, coils, rows, width = held.shape
    copies = []
    for part in range(2):
        place = pl.ds(pl.multiple_of(starts_ref[2 + part], rows), rows)
        copies.append(pltpu.make_async_copy(sens_ref.at[:, place], held.at[part], sems.at[part]))
        copies[part].start()
    half = width // 2
    quarter = half // 2
    message = message_ref[...].astype(F32)
    for t in range(per):
        masks[t] = dot(message[:, t, :half].astype(BF16), picks_ref[...])

    @pl.loop(0, groups)
    def _(group):
        for t in range(per):
            keep = masks[t, pl.ds(group, 1), :]
            for k in range(2):
                lines = keep[:, k * quarter : (k + 1) * quarter]
                left = (left_ref[k].astype(F32) * jnp.concatenate([lines, lines], 1)).astype(BF16)
                near = dot(left, right_ref[k]).astype(BF16)
                table[group, t, k, :quarter] = near
                table[group, t, k, quarter:, :quarter] = -near[:, quarter:]
                table[group, t, k, quarter:, quarter:] = near[:, :quarter]

    for copy in copies:
        copy.wait()
    wide[...] = held[...].astype(F32)

    @pl.loop(0, groups)
    def _(group):
        for t in range(per):
            place = pl.ds(pl.multiple_of((group * per + t) * rows, rows), rows)
            plus, minus = [], []
            for part, image_ref in enumerate((own_ref, other_ref)):
                image = image_ref[place, :].astype(F32)
                image_r, image_i = image[:, :half], image[:, half:]
                sens_r, sens_i = wide[part, :, :, :half], wide[part, :, :, half:]
                coil_r = sens_r * image_r - sens_i * image_i
                coil_i = sens_r * image_i + sens_i * image_r
                low_r, high_r = coil_r[..., :quarter], coil_r[..., quarter:]
                low_i, high_i = coil_i[..., :quarter], coil_i[..., quarter:]
                shape = (coils * rows, half)
                plus.append(jnp.concatenate([low_r + high_r, low_i + high_i], -1).astype(BF16).reshape(shape))
                minus.append(jnp.concatenate([low_r - high_r, low_i - high_i], -1).astype(BF16).reshape(shape))
            shape = (2, coils, rows, half)
            plus = dot(jnp.concatenate(plus, 0), table[group, t, 0]).reshape(shape)
            minus = dot(jnp.concatenate(minus, 0), table[group, t, 1]).reshape(shape)
            for k, both in enumerate((plus + minus, plus - minus)):
                low = slice(k * quarter, (k + 1) * quarter)
                high = slice(half + k * quarter, half + (k + 1) * quarter)
                for part, out_ref in enumerate((own_out, other_out)):
                    real, imag = conj_sum(both[part], wide[part, :, :, low], wide[part, :, :, high])
                    out_ref[place, low] = real
                    out_ref[place, high] = imag


def normal_plain(message, images, sens, left, right):
    half = left.shape[2]
    quarter = half // 2
    flat = message.reshape(-1, message.shape[-1])[:, :half]
    frames = flat.shape[0]
    outs = []
    for image, own in zip(images, sens):
        image = image.reshape(frames, 1, -1, 2 * half).astype(F32)
        own = own.astype(F32)[None]
        coil_r = own[..., :half] * image[..., :half] - own[..., half:] * image[..., half:]
        coil_i = own[..., :half] * image[..., half:] + own[..., half:] * image[..., :half]
        low = [coil_r[..., :quarter], coil_i[..., :quarter]]
        high = [coil_r[..., quarter:], coil_i[..., quarter:]]
        sums = []
        for k, sign in enumerate((1, -1)):
            lines = flat[:, k::2]
            keep = jnp.concatenate([lines, lines], 1)
            near = jnp.einsum("yk,tk,kz->tyz", left[k], keep, right[k], preferred_element_type=F32)
            turned = jnp.concatenate([-near[..., quarter:], near[..., :quarter]], -1)
            table = jnp.concatenate([near, turned], 1).astype(BF16)
            mixed = jnp.concatenate([a + sign * b for a, b in zip(low, high)], -1).astype(BF16)
            sums.append(jnp.einsum("tcxy,tyz->tcxz", mixed, table, preferred_element_type=F32))
        both = [sums[0] + sums[1], sums[0] - sums[1]]
        real = jnp.concatenate([b[..., :quarter] for b in both], -1)
        imag = jnp.concatenate([b[..., quarter:] for b in both], -1)
        out_r = jnp.sum(own[..., :half] * real + own[..., half:] * imag, 1)
        out_i = jnp.sum(own[..., :half] * imag - own[..., half:] * real, 1)
        outs.append(jnp.concatenate([out_r, out_i], -1).reshape(-1, 2 * half))
    return outs


def cost(flops, moved):
    return pl.CostEstimate(flops=int(flops), bytes_accessed=int(moved), transcendentals=0)


VMEM = pl.BlockSpec(memory_space=pltpu.VMEM)
SMEM = pl.BlockSpec(memory_space=pltpu.SMEM)
HBM = pl.BlockSpec(memory_space=pltpu.HBM)
MIB = 1 << 20


def local(array):
    return pltpu.with_memory_space_constraint(array, pltpu.VMEM)


def remote(array):
    return pltpu.with_memory_space_constraint(array, pltpu.HBM)


def grant(mib):
    return pltpu.CompilerParams(vmem_limit_bytes=mib * MIB)


def data_term(starts, sampled, block, spatial, kspace, sens, per):
    frames, coils, rows, width = kspace.shape
    own = (rows // 2 // per, frames, per, width)
    plan = data_plan(rows // 2, 32)
    scratch = [
        pltpu.VMEM(sampled.shape, jnp.int32),
        pltpu.VMEM(block.shape, BF16),
        pltpu.VMEM((frames, width, width), BF16),
        pltpu.SemaphoreType.DMA((3,)),
    ]
    for _, _, size in plan:
        scratch += [
            pltpu.VMEM((frames, coils, size, width), BF16),
            pltpu.VMEM((coils, size, width), BF16),
            pltpu.SemaphoreType.DMA,
            pltpu.SemaphoreType.DMA,
        ]
    return pl.pallas_call(
        functools.partial(data_kernel, plan),
        in_specs=[SMEM] + [HBM] * 5,
        out_specs=[VMEM] * 3,
        out_shape=[
            pltpu.VMEM(own, F32),
            pltpu.VMEM(own, F32),
            pltpu.VMEM(spatial.shape, BF16),
        ],
        scratch_shapes=scratch,
        cost_estimate=cost(2 * frames * coils * rows * width * width, 2 * kspace.size),
        compiler_params=grant(44),
        name="data_term",
    )(starts, remote(sampled), remote(block), remote(spatial), remote(kspace), remote(sens))


def normal_term(starts, message, own, other, sens, left, right, picks):
    groups, per, _ = message.shape
    coils, _, width = sens.shape
    rows = own.shape[0] // (groups * per)
    half = width // 2
    return pl.pallas_call(
        normal_kernel,
        in_specs=[SMEM] + [VMEM] * 3 + [HBM] + [VMEM] * 3,
        out_specs=[VMEM] * 2,
        out_shape=[pltpu.VMEM(own.shape, F32)] * 2,
        scratch_shapes=[
            pltpu.VMEM((per, groups, half), F32),
            pltpu.VMEM((groups, per, 2, half, half), BF16),
            pltpu.VMEM((2, coils, rows, width), F32),
            pltpu.VMEM((2, coils, rows, width), BF16),
            pltpu.SemaphoreType.DMA((2,)),
        ],
        cost_estimate=cost(2 * groups * per * coils * rows * width * width, 4 * own.size),
        compiler_params=grant(40),
        name="normal_term",
    )(starts, message, local(own), local(other), remote(sens), local(left), local(right), local(picks))


def on_device(frame_size, coil_size, spatial, temporal, kspace, sampled, sensitivity):
    rows, rank, width = spatial.shape
    per = temporal.shape[0]
    total = per * frame_size
    half_rows = rows * frame_size
    half = width // 2
    swap = [(i, (i + 1) % coil_size) for i in range(coil_size)]
    own = lax.axis_index("coil") * half_rows
    other = (own + half_rows) % (coil_size * half_rows)
    row = lax.axis_index("frame") * rows
    starts = jnp.stack([other, own, own + row, other + row])
    spatial2 = spatial.reshape(rows * rank, width)
    block, left, right, picks = [jnp.asarray(table) for table in dft_tables(half)]

    message = jnp.concatenate([sampled.astype(BF16), temporal], 1)
    message = lax.all_to_all(
        jnp.broadcast_to(message[None], (frame_size, *message.shape)), "frame", 0, 0, tiled=True
    )
    regroup = rows % 16 != 0
    data_other, data_own, near = data_term(
        starts, sampled, block, spatial2, kspace, sensitivity, 16 if regroup else rows
    )
    message, data_other = lax.optimization_barrier((message, data_other))
    received = lax.ppermute(data_other, "coil", swap)
    image = image_rows(total, rows, rank, message[:, :, half:], near)
    image_other = lax.ppermute(image, "coil", swap)
    data = (data_own + received).astype(BF16)
    if regroup:
        data = data.transpose(1, 0, 2, 3).reshape(per, frame_size, rows, width).transpose(1, 0, 2, 3)
    image, image_other, data = lax.optimization_barrier((image, image_other, data))
    data = lax.all_to_all(data, "frame", 0, 0, tiled=True)
    data = data.reshape(total * rows, width)
    if regroup:
        sens = [lax.dynamic_slice_in_dim(sensitivity, at + row, rows, 1) for at in (own, other)]
        keep_own, send = normal_plain(message, (image, image_other), sens, left, right)
    else:
        keep_own, send = normal_term(starts, message, image, image_other, sensitivity, left, right, picks)
    grad = (keep_own + lax.ppermute(send, "coil", swap) - data.astype(F32)).astype(BF16)
    grad = local(grad)

    partial = pl.pallas_call(
        functools.partial(temporal_kernel, total, rows, rank),
        in_specs=[VMEM, VMEM],
        out_specs=VMEM,
        out_shape=pltpu.VMEM((frame_size * coil_size, 1, per * 2 * rank), F32),
        compiler_params=grant(12),
        name="temporal_rows",
    )(local(spatial2), grad)
    partial = lax.all_to_all(partial, ("frame", "coil"), 0, 0, tiled=True)
    spatial_grad = pl.pallas_call(
        functools.partial(spatial_kernel, total, rows, rank),
        in_specs=[VMEM, VMEM],
        out_specs=VMEM,
        out_shape=jax.ShapeDtypeStruct((rows * rank, width), F32),
        compiler_params=grant(12),
        name="spatial_rows",
    )(local(message[:, :, half:]), grad)
    temporal_grad = pl.pallas_call(
        sum_kernel,
        in_specs=[VMEM],
        out_specs=VMEM,
        out_shape=jax.ShapeDtypeStruct((per, 2 * rank), F32),
        compiler_params=grant(2),
        name="temporal_sum",
    )(partial)
    return (spatial_grad.reshape(rows, rank, width), temporal_grad)


def solution(mesh):
    placed = (
        P(("cuts", "coil", "frame"), None, None),
        P(("cuts", "frame"), None),
        P(("cuts", "frame"), "coil", None, None),
        P(("cuts", "frame"), None),
        P(("cuts", "coil"), None, None),
    )

    def body(*arrays):
        return on_device(mesh.shape["frame"], mesh.shape["coil"], *arrays)

    return jax.shard_map(
        body,
        mesh=mesh,
        in_specs=placed,
        out_specs=(P(("cuts", "coil", "frame"), None, None), P(("cuts", "frame"), None)),
        check_vma=False,
    )
```

time: 63.7 us -> 58.8 us (0.923)
  waiting for transfers between devices: 9.47 us -> 5.94 us
  starting transfers between devices: 15 us -> 12.1 us
  other arithmetic: 0.26 us -> 1.68 us
  Pallas kernels: 22.3 us -> 21.5 us
  blocking collectives: 14.2 us -> 15 us
    all_to_all x2 -> x1, waiting for transfers between devices: 4.79 us -> 0.01 us  [on_device(): lax.all_to_all(jnp.broadcast_to(message[None], (frame_size, *message.shap...]
    all_to_all x2 -> x1, starting transfers between devices: 10.7 us -> 7.31 us  [on_device(): lax.all_to_all(jnp.broadcast_to(message[None], (frame_size, *message.shap...]
    ppermute x1, waiting for transfers between devices: 0.01 us -> 1.2 us  [on_device(): image_other = lax.ppermute(image, 'coil', swap)]
    unnamed x4 -> x10, local copies, waits for them, and re-layouts: 0.01 us -> 0.96 us
    pallas_call x5 -> x2, Pallas kernels: 17.5 us -> 16.7 us  [the longest x1 8.46 us: normal_term(): pl.pallas_call(normal_kernel, in_specs=[SMEM] + [VMEM] * 3 + [HBM] + [VME...]
    all_to_all x1, blocking collectives: 14.2 us -> 15 us  [on_device(): data = lax.all_to_all(data, 'frame', 0, 0, tiled=True)]
    convert_element_type x1 -> x3, other arithmetic: 0.19 us -> 0.94 us  [the longest x1 0.69 us: on_device(): message = jnp.concatenate([sampled.astype(BF16), temporal], 1)]
    concatenate x0 -> x1, other arithmetic: none -> 0.66 us  [on_device(): message = jnp.concatenate([sampled.astype(BF16), temporal], 1)]
  transfers between devices with their start and end apart: 5 -> 5, of which waited for: 3 -> 3; matrix products, arithmetic and copies ran while one was open for 0% -> 0% of each run, Pallas kernels for 25% -> 19%
where the time goes in v9:
time: 58.8 us; the launch traced here: 58.5 us
  Pallas kernels  21.5 us (37%)
  blocking collectives  15 us (26%)
  starting transfers between devices  12.1 us (21%)
  waiting for transfers between devices  5.94 us (10%)
  other arithmetic  1.68 us (3%)
  local copies, waits for them, and re-layouts  1.58 us (3%)
  between operations  0.72 us (1%)
    all_to_all x1, blocking collectives, on_device(): data = lax.all_to_all(data, 'frame', 0, 0, tiled=True)  15 us
    pallas_call x1, Pallas kernels, normal_term(): pl.pallas_call(normal_kernel, in_specs=[SMEM] + [VMEM] * 3 + [HBM] + [VME...  8.46 us
    pallas_call x1, Pallas kernels, data_term(): pl.pallas_call(functools.partial(data_kernel, plan), in_specs=[SMEM] + [H...  8.19 us
    all_to_all x1, starting transfers between devices, on_device(): lax.all_to_all(jnp.broadcast_to(message[None], (frame_size, *message.shap...  7.31 us
    all_to_all x1, waiting for transfers between devices, on_device(): partial = lax.all_to_all(partial, ('frame', 'coil'), 0, 0, tiled=True)  4.67 us
    all_to_all x1, starting transfers between devices, on_device(): partial = lax.all_to_all(partial, ('frame', 'coil'), 0, 0, tiled=True)  3.69 us
    pallas_call x1, Pallas kernels, on_device(): pl.pallas_call(functools.partial(spatial_kernel, total, rows, rank), in_s...  1.75 us
    pallas_call x1, Pallas kernels, image_rows(): pl.pallas_call(functools.partial(body, total, rows, rank), in_specs=[VMEM...  1.25 us
  transfers between devices with their start and end apart: 5, of which 3 were waited for; matrix products, arithmetic and copies ran while one was open for 0% of the time, Pallas kernels for 19%

profile of v9, /device:TPU:0, one launch (start us, length us, event | category | flops | bytes accessed | tf_op | source)
XLA Modules:
  0.0 58.5 jit_solution(4908585014843028156)
XLA Ops:
  0.6 0.7 %convert_element_type.15 = bf16[2,256]{1,0:T(2,128)(2,1)S(1)} convert(s32[2,256]{1,0:T(2,128)} %sampled_ref.1) | non-fusion elementwise | flops 512 | bytes 3072 | tf_op jit(solution)/shard_map/convert_element_type | solution.py:445
  1.3 0.7 %pad_maximum_fusion = bf16[2,320]{1,0:T(2,128)(2,1)S(1)} fusion(bf16[2,64]{1,0:T(2,128)(2,1)} %param.10, bf16[2,256]{1,0:T(2,128)(2,1)S(1)} %convert_element_type.15), kind=kLoop, calls=%fused_computation.3 | loop fusion | flops 2560 | bytes 2560 | tf_op jit(solution)/shard_map/concatenate | solution.py:445
  2.0 0.6 %broadcast_in_dim.2 = bf16[8,2,320]{2,1,0:T(2,128)(2,1)} broadcast(bf16[2,320]{1,0:T(2,128)(2,1)S(1)} %pad_maximum_fusion), dimensions={1,2} | broadcast | bytes 11520 | tf_op jit(solution)/shard_map/broadcast_in_dim | solution.py:447
  2.6 7.3 %all-to-all-start = ((bf16[8,2,320]{2,1,0:T(2,128)(2,1)}), bf16[8,2,320]{2,1,0:T(2,128)(2,1)S(1)}, u32[]{:S(2)}, u32[]{:S(2)}) async-start(bf16[8,2,320]{2,1,0:T(2,128)(2,1)} %broadcast_in_dim.2), calls=%async_computation | async-start | bytes 24576 | tf_op jit(solution)/shard_map/all_to_all | solution.py:446
  9.9 0.1 pad_add_fusion.starts_ref
  10.0 0.0 copy-start.2
  10.0 0.0 copy-start.3
  10.0 0.0 copy-start.4
  10.0 8.2 %data_term.1 = (f32[8,2,16,512]{3,2,1,0:T(8,128)S(1)}, f32[8,2,16,512]{3,2,1,0:T(8,128)S(1)}, bf16[512,512]{1,0:T(8,128)(2,1)S(1)}) custom-call(s32[4]{0:T(128)S(1)} %pad_add_fusion.starts_ref, s32[2,256]{1,0:T(2,128)} %sampled_ref.1, bf16[256,512]{1,0:T(8,128)(2,1)} %constant.33.clone.block_ref, bf16[512,512]{1,0:T(8,128)(2,1)} %bitcast.9, ...), custom_call_target="tpu_custom_call" | custom-call | flops 4294967296 | bytes 8388608 | tf_op jit(solution)/shard_map/data_term/pallas_call | solution.py:392
  18.2 0.0 copy-start
  18.2 0.0 all-to-all-done.message_ref
  18.2 0.1 collective-permute-start.1
  18.3 1.2 %image_rows.1.own_ref = bf16[256,512]{1,0:T(8,128)(2,1)} custom-call(bf16[8,2,64]{2,1,0:T(2,128)(2,1)S(1)} %slice.4.factors_ref, bf16[512,512]{1,0:T(8,128)(2,1)S(1)} %get-tuple-element.14.spatial_ref), custom_call_target="tpu_custom_call" | custom-call | tf_op jit(solution)/shard_map/image_rows/pallas_call | solution.py:118
  19.6 0.6 collective-permute-start
  20.1 0.1 collective-permute-done.1
  20.2 0.1 add_convert_fusion
  20.3 1.2 %collective-permute-done.other_ref = bf16[256,512]{1,0:T(8,128)(2,1)S(1)} collective-permute-done((bf16[256,512]{1,0:T(8,128)(2,1)}, bf16[256,512]{1,0:T(8,128)(2,1)S(1)}, u32[]{:S(2)}, u32[]{:S(2)}) %collective-permute-start) | collective-permute-done | bytes 262176 | tf_op jit(solution)/shard_map/ppermute | solution.py:456
  21.5 0.0 copy-done.2
  21.5 0.0 copy-done.3
  21.5 0.0 copy-done.4
  21.5 0.9 %copy-done.1 = bf16[256,512]{1,0:T(8,128)(2,1)S(1)} copy-done((bf16[256,512]{1,0:T(8,128)(2,1)S(1)}, bf16[256,512]{1,0:T(8,128)(2,1)}, u32[]{:S(2)}) %copy-start.1) | copy-done | bytes 262168
  22.5 8.5 %normal_term.1 = (f32[256,512]{1,0:T(8,128)S(1)}, f32[256,512]{1,0:T(8,128)S(1)}) custom-call(s32[4]{0:T(128)S(1)} %pad_add_fusion.starts_ref, bf16[8,2,320]{2,1,0:T(2,128)(2,1)S(1)} %all-to-all-done.message_ref, bf16[256,512]{1,0:T(8,128)(2,1)S(1)} %copy-done.1, bf16[256,512]{1,0:T(8,128)(2,1)S(1)} %collective-permute-done.other_ref, ...), custom_call_target="tpu_custom_call" | custom-call | flops 2147483648 | bytes 524288 | tf_op jit(solution)/shard_map/normal_term/pallas_call | solution.py:413
  30.9 0.4 collective-permute-start.2
  31.4 15.0 %all_to_all.15 = bf16[8,2,16,512]{3,2,1,0:T(8,128)(2,1)S(1)} all-to-all(bf16[8,2,16,512]{3,2,1,0:T(8,128)(2,1)S(1)} %add_convert_fusion), channel_id=1, replica_groups=mesh['cuts'=2,'frame'=8,'coil'=2] {'frame'}, dimensions={0} | all-to-all | bytes 524288 | tf_op jit(solution)/shard_map/all_to_all | solution.py:461
  46.4 0.0 collective-permute-done.2
  46.4 0.2 fusion.grad_ref
  46.5 0.0 copy-done
  46.5 1.2 %temporal_rows.1 = f32[16,1,128]{2,1,0:T(1,128)} custom-call(bf16[512,512]{1,0:T(8,128)(2,1)S(1)} %bitcast.10, bf16[256,512]{1,0:T(8,128)(2,1)S(1)} %fusion.grad_ref), custom_call_target="tpu_custom_call" | custom-call | tf_op jit(solution)/shard_map/temporal_rows/pallas_call | solution.py:471
  47.7 3.7 %all-to-all-start.2 = ((f32[16,1,128]{2,1,0:T(1,128)}), f32[16,1,128]{2,1,0:T(1,128)S(1)}, u32[]{:S(2)}, u32[]{:S(2)}) async-start(f32[16,1,128]{2,1,0:T(1,128)} %temporal_rows.1), calls=%async_computation.2 | async-start | bytes 16384 | tf_op jit(solution)/shard_map/all_to_all | solution.py:479
  51.4 1.7 %spatial_rows.1 = f32[512,512]{1,0:T(8,128)} custom-call(bf16[8,2,64]{2,1,0:T(2,128)(2,1)S(1)} %slice.4.factors_ref, bf16[256,512]{1,0:T(8,128)(2,1)S(1)} %fusion.grad_ref), custom_call_target="tpu_custom_call" | custom-call | tf_op jit(solution)/shard_map/spatial_rows/pallas_call | solution.py:480
  53.2 4.7 %all-to-all-done.2.parts_ref = f32[16,1,128]{2,1,0:T(1,128)S(1)} async-done(((f32[16,1,128]{2,1,0:T(1,128)}), f32[16,1,128]{2,1,0:T(1,128)S(1)}, u32[]{:S(2)}, u32[]{:S(2)}) %all-to-all-start.2) | async-done | bytes 8224 | tf_op jit(solution)/shard_map/all_to_all | solution.py:479
  57.9 0.6 %temporal_sum.1 = f32[2,64]{1,0:T(2,128)} custom-call(f32[16,1,128]{2,1,0:T(1,128)S(1)} %all-to-all-done.2.parts_ref), custom_call_target="tpu_custom_call" | custom-call | tf_op jit(solution)/shard_map/temporal_sum/pallas_call | solution.py:488
  (2 shorter events, 0.0 us)
Async XLA Ops:
  2.6 15.6 %all-to-all-start = ((bf16[8,2,320]{2,1,0:T(2,128)(2,1)}), bf16[8,2,320]{2,1,0:T(2,128)(2,1)S(1)}, u32[]{:S(2)}, u32[]{:S(2)}) async-start(bf16[8,2,320]{2,1,0:T(2,128)(2,1)} %broadcast_in_dim.2), calls=%async_computation | async-start | bytes 24576 | tf_op jit(solution)/shard_map/all_to_all | solution.py:446
  10.0 11.5 %copy-start.2 = (bf16[2,256,256]{2,1,0:T(8,128)(2,1)S(1)}, bf16[2,256,256]{2,1,0:T(8,128)(2,1)}, u32[]{:S(2)}) copy-start(bf16[2,256,256]{2,1,0:T(8,128)(2,1)} %constant.35.clone.right_ref) | copy-start | bytes 786436
  10.0 11.5 %copy-start.3 = (bf16[2,128,256]{2,1,0:T(8,128)(2,1)S(1)}, bf16[2,128,256]{2,1,0:T(8,128)(2,1)}, u32[]{:S(2)}) copy-start(bf16[2,128,256]{2,1,0:T(8,128)(2,1)} %constant.34.clone.left_ref) | copy-start | bytes 393220
  10.0 11.5 %copy-start.4 = (bf16[256,256]{1,0:T(8,128)(2,1)S(1)}, bf16[256,256]{1,0:T(8,128)(2,1)}, u32[]{:S(2)}) copy-start(bf16[256,256]{1,0:T(8,128)(2,1)} %constant.36.clone.picks_ref) | copy-start | bytes 393220
  18.2 28.3 %copy-start = (bf16[16,32,512]{2,1,0:T(8,128)(2,1)S(1)}, bf16[16,32,512]{2,1,0:T(8,128)(2,1)}, u32[]{:S(2)}) copy-start(bf16[16,32,512]{2,1,0:T(8,128)(2,1)} %param.9) | copy-start | bytes 1572868
  18.2 2.0 %collective-permute-start.1 = (f32[8,2,16,512]{3,2,1,0:T(8,128)S(1)}, f32[8,2,16,512]{3,2,1,0:T(8,128)S(1)}, u32[]{:S(2)}, u32[]{:S(2)}) collective-permute-start(f32[8,2,16,512]{3,2,1,0:T(8,128)S(1)} %get-tuple-element.16), channel_id=1, source_target_pairs={{0,1},{1,0},{2,3},{3,2},{4,5},{5,4},{6,7},{7,6},{8,9},{9,8},{10,11... | collective-permute-start | bytes 1572872 | tf_op jit(solution)/shard_map/ppermute | solution.py:454
  19.6 1.9 %collective-permute-start = (bf16[256,512]{1,0:T(8,128)(2,1)}, bf16[256,512]{1,0:T(8,128)(2,1)S(1)}, u32[]{:S(2)}, u32[]{:S(2)}) collective-permute-start(bf16[256,512]{1,0:T(8,128)(2,1)} %image_rows.1.own_ref), channel_id=1, source_target_pairs={{0,1},{1,0},{2,3},{3,2},{4,5},{5,4},{6,7},{7,6},{8,9},{9,8},{10,11... | collective-permute-start | bytes 786440 | tf_op jit(solution)/shard_map/ppermute | solution.py:456
  21.5 1.0 %copy-start.1 = (bf16[256,512]{1,0:T(8,128)(2,1)S(1)}, bf16[256,512]{1,0:T(8,128)(2,1)}, u32[]{:S(2)}) copy-start(bf16[256,512]{1,0:T(8,128)(2,1)} %image_rows.1.own_ref) | copy-start | bytes 786436
  30.9 15.4 %collective-permute-start.2 = (f32[256,512]{1,0:T(8,128)S(1)}, f32[256,512]{1,0:T(8,128)S(1)}, u32[]{:S(2)}, u32[]{:S(2)}) collective-permute-start(f32[256,512]{1,0:T(8,128)S(1)} %get-tuple-element.20), channel_id=1, source_target_pairs={{0,1},{1,0},{2,3},{3,2},{4,5},{5,4},{6,7},{7,6},{8,9},{9,8},{10,11... | collective-permute-start | bytes 1572872 | tf_op jit(solution)/shard_map/ppermute | solution.py:468
  47.7 10.1 %all-to-all-start.2 = ((f32[16,1,128]{2,1,0:T(1,128)}), f32[16,1,128]{2,1,0:T(1,128)S(1)}, u32[]{:S(2)}, u32[]{:S(2)}) async-start(f32[16,1,128]{2,1,0:T(1,128)} %temporal_rows.1), calls=%async_computation.2 | async-start | bytes 16384 | tf_op jit(solution)/shard_map/all_to_all | solution.py:479

commit v10 on v9

--- a/solution.py
+++ b/solution.py
@@ -73,7 +73,7 @@
     image_ref[:, mid_col:] = (product[:half, mid_col:] + product[half:, :mid_col]).astype(BF16)
 
 
-def image_block_kernel(total, rows, rank, factors_ref, spatial_ref, image_ref, wide, held, sems):
+def image_block_kernel(total, rows, rank, factors_ref, spatial_ref, image_ref, wide):
     groups, per, lanes = factors_ref.shape
     width = rows * rank
     half = total * rows
@@ -91,35 +91,23 @@
                 wide[at : at + rows] = jnp.where(same, line, 0.0).astype(BF16)
     spatial = spatial_ref[...]
     mid = spatial.shape[1] // 2
-    copies = []
-    for piece in range(2):
-        place = slice(piece * half // 2, (piece + 1) * half // 2)
-        real = dot(wide[place], spatial)
-        imag = dot(wide[half + place.start : half + place.stop], spatial)
-        held[place, :mid] = (real[:, :mid] - imag[:, mid:]).astype(BF16)
-        held[place, mid:] = (real[:, mid:] + imag[:, :mid]).astype(BF16)
-        copies.append(pltpu.make_async_copy(held.at[place], image_ref.at[place], sems.at[piece]))
-        copies[-1].start()
-    for copy in copies:
-        copy.wait()
+    real = dot(wide[:half], spatial)
+    imag = dot(wide[half:], spatial)
+    image_ref[:, :mid] = (real[:, :mid] - imag[:, mid:]).astype(BF16)
+    image_ref[:, mid:] = (real[:, mid:] + imag[:, :mid]).astype(BF16)
 
 
 def image_rows(total, rows, rank, factors, spatial):
     shape = (total * rows, spatial.shape[1])
     if rows % 16:
-        body, outs, space, scratch = image_kernel, pltpu.VMEM(shape, BF16), VMEM, []
+        body, scratch = image_kernel, []
     else:
-        body, outs, space = image_block_kernel, pltpu.HBM(shape, BF16), HBM
-        scratch = [
-            pltpu.VMEM((2 * total * rows, rows * rank), BF16),
-            pltpu.VMEM(shape, BF16),
-            pltpu.SemaphoreType.DMA((2,)),
-        ]
+        body, scratch = image_block_kernel, [pltpu.VMEM((2 * total * rows, rows * rank), BF16)]
     return pl.pallas_call(
         functools.partial(body, total, rows, rank),
         in_specs=[VMEM, VMEM],
-        out_specs=space,
-        out_shape=outs,
+        out_specs=VMEM,
+        out_shape=pltpu.VMEM(shape, BF16),
         scratch_shapes=scratch,
         compiler_params=grant(12),
         name="image_rows",
@@ -275,7 +263,7 @@
     for t in range(per):
         masks[t] = dot(message[:, t, :half].astype(BF16), picks_ref[...])
 
-    @pl.loop(0, groups)
+    @pl.loop(0, groups, unroll=4)
     def _(group):
         for t in range(per):
             keep = masks[t, pl.ds(group, 1), :]
@@ -291,7 +279,7 @@
         copy.wait()
     wide[...] = held[...].astype(F32)
 
-    @pl.loop(0, groups)
+    @pl.loop(0, groups, unroll=2)
     def _(group):
         for t in range(per):
             place = pl.ds(pl.multiple_of((group * per + t) * rows, rows), rows)
@@ -442,7 +430,8 @@
     spatial2 = spatial.reshape(rows * rank, width)
     block, left, right, picks = [jnp.asarray(table) for table in dft_tables(half)]
 
-    message = jnp.concatenate([sampled.astype(BF16), temporal], 1)
+    message = jnp.pad(sampled, ((0, 0), (0, 2 * rank))).astype(F32)
+    message = (message + jnp.pad(temporal, ((0, 0), (half, 0))).astype(F32)).astype(BF16)
     message = lax.all_to_all(
         jnp.broadcast_to(message[None], (frame_size, *message.shape)), "frame", 0, 0, tiled=True
     )

time: 58.8 us -> 55.2 us (0.939)
  Pallas kernels: 21.5 us -> 19.7 us
  local copies, waits for them, and re-layouts: 1.58 us -> 0.63 us
  other arithmetic: 1.68 us -> 1.01 us
    pallas_call x1, Pallas kernels: 8.46 us -> 7.37 us  [normal_term(): pl.pallas_call(normal_kernel, in_specs=[SMEM] + [VMEM] * 3 + [HBM] + [VME...]
    unnamed x10 -> x8, local copies, waits for them, and re-layouts: 0.96 us -> 0.02 us
    ppermute x1, waiting for transfers between devices: 1.2 us -> 0.31 us  [on_device(): image_other = lax.ppermute(image, 'coil', swap)]
    ppermute x1, waiting for transfers between devices: 0.06 us -> 0.76 us  [on_device(): received = lax.ppermute(data_other, 'coil', swap)]
    pallas_call x1, Pallas kernels: 1.25 us -> 0.55 us  [image_rows(): pl.pallas_call(functools.partial(body, total, rows, rank), in_specs=[VMEM...]
    concatenate x1 -> x0, other arithmetic: 0.66 us -> none  [on_device(): message = jnp.concatenate([sampled.astype(BF16), temporal], 1)]
where the time goes in v10:
time: 55.2 us; the launch traced here: 54.9 us
  Pallas kernels  19.7 us (36%)
  blocking collectives  15 us (27%)
  starting transfers between devices  12.1 us (22%)
  waiting for transfers between devices  5.75 us (10%)
  other arithmetic  1.01 us (2%)
  between operations  0.72 us (1%)
  local copies, waits for them, and re-layouts  0.63 us (1%)
    all_to_all x1, blocking collectives, on_device(): data = lax.all_to_all(data, 'frame', 0, 0, tiled=True)  15 us
    pallas_call x1, Pallas kernels, data_term(): pl.pallas_call(functools.partial(data_kernel, plan), in_specs=[SMEM] + [H...  8.19 us
    pallas_call x1, Pallas kernels, normal_term(): pl.pallas_call(normal_kernel, in_specs=[SMEM] + [VMEM] * 3 + [HBM] + [VME...  7.37 us
    all_to_all x1, starting transfers between devices, on_device(): lax.all_to_all(jnp.broadcast_to(message[None], (frame_size, *message.shap...  7.31 us
    all_to_all x1, waiting for transfers between devices, on_device(): partial = lax.all_to_all(partial, ('frame', 'coil'), 0, 0, tiled=True)  4.68 us
    all_to_all x1, starting transfers between devices, on_device(): partial = lax.all_to_all(partial, ('frame', 'coil'), 0, 0, tiled=True)  3.69 us
    pallas_call x1, Pallas kernels, on_device(): pl.pallas_call(functools.partial(spatial_kernel, total, rows, rank), in_s...  1.75 us
    pallas_call x1, Pallas kernels, on_device(): pl.pallas_call(functools.partial(temporal_kernel, total, rows, rank), in_...  1.21 us
  transfers between devices with their start and end apart: 5, of which 3 were waited for; matrix products, arithmetic and copies ran while one was open for 0% of the time, Pallas kernels for 19%

profile of v10, /device:TPU:0, one launch (start us, length us, event | category | flops | bytes accessed | tf_op | source)
XLA Modules:
  0.0 54.9 jit_solution(12172483812732777004)
XLA Ops:
  0.6 0.7 %add_convert_fusion.1 = bf16[2,320]{1,0:T(2,128)(2,1)S(1)} fusion(s32[2,256]{1,0:T(2,128)} %sampled_ref.1, bf16[2,64]{1,0:T(2,128)(2,1)} %param.10), kind=kLoop, calls=%fused_computation.3 | loop fusion | flops 2560 | bytes 3584 | tf_op jit(solution)/shard_map/convert_element_type | solution.py:434
  1.3 0.6 %broadcast_in_dim.2 = bf16[8,2,320]{2,1,0:T(2,128)(2,1)} broadcast(bf16[2,320]{1,0:T(2,128)(2,1)S(1)} %add_convert_fusion.1), dimensions={1,2} | broadcast | bytes 11520 | tf_op jit(solution)/shard_map/broadcast_in_dim | solution.py:436
  1.9 7.3 %all-to-all-start = ((bf16[8,2,320]{2,1,0:T(2,128)(2,1)}), bf16[8,2,320]{2,1,0:T(2,128)(2,1)S(1)}, u32[]{:S(2)}, u32[]{:S(2)}) async-start(bf16[8,2,320]{2,1,0:T(2,128)(2,1)} %broadcast_in_dim.2), calls=%async_computation | async-start | bytes 24576 | tf_op jit(solution)/shard_map/all_to_all | solution.py:435
  9.2 0.1 pad_add_fusion.starts_ref
  9.3 0.0 copy-start.1
  9.3 0.0 copy-start.2
  9.3 0.0 copy-start.3
  9.3 8.2 %data_term.1 = (f32[8,2,16,512]{3,2,1,0:T(8,128)S(1)}, f32[8,2,16,512]{3,2,1,0:T(8,128)S(1)}, bf16[512,512]{1,0:T(8,128)(2,1)S(1)}) custom-call(s32[4]{0:T(128)S(1)} %pad_add_fusion.starts_ref, s32[2,256]{1,0:T(2,128)} %sampled_ref.1, bf16[256,512]{1,0:T(8,128)(2,1)} %constant.36.clone.block_ref, bf16[512,512]{1,0:T(8,128)(2,1)} %bitcast.9, ...), custom_call_target="tpu_custom_call" | custom-call | flops 4294967296 | bytes 8388608 | tf_op jit(solution)/shard_map/data_term/pallas_call | solution.py:380
  17.5 0.0 copy-start
  17.5 0.0 all-to-all-done.message_ref
  17.6 0.1 collective-permute-start.1
  17.6 0.6 %image_rows.1.own_ref = bf16[256,512]{1,0:T(8,128)(2,1)S(1)} custom-call(bf16[8,2,64]{2,1,0:T(2,128)(2,1)S(1)} %slice.4.factors_ref, bf16[512,512]{1,0:T(8,128)(2,1)S(1)} %get-tuple-element.14.spatial_ref), custom_call_target="tpu_custom_call" | custom-call | tf_op jit(solution)/shard_map/image_rows/pallas_call | solution.py:106
  18.2 0.6 %collective-permute-start = (bf16[256,512]{1,0:T(8,128)(2,1)S(1)}, bf16[256,512]{1,0:T(8,128)(2,1)S(1)}, u32[]{:S(2)}, u32[]{:S(2)}) collective-permute-start(bf16[256,512]{1,0:T(8,128)(2,1)S(1)} %image_rows.1.own_ref), channel_id=1, source_target_pairs={{0,1},{1,0},{2,3},{3,2},{4,5},{5,4},{6,7},{7,6},{8,9},{9,8},{10,11... | collective-permute-start | bytes 786440 | tf_op jit(solution)/shard_map/ppermute | solution.py:445
  18.8 0.8 %collective-permute-done.1 = f32[8,2,16,512]{3,2,1,0:T(8,128)S(1)} collective-permute-done((f32[8,2,16,512]{3,2,1,0:T(8,128)S(1)}, f32[8,2,16,512]{3,2,1,0:T(8,128)S(1)}, u32[]{:S(2)}, u32[]{:S(2)}) %collective-permute-start.1) | collective-permute-done | bytes 524320 | tf_op jit(solution)/shard_map/ppermute | solution.py:443
  19.5 0.1 add_convert_fusion
  19.6 0.3 collective-permute-done.other_ref
  19.9 0.0 copy-done.1
  19.9 0.0 copy-done.2
  19.9 0.0 copy-done.3
  19.9 7.4 %normal_term.1 = (f32[256,512]{1,0:T(8,128)S(1)}, f32[256,512]{1,0:T(8,128)S(1)}) custom-call(s32[4]{0:T(128)S(1)} %pad_add_fusion.starts_ref, bf16[8,2,320]{2,1,0:T(2,128)(2,1)S(1)} %all-to-all-done.message_ref, bf16[256,512]{1,0:T(8,128)(2,1)S(1)} %image_rows.1.own_ref, bf16[256,512]{1,0:T(8,128)(2,1)S(1)} %collective-permute-done.other_ref, ...), custom_call_target="tpu_custom_call" | custom-call | flops 2147483648 | bytes 524288 | tf_op jit(solution)/shard_map/normal_term/pallas_call | solution.py:401
  27.3 0.5 collective-permute-start.2
  27.8 15.0 %all_to_all.15 = bf16[8,2,16,512]{3,2,1,0:T(8,128)(2,1)S(1)} all-to-all(bf16[8,2,16,512]{3,2,1,0:T(8,128)(2,1)S(1)} %add_convert_fusion), channel_id=1, replica_groups=mesh['cuts'=2,'frame'=8,'coil'=2] {'frame'}, dimensions={0} | all-to-all | bytes 524288 | tf_op jit(solution)/shard_map/all_to_all | solution.py:450
  42.7 0.0 collective-permute-done.2
  42.8 0.2 fusion.grad_ref
  42.9 0.0 copy-done
  42.9 1.2 %temporal_rows.1 = f32[16,1,128]{2,1,0:T(1,128)} custom-call(bf16[512,512]{1,0:T(8,128)(2,1)S(1)} %bitcast.10, bf16[256,512]{1,0:T(8,128)(2,1)S(1)} %fusion.grad_ref), custom_call_target="tpu_custom_call" | custom-call | tf_op jit(solution)/shard_map/temporal_rows/pallas_call | solution.py:460
  44.1 3.7 %all-to-all-start.2 = ((f32[16,1,128]{2,1,0:T(1,128)}), f32[16,1,128]{2,1,0:T(1,128)S(1)}, u32[]{:S(2)}, u32[]{:S(2)}) async-start(f32[16,1,128]{2,1,0:T(1,128)} %temporal_rows.1), calls=%async_computation.2 | async-start | bytes 16384 | tf_op jit(solution)/shard_map/all_to_all | solution.py:468
  47.8 1.7 %spatial_rows.1 = f32[512,512]{1,0:T(8,128)} custom-call(bf16[8,2,64]{2,1,0:T(2,128)(2,1)S(1)} %slice.4.factors_ref, bf16[256,512]{1,0:T(8,128)(2,1)S(1)} %fusion.grad_ref), custom_call_target="tpu_custom_call" | custom-call | tf_op jit(solution)/shard_map/spatial_rows/pallas_call | solution.py:469
  49.6 4.7 %all-to-all-done.2.parts_ref = f32[16,1,128]{2,1,0:T(1,128)S(1)} async-done(((f32[16,1,128]{2,1,0:T(1,128)}), f32[16,1,128]{2,1,0:T(1,128)S(1)}, u32[]{:S(2)}, u32[]{:S(2)}) %all-to-all-start.2) | async-done | bytes 8224 | tf_op jit(solution)/shard_map/all_to_all | solution.py:468
  54.3 0.6 %temporal_sum.1 = f32[2,64]{1,0:T(2,128)} custom-call(f32[16,1,128]{2,1,0:T(1,128)S(1)} %all-to-all-done.2.parts_ref), custom_call_target="tpu_custom_call" | custom-call | tf_op jit(solution)/shard_map/temporal_sum/pallas_call | solution.py:477
  (1 shorter events, 0.0 us)
Async XLA Ops:
  1.9 15.6 %all-to-all-start = ((bf16[8,2,320]{2,1,0:T(2,128)(2,1)}), bf16[8,2,320]{2,1,0:T(2,128)(2,1)S(1)}, u32[]{:S(2)}, u32[]{:S(2)}) async-start(bf16[8,2,320]{2,1,0:T(2,128)(2,1)} %broadcast_in_dim.2), calls=%async_computation | async-start | bytes 24576 | tf_op jit(solution)/shard_map/all_to_all | solution.py:435
  9.3 10.6 %copy-start.1 = (bf16[2,256,256]{2,1,0:T(8,128)(2,1)S(1)}, bf16[2,256,256]{2,1,0:T(8,128)(2,1)}, u32[]{:S(2)}) copy-start(bf16[2,256,256]{2,1,0:T(8,128)(2,1)} %constant.38.clone.right_ref) | copy-start | bytes 786436
  9.3 10.6 %copy-start.2 = (bf16[2,128,256]{2,1,0:T(8,128)(2,1)S(1)}, bf16[2,128,256]{2,1,0:T(8,128)(2,1)}, u32[]{:S(2)}) copy-start(bf16[2,128,256]{2,1,0:T(8,128)(2,1)} %constant.37.clone.left_ref) | copy-start | bytes 393220
  9.3 10.6 %copy-start.3 = (bf16[256,256]{1,0:T(8,128)(2,1)S(1)}, bf16[256,256]{1,0:T(8,128)(2,1)}, u32[]{:S(2)}) copy-start(bf16[256,256]{1,0:T(8,128)(2,1)} %constant.39.clone.picks_ref) | copy-start | bytes 393220
  17.5 25.4 %copy-start = (bf16[16,32,512]{2,1,0:T(8,128)(2,1)S(1)}, bf16[16,32,512]{2,1,0:T(8,128)(2,1)}, u32[]{:S(2)}) copy-start(bf16[16,32,512]{2,1,0:T(8,128)(2,1)} %param.9) | copy-start | bytes 1572868
  17.6 2.0 %collective-permute-start.1 = (f32[8,2,16,512]{3,2,1,0:T(8,128)S(1)}, f32[8,2,16,512]{3,2,1,0:T(8,128)S(1)}, u32[]{:S(2)}, u32[]{:S(2)}) collective-permute-start(f32[8,2,16,512]{3,2,1,0:T(8,128)S(1)} %get-tuple-element.16), channel_id=1, source_target_pairs={{0,1},{1,0},{2,3},{3,2},{4,5},{5,4},{6,7},{7,6},{8,9},{9,8},{10,11... | collective-permute-start | bytes 1572872 | tf_op jit(solution)/shard_map/ppermute | solution.py:443
  18.2 1.7 %collective-permute-start = (bf16[256,512]{1,0:T(8,128)(2,1)S(1)}, bf16[256,512]{1,0:T(8,128)(2,1)S(1)}, u32[]{:S(2)}, u32[]{:S(2)}) collective-permute-start(bf16[256,512]{1,0:T(8,128)(2,1)S(1)} %image_rows.1.own_ref), channel_id=1, source_target_pairs={{0,1},{1,0},{2,3},{3,2},{4,5},{5,4},{6,7},{7,6},{8,9},{9,8},{10,11... | collective-permute-start | bytes 786440 | tf_op jit(solution)/shard_map/ppermute | solution.py:445
  27.3 15.4 %collective-permute-start.2 = (f32[256,512]{1,0:T(8,128)S(1)}, f32[256,512]{1,0:T(8,128)S(1)}, u32[]{:S(2)}, u32[]{:S(2)}) collective-permute-start(f32[256,512]{1,0:T(8,128)S(1)} %get-tuple-element.20), channel_id=1, source_target_pairs={{0,1},{1,0},{2,3},{3,2},{4,5},{5,4},{6,7},{7,6},{8,9},{9,8},{10,11... | collective-permute-start | bytes 1572872 | tf_op jit(solution)/shard_map/ppermute | solution.py:457
  44.1 10.1 %all-to-all-start.2 = ((f32[16,1,128]{2,1,0:T(1,128)}), f32[16,1,128]{2,1,0:T(1,128)S(1)}, u32[]{:S(2)}, u32[]{:S(2)}) async-start(f32[16,1,128]{2,1,0:T(1,128)} %temporal_rows.1), calls=%async_computation.2 | async-start | bytes 16384 | tf_op jit(solution)/shard_map/all_to_all | solution.py:468

commit v11 on v10

--- a/solution.py
+++ b/solution.py
@@ -184,7 +184,7 @@
 
 def data_plan(rows, tile):
     own = [(1, at, tile) for at in range(0, rows // 2, tile)]
-    return own + [(0, 0, tile), (1, rows // 2, rows // 2), (0, tile, rows - tile)]
+    return own + [(part, at, rows // 2) for part, at in ((1, rows // 2), (0, 0), (0, rows // 2))]
 
 
 def data_kernel(plan, starts_ref, sampled_ref, block_ref, spatial_ref, kspace_ref, sens_ref,
@@ -242,8 +242,8 @@
         for t in range(frames):
             adjoint = dot(kspace_held[t].reshape(coils * size, width), back[t])
             real, imag = conj_sum(adjoint.reshape(coils, size, width), sens_r, sens_i)
-            out_ref[group, t, :, :half] = real.reshape(size // per, per, half)
-            out_ref[group, t, :, half:] = imag.reshape(size // per, per, half)
+            out_ref[group, t, :, :half] = real.reshape(size // per, per, half).astype(out_ref.dtype)
+            out_ref[group, t, :, half:] = imag.reshape(size // per, per, half).astype(out_ref.dtype)
     for copy in staging:
         copy.wait()
 
@@ -303,8 +303,8 @@
                 high = slice(half + k * quarter, half + (k + 1) * quarter)
                 for part, out_ref in enumerate((own_out, other_out)):
                     real, imag = conj_sum(both[part], wide[part, :, :, low], wide[part, :, :, high])
-                    out_ref[place, low] = real
-                    out_ref[place, high] = imag
+                    out_ref[place, low] = real.astype(out_ref.dtype)
+                    out_ref[place, high] = imag.astype(out_ref.dtype)
 
 
 def normal_plain(message, images, sens, left, right):
@@ -382,7 +382,7 @@
         in_specs=[SMEM] + [HBM] * 5,
         out_specs=[VMEM] * 3,
         out_shape=[
-            pltpu.VMEM(own, F32),
+            pltpu.VMEM(own, BF16),
             pltpu.VMEM(own, F32),
             pltpu.VMEM(spatial.shape, BF16),
         ],
@@ -402,7 +402,7 @@
         normal_kernel,
         in_specs=[SMEM] + [VMEM] * 3 + [HBM] + [VMEM] * 3,
         out_specs=[VMEM] * 2,
-        out_shape=[pltpu.VMEM(own.shape, F32)] * 2,
+        out_shape=[pltpu.VMEM(own.shape, F32), pltpu.VMEM(own.shape, BF16)],
         scratch_shapes=[
             pltpu.VMEM((per, groups, half), F32),
             pltpu.VMEM((groups, per, 2, half, half), BF16),

time: 55.2 us -> 49.7 us (0.900)
  blocking collectives: 15 us -> 0 us
  starting transfers between devices: 12.1 us -> 19.7 us
  waiting for transfers between devices: 5.75 us -> 6.97 us
  other arithmetic: 1.01 us -> 1.68 us
    all_to_all x1 -> x0, blocking collectives: 15 us -> none  [on_device(): data = lax.all_to_all(data, 'frame', 0, 0, tiled=True)]
    all_to_all x0 -> x1, starting transfers between devices: none -> 6 us  [on_device(): data = lax.all_to_all(data, 'frame', 0, 0, tiled=True)]
    all_to_all x1, starting transfers between devices: 3.69 us -> 5.67 us  [on_device(): partial = lax.all_to_all(partial, ('frame', 'coil'), 0, 0, tiled=True)]
    ppermute x1, waiting for transfers between devices: 0.01 us -> 1.46 us  [on_device(): lax.ppermute(send, 'coil', swap)]
    convert_element_type x1, other arithmetic: 0.09 us -> 0.78 us  [on_device(): data = (data_own + received).astype(BF16)]
  transfers between devices with their start and end apart: 5 -> 6, of which waited for: 3 -> 4; matrix products, arithmetic and copies ran while one was open for 0% -> 2% of each run, Pallas kernels for 19% -> 36%
where the time goes in v11:
time: 49.7 us; the launch traced here: 49.3 us
  starting transfers between devices  19.7 us (40%)
  Pallas kernels  19.5 us (39%)
  waiting for transfers between devices  6.97 us (14%)
  other arithmetic  1.68 us (3%)
  between operations  0.73 us (1%)
  local copies, waits for them, and re-layouts  0.63 us (1%)
    pallas_call x1, Pallas kernels, data_term(): pl.pallas_call(functools.partial(data_kernel, plan), in_specs=[SMEM] + [H...  7.99 us
    pallas_call x1, Pallas kernels, normal_term(): pl.pallas_call(normal_kernel, in_specs=[SMEM] + [VMEM] * 3 + [HBM] + [VME...  7.38 us
    all_to_all x1, starting transfers between devices, on_device(): lax.all_to_all(jnp.broadcast_to(message[None], (frame_size, *message.shap...  7.31 us
    all_to_all x1, starting transfers between devices, on_device(): data = lax.all_to_all(data, 'frame', 0, 0, tiled=True)  6 us
    all_to_all x1, starting transfers between devices, on_device(): partial = lax.all_to_all(partial, ('frame', 'coil'), 0, 0, tiled=True)  5.67 us
    all_to_all x1, waiting for transfers between devices, on_device(): partial = lax.all_to_all(partial, ('frame', 'coil'), 0, 0, tiled=True)  4.69 us
    pallas_call x1, Pallas kernels, on_device(): pl.pallas_call(functools.partial(spatial_kernel, total, rows, rank), in_s...  1.75 us
    ppermute x1, waiting for transfers between devices, on_device(): lax.ppermute(send, 'coil', swap)  1.46 us
  transfers between devices with their start and end apart: 6, of which 4 were waited for; matrix products, arithmetic and copies ran while one was open for 2% of the time, Pallas kernels for 36%

profile of v11, /device:TPU:0, one launch (start us, length us, event | category | flops | bytes accessed | tf_op | source)
XLA Modules:
  0.0 49.3 jit_solution(388344512029419277)
XLA Ops:
  0.6 0.7 %add_convert_fusion.1 = bf16[2,320]{1,0:T(2,128)(2,1)S(1)} fusion(s32[2,256]{1,0:T(2,128)} %sampled_ref.1, bf16[2,64]{1,0:T(2,128)(2,1)} %param.10), kind=kLoop, calls=%fused_computation.3 | loop fusion | flops 2560 | bytes 3584 | tf_op jit(solution)/shard_map/convert_element_type | solution.py:434
  1.3 0.6 %broadcast_in_dim.2 = bf16[8,2,320]{2,1,0:T(2,128)(2,1)} broadcast(bf16[2,320]{1,0:T(2,128)(2,1)S(1)} %add_convert_fusion.1), dimensions={1,2} | broadcast | bytes 11520 | tf_op jit(solution)/shard_map/broadcast_in_dim | solution.py:436
  1.9 7.3 %all-to-all-start = ((bf16[8,2,320]{2,1,0:T(2,128)(2,1)}), bf16[8,2,320]{2,1,0:T(2,128)(2,1)S(1)}, u32[]{:S(2)}, u32[]{:S(2)}) async-start(bf16[8,2,320]{2,1,0:T(2,128)(2,1)} %broadcast_in_dim.2), calls=%async_computation | async-start | bytes 24576 | tf_op jit(solution)/shard_map/all_to_all | solution.py:435
  9.2 0.1 pad_add_fusion.starts_ref
  9.3 0.0 copy-start.1
  9.3 0.0 copy-start.2
  9.3 0.0 copy-start.3
  9.3 8.0 %data_term.1 = (bf16[8,2,16,512]{3,2,1,0:T(8,128)(2,1)S(1)}, f32[8,2,16,512]{3,2,1,0:T(8,128)S(1)}, bf16[512,512]{1,0:T(8,128)(2,1)S(1)}) custom-call(s32[4]{0:T(128)S(1)} %pad_add_fusion.starts_ref, s32[2,256]{1,0:T(2,128)} %sampled_ref.1, bf16[256,512]{1,0:T(8,128)(2,1)} %constant.36.clone.block_ref, bf16[512,512]{1,0:T(8,128)(2,1)} %bitcast.9, ...), custom_call_target="tpu_custom_call" | custom-call | flops 4294967296 | bytes 8388608 | tf_op jit(solution)/shard_map/data_term/pallas_call | solution.py:380
  17.3 0.0 copy-start
  17.3 0.0 all-to-all-done.message_ref
  17.3 0.1 collective-permute-start.1
  17.4 0.6 %image_rows.1.own_ref = bf16[256,512]{1,0:T(8,128)(2,1)S(1)} custom-call(bf16[8,2,64]{2,1,0:T(2,128)(2,1)S(1)} %slice.4.factors_ref, bf16[512,512]{1,0:T(8,128)(2,1)S(1)} %get-tuple-element.14.spatial_ref), custom_call_target="tpu_custom_call" | custom-call | tf_op jit(solution)/shard_map/image_rows/pallas_call | solution.py:106
  18.0 0.6 %collective-permute-start = (bf16[256,512]{1,0:T(8,128)(2,1)S(1)}, bf16[256,512]{1,0:T(8,128)(2,1)S(1)}, u32[]{:S(2)}, u32[]{:S(2)}) collective-permute-start(bf16[256,512]{1,0:T(8,128)(2,1)S(1)} %image_rows.1.own_ref), channel_id=1, source_target_pairs={{0,1},{1,0},{2,3},{3,2},{4,5},{5,4},{6,7},{7,6},{8,9},{9,8},{10,11... | collective-permute-start | bytes 786440 | tf_op jit(solution)/shard_map/ppermute | solution.py:445
  18.6 0.4 collective-permute-done.1
  18.9 0.8 %add_convert_fusion = bf16[8,2,16,512]{3,2,1,0:T(8,128)(2,1)} fusion(f32[8,2,16,512]{3,2,1,0:T(8,128)S(1)} %get-tuple-element.15, bf16[8,2,16,512]{3,2,1,0:T(8,128)(2,1)S(1)} %collective-permute-done.1), kind=kLoop, calls=%fused_computation.2 | loop fusion | flops 393216 | bytes 1048576 | tf_op jit(solution)/shard_map/convert_element_type | solution.py:446
  19.7 0.0 collective-permute-done.other_ref
  19.7 6.0 %all-to-all-start.1 = ((bf16[8,2,16,512]{3,2,1,0:T(8,128)(2,1)}), bf16[8,2,16,512]{3,2,1,0:T(8,128)(2,1)S(1)}, u32[]{:S(2)}, u32[]{:S(2)}) async-start(bf16[8,2,16,512]{3,2,1,0:T(8,128)(2,1)} %add_convert_fusion), calls=%async_computation.1 | async-start | bytes 524288 | tf_op jit(solution)/shard_map/all_to_all | solution.py:450
  25.7 0.0 copy-done.1
  25.7 0.0 copy-done.2
  25.7 0.0 copy-done.3
  25.8 7.4 %normal_term.1 = (f32[256,512]{1,0:T(8,128)S(1)}, bf16[256,512]{1,0:T(8,128)(2,1)S(1)}) custom-call(s32[4]{0:T(128)S(1)} %pad_add_fusion.starts_ref, bf16[8,2,320]{2,1,0:T(2,128)(2,1)S(1)} %all-to-all-done.message_ref, bf16[256,512]{1,0:T(8,128)(2,1)S(1)} %image_rows.1.own_ref, bf16[256,512]{1,0:T(8,128)(2,1)S(1)} %collective-permute-done.other_ref, ...), custom_call_target="tpu_custom_call" | custom-call | flops 2147483648 | bytes 524288 | tf_op jit(solution)/shard_map/normal_term/pallas_call | solution.py:401
  33.1 0.1 collective-permute-start.2
  33.3 1.5 %collective-permute-done.2 = bf16[256,512]{1,0:T(8,128)(2,1)S(1)} collective-permute-done((bf16[256,512]{1,0:T(8,128)(2,1)S(1)}, bf16[256,512]{1,0:T(8,128)(2,1)S(1)}, u32[]{:S(2)}, u32[]{:S(2)}) %collective-permute-start.2) | collective-permute-done | bytes 262176 | tf_op jit(solution)/shard_map/ppermute | solution.py:457
  34.7 0.4 all-to-all-done.1
  35.2 0.1 fusion.grad_ref
  35.3 0.0 copy-done
  35.3 1.2 %temporal_rows.1 = f32[16,1,128]{2,1,0:T(1,128)} custom-call(bf16[512,512]{1,0:T(8,128)(2,1)S(1)} %bitcast.10, bf16[256,512]{1,0:T(8,128)(2,1)S(1)} %fusion.grad_ref), custom_call_target="tpu_custom_call" | custom-call | tf_op jit(solution)/shard_map/temporal_rows/pallas_call | solution.py:460
  36.5 5.7 %all-to-all-start.2 = ((f32[16,1,128]{2,1,0:T(1,128)}), f32[16,1,128]{2,1,0:T(1,128)S(1)}, u32[]{:S(2)}, u32[]{:S(2)}) async-start(f32[16,1,128]{2,1,0:T(1,128)} %temporal_rows.1), calls=%async_computation.2 | async-start | bytes 16384 | tf_op jit(solution)/shard_map/all_to_all | solution.py:468
  42.2 1.7 %spatial_rows.1 = f32[512,512]{1,0:T(8,128)} custom-call(bf16[8,2,64]{2,1,0:T(2,128)(2,1)S(1)} %slice.4.factors_ref, bf16[256,512]{1,0:T(8,128)(2,1)S(1)} %fusion.grad_ref), custom_call_target="tpu_custom_call" | custom-call | tf_op jit(solution)/shard_map/spatial_rows/pallas_call | solution.py:469
  44.0 4.7 %all-to-all-done.2.parts_ref = f32[16,1,128]{2,1,0:T(1,128)S(1)} async-done(((f32[16,1,128]{2,1,0:T(1,128)}), f32[16,1,128]{2,1,0:T(1,128)S(1)}, u32[]{:S(2)}, u32[]{:S(2)}) %all-to-all-start.2) | async-done | bytes 8224 | tf_op jit(solution)/shard_map/all_to_all | solution.py:468
  48.6 0.6 %temporal_sum.1 = f32[2,64]{1,0:T(2,128)} custom-call(f32[16,1,128]{2,1,0:T(1,128)S(1)} %all-to-all-done.2.parts_ref), custom_call_target="tpu_custom_call" | custom-call | tf_op jit(solution)/shard_map/temporal_sum/pallas_call | solution.py:477
  (1 shorter events, 0.0 us)
Async XLA Ops:
  1.9 15.4 %all-to-all-start = ((bf16[8,2,320]{2,1,0:T(2,128)(2,1)}), bf16[8,2,320]{2,1,0:T(2,128)(2,1)S(1)}, u32[]{:S(2)}, u32[]{:S(2)}) async-start(bf16[8,2,320]{2,1,0:T(2,128)(2,1)} %broadcast_in_dim.2), calls=%async_computation | async-start | bytes 24576 | tf_op jit(solution)/shard_map/all_to_all | solution.py:435
  9.3 16.4 %copy-start.1 = (bf16[2,256,256]{2,1,0:T(8,128)(2,1)S(1)}, bf16[2,256,256]{2,1,0:T(8,128)(2,1)}, u32[]{:S(2)}) copy-start(bf16[2,256,256]{2,1,0:T(8,128)(2,1)} %constant.38.clone.right_ref) | copy-start | bytes 786436
  9.3 16.4 %copy-start.2 = (bf16[2,128,256]{2,1,0:T(8,128)(2,1)S(1)}, bf16[2,128,256]{2,1,0:T(8,128)(2,1)}, u32[]{:S(2)}) copy-start(bf16[2,128,256]{2,1,0:T(8,128)(2,1)} %constant.37.clone.left_ref) | copy-start | bytes 393220
  9.3 16.4 %copy-start.3 = (bf16[256,256]{1,0:T(8,128)(2,1)S(1)}, bf16[256,256]{1,0:T(8,128)(2,1)}, u32[]{:S(2)}) copy-start(bf16[256,256]{1,0:T(8,128)(2,1)} %constant.39.clone.picks_ref) | copy-start | bytes 393220
  17.3 18.0 %copy-start = (bf16[16,32,512]{2,1,0:T(8,128)(2,1)S(1)}, bf16[16,32,512]{2,1,0:T(8,128)(2,1)}, u32[]{:S(2)}) copy-start(bf16[16,32,512]{2,1,0:T(8,128)(2,1)} %param.9) | copy-start | bytes 1572868
  17.3 1.6 %collective-permute-start.1 = (bf16[8,2,16,512]{3,2,1,0:T(8,128)(2,1)S(1)}, bf16[8,2,16,512]{3,2,1,0:T(8,128)(2,1)S(1)}, u32[]{:S(2)}, u32[]{:S(2)}) collective-permute-start(bf16[8,2,16,512]{3,2,1,0:T(8,128)(2,1)S(1)} %get-tuple-element.16), channel_id=1, source_target_pairs={{0,1},{1,0},{2,3},{3,2},{4,5},{5,4},{6,7},{7,6},{8,9},{9,8},{10,11... | collective-permute-start | bytes 786440 | tf_op jit(solution)/shard_map/ppermute | solution.py:443
  18.0 1.7 %collective-permute-start = (bf16[256,512]{1,0:T(8,128)(2,1)S(1)}, bf16[256,512]{1,0:T(8,128)(2,1)S(1)}, u32[]{:S(2)}, u32[]{:S(2)}) collective-permute-start(bf16[256,512]{1,0:T(8,128)(2,1)S(1)} %image_rows.1.own_ref), channel_id=1, source_target_pairs={{0,1},{1,0},{2,3},{3,2},{4,5},{5,4},{6,7},{7,6},{8,9},{9,8},{10,11... | collective-permute-start | bytes 786440 | tf_op jit(solution)/shard_map/ppermute | solution.py:445
  19.7 15.4 %all-to-all-start.1 = ((bf16[8,2,16,512]{3,2,1,0:T(8,128)(2,1)}), bf16[8,2,16,512]{3,2,1,0:T(8,128)(2,1)S(1)}, u32[]{:S(2)}, u32[]{:S(2)}) async-start(bf16[8,2,16,512]{3,2,1,0:T(8,128)(2,1)} %add_convert_fusion), calls=%async_computation.1 | async-start | bytes 524288 | tf_op jit(solution)/shard_map/all_to_all | solution.py:450
  33.1 1.6 %collective-permute-start.2 = (bf16[256,512]{1,0:T(8,128)(2,1)S(1)}, bf16[256,512]{1,0:T(8,128)(2,1)S(1)}, u32[]{:S(2)}, u32[]{:S(2)}) collective-permute-start(bf16[256,512]{1,0:T(8,128)(2,1)S(1)} %get-tuple-element.20), channel_id=1, source_target_pairs={{0,1},{1,0},{2,3},{3,2},{4,5},{5,4},{6,7},{7,6},{8,9},{9,8},{10,11... | collective-permute-start | bytes 786440 | tf_op jit(solution)/shard_map/ppermute | solution.py:457
  36.5 12.1 %all-to-all-start.2 = ((f32[16,1,128]{2,1,0:T(1,128)}), f32[16,1,128]{2,1,0:T(1,128)S(1)}, u32[]{:S(2)}, u32[]{:S(2)}) async-start(f32[16,1,128]{2,1,0:T(1,128)} %temporal_rows.1), calls=%async_computation.2 | async-start | bytes 16384 | tf_op jit(solution)/shard_map/all_to_all | solution.py:468
